TPU v7x, 128 devices: a whole 4x4x4 slice. The times are simulated.
128 devices in a mesh: dict: 8 (over x, z_hi), dp: 16 (over z_lo, y, core).
Axes of the slice: x: 4, y: 4, z: 4 (z_hi: 2, z_lo: 2; z = z_hi * 2 + z_lo), core: 2. Of those that a mesh axis runs over, the one named last changes fastest.
Arguments:
- activations: bfloat16 [4096, 3584], P('dp', 'dict'), may hold values from -6 to 6
- dictionary: bfloat16 [65536, 3584], P(('dict', 'dp')), may hold values from -0.09375 to 0.09375
- enc_bias: bfloat16 [65536], P(('dict', 'dp')), may hold values from -1.5 to 0
- dec_bias: float32 [3584], replicated, may hold values from -3 to 3
- block_codes: int32 [32, 8, 16], P('dp'), may hold values from -1 to 511, as said below
Outputs:
- error: bfloat16 [4096, 3584], P('dp', 'dict')
- grad_dict: float32 [65536, 3584], P(('dict', 'dp'))
- grad_enc_bias: float32 [65536], P(('dict', 'dp'))
Inputs may be any that keep to these rules, and one draw needn't show every extreme that they name: `block_codes`: entry [b, s, m] is either -1 (an empty slot) or a latent block of shard s, that is one of the blocks s * 64 upward. Block k is held by the dp index (k % 64) // 4. Every token block names exactly 64 blocks in all and at most 16 in one shard, reached in every draw; within one shard its blocks are held by distinct dp indices. All token blocks of one dp index that name a block held by the same dp index of the same shard name the same block.
All inputs are finite; a program needn't handle non-finite values.
Results may differ from a plain program's by a relative error of at most 0.012.
The roundings to bfloat16 on the way count: a program that leaves them out, or rounds other values in their place, can miss the bound.
Values may be sent and summed in bfloat16 or wider, within the bound.
A program may use at most 128 MiB of HBM per device.

v0:
```python
import jax
import jax.numpy as jnp
from jax import lax
from jax.sharding import PartitionSpec as P

DICT_SPAN = 128
SAMPLE_SPAN = 128


def flat_dot(left, right):
    return lax.dot_general(
        left, right, (((1,), (1,)), ((), ())), preferred_element_type=jnp.float32
    )


def shards(activations, dictionary, enc_bias, dec_bias, block_codes):
    replica_total = lax.axis_size("dp")
    shard_index = lax.axis_index("dict")
    model_width = dictionary.shape[1]
    own_blocks = dictionary.shape[0] // DICT_SPAN
    shard_blocks = own_blocks * replica_total
    sample_matrix = activations.shape[0]
    gathered = lax.all_gather(activations, "dict", axis=1, tiled=True)
    my_codes = lax.dynamic_index_in_dim(block_codes, shard_index, axis=1, keepdims=False)
    filled = my_codes >= 0
    local_id = my_codes - shard_index * shard_blocks
    owning = jnp.where(filled, local_id // own_blocks, -1)
    inside = jnp.where(filled, local_id % own_blocks, -1)
    peer_ids = jnp.arange(replica_total, dtype=jnp.int32)
    matches = owning[:, :, None] == peer_ids
    selected_entries = jnp.any(matches, axis=1)
    wanted = jnp.max(jnp.where(matches, inside[:, :, None], -1), axis=(0, 1))
    asked = lax.all_to_all(wanted, "dp", split_axis=0, concat_axis=0, tiled=True)
    own_w = dictionary.reshape(own_blocks, DICT_SPAN, model_width)
    own_b = enc_bias.reshape(own_blocks, DICT_SPAN)
    picked = jnp.maximum(asked, 0)
    answered = asked >= 0
    send_w = jnp.where(answered[:, None, None], own_w[picked], jnp.zeros((), jnp.bfloat16))
    send_b = jnp.where(answered[:, None], own_b[picked], jnp.zeros((), jnp.bfloat16))
    got_w, got_b = (
        lax.all_to_all(send_w, "dp", split_axis=0, concat_axis=0, tiled=True),
        lax.all_to_all(send_b, "dp", split_axis=0, concat_axis=0, tiled=True),
    )
    slot_rows = replica_total * DICT_SPAN
    fetched = got_w.reshape(slot_rows, model_width)
    bias_flat = got_b.reshape(slot_rows).astype(jnp.float32)
    mean_removed = (gathered.astype(jnp.float32) - dec_bias).astype(jnp.bfloat16)
    preact = flat_dot(mean_removed, fetched) + bias_flat
    encoder_input_tiles = preact.reshape(sample_matrix, replica_total, DICT_SPAN)
    nonzero_indicator = jnp.repeat(selected_entries, SAMPLE_SPAN, axis=0)[:, :, None]
    hidden_activity = jnp.where(
        nonzero_indicator, jnp.maximum(encoder_input_tiles, 0.0), 0.0
    ).astype(jnp.bfloat16)
    partial_product = jnp.dot(
        hidden_activity.reshape(sample_matrix, slot_rows),
        fetched,
        preferred_element_type=jnp.float32,
    )
    summed = lax.psum(partial_product, "dict")
    error_full = (summed + dec_bias - gathered.astype(jnp.float32)).astype(jnp.bfloat16)
    share = model_width // lax.axis_size("dict")
    error_out = lax.dynamic_slice_in_dim(error_full, shard_index * share, share, 1)
    returned_entries = flat_dot(error_full, fetched)
    derivative_factor = jnp.where(
        nonzero_indicator & (encoder_input_tiles > 0),
        returned_entries.reshape(sample_matrix, replica_total, DICT_SPAN),
        0.0,
    ).astype(jnp.bfloat16)
    bias_terms = jnp.sum(derivative_factor.astype(jnp.float32), axis=0).astype(jnp.bfloat16)

    def block_grad(paired):
        latent_one, slope_one = paired
        first_term = lax.dot_general(
            latent_one, error_full, (((0,), (0,)), ((), ())), preferred_element_type=jnp.float32
        )
        second_term = lax.dot_general(
            slope_one, mean_removed, (((0,), (0,)), ((), ())), preferred_element_type=jnp.float32
        )
        return (first_term + second_term).astype(jnp.bfloat16)

    weight_terms = lax.map(
        block_grad, (jnp.swapaxes(hidden_activity, 0, 1), jnp.swapaxes(derivative_factor, 0, 1))
    )
    back_w, back_b = (
        lax.all_to_all(weight_terms, "dp", split_axis=0, concat_axis=0, tiled=True),
        lax.all_to_all(bias_terms, "dp", split_axis=0, concat_axis=0, tiled=True),
    )
    onehot = (asked[:, None] == jnp.arange(own_blocks, dtype=jnp.int32)).astype(jnp.bfloat16)
    grad_w = jnp.einsum("rk,rld->kld", onehot, back_w, preferred_element_type=jnp.float32)
    grad_b = jnp.einsum("rk,rl->kl", onehot, back_b, preferred_element_type=jnp.float32)
    return (
        error_out,
        grad_w.reshape(own_blocks * DICT_SPAN, model_width),
        grad_b.reshape(own_blocks * DICT_SPAN),
    )


def solution(mesh):
    in_specs = (
        P("dp", "dict"),
        P(("dict", "dp"), None),
        P(("dict", "dp")),
        P(),
        P("dp", None, None),
    )
    out_specs = (P("dp", "dict"), P(("dict", "dp"), None), P(("dict", "dp")))
    return jax.shard_map(shards, mesh=mesh, in_specs=in_specs, out_specs=out_specs, check_vma=False)
```

profile of v0, /device:TPU:1, one launch (start us, length us, event | category | flops | bytes accessed | tf_op | source)
XLA Modules:
  0.0 758.1 jit_solution(12832547715787144587)
XLA Ops:
  7.2 0.7 broadcast_compare_fusion.2
  7.9 0.7 broadcast_subtract_fusion
  8.8 12.6 %all_to_all.40 = s32[16,1,1]{2,1,0:T(1,128)S(1)} all-to-all(s32[16,1,1]{2,1,0:T(1,128)S(1)} %copy.38), channel_id=1, replica_groups=mesh['dict'=8,'dp'=16] {'dp'}, dimensions={0} | all-to-all | bytes 128 | tf_op jit(solution)/shard_map/all_to_all | solution.py:33
  21.4 0.7 fusion.29
  22.1 9.4 %gather_fusion = bf16[16,128,3584]{2,1,0:T(8,128)(2,1)} fusion(bf16[4,128,3584]{2,1,0:T(8,128)(2,1)} %bitcast.90, s32[1024]{0:T(1024)S(1)} %pad_clamp_fusion), kind=kCustom, calls=%fused_computation | custom fusion | bytes 29360192 | tf_op jit(solution)/shard_map/gather | solution.py:38
  31.5 0.6 gather_fusion.1
  32.1 0.6 copy.39
  32.7 3.7 all-to-all-start.2
  36.9 13.4 %broadcast_select_fusion = bf16[16,128,3584]{2,1,0:T(8,128)(2,1)} fusion(bf16[16,128,3584]{2,1,0:T(8,128)(2,1)} %gather_fusion, pred[16]{0:T(512)(128)(4,1)S(1)} %compare_reduce_fusion), kind=kLoop, calls=%fused_computation.15 | loop fusion | flops 7340032 | bytes 29360144 | tf_op jit(solution)/shard_map/jit(_where)/select_n | solution.py:38
  50.2 5.8 all-to-all-start.1
  56.1 0.7 all-gather.2.cloned.1.call-update
  57.1 170.8 %all-gather.2.cloned.1.call-done = bf16[256,3584]{0,1:T(8,128)(2,1)} async-done(((bf16[256,448]{0,1:T(8,128)(2,1)}), bf16[256,3584]{0,1:T(8,128)(2,1)}) %all-gather.2.cloned.1.call-update) | async-done | bytes 1835024 | tf_op jit(solution)/shard_map/all_gather | solution.py:23
  227.9 3.8 copy.37
  231.7 1.8 fusion.12
  233.6 18.9 %all-to-all-done.1 = bf16[16,128,3584]{2,1,0:T(8,128)(2,1)} async-done(((bf16[16,128,3584]{2,1,0:T(8,128)(2,1)}), bf16[16,128,3584]{2,1,0:T(8,128)(2,1)}, u32[]{:S(2)}, u32[]{:S(2)}) %all-to-all-start.1) | async-done | bytes 14680096 | tf_op jit(solution)/shard_map/all_to_all | solution.py:41
  252.4 7.3 convolution_add_fusion.1
  259.7 1.3 copy-done.4
  261.0 11.1 %convolution_bitcast_fusion = f32[256,3584]{1,0:T(8,128)} fusion(bf16[16,128,3584]{2,1,0:T(8,128)(2,1)} %all-to-all-done.1, pred[256,16]{0,1:T(8,128)(4,1)S(1)} %bitcast.94, f32[256,2048]{1,0:T(8,128)S(1)} %convolution_add_fusion.1), kind=kOutput, calls=%fused_computation.16 | convolution fusion | flops 3759669248 | bytes 20451328 | tf_op jit(solution)/shard_map/dot_general | solution.py:54
  272.1 1.6 copy-done.5
  273.7 0.7 fusion.19
  274.4 164.5 %all-reduce.2.cloned.1.call-done = f32[256,3584]{1,0:T(8,128)} async-done(((f32[256,3584]{1,0:T(8,128)}), f32[256,3584]{1,0:T(8,128)}) %all-reduce.2.cloned.1.call-update) | async-done | bytes 3670032 | tf_op jit(solution)/shard_map/psum | solution.py:59
  438.9 3.2 fusion.13
  442.2 8.2 %fusion.30 = (bf16[16,128]{1,0:T(8,128)(2,1)S(1)}, bf16[256,16,128]{2,0,1:T(8,128)(2,1)}) fusion(bf16[16,128,3584]{2,1,0:T(8,128)(2,1)} %all-to-all-done.1, bf16[256,3584]{1,0:T(8,128)(2,1)S(1)} %fusion.13, pred[256,16]{0,1:T(8,128)(4,1)S(1)} %bitcast.96, f32[256,2048]{1,0:T(8,128)S(1)} %copy-done.6), kind=kOutput, calls=%fused_computation.62 | convolution fusion | flops 3760715776 | bytes 19668992 | tf_op jit(solution)/shard_map/dot_general | solution.py:11
  450.4 0.6 copy.44
  451.0 5.6 all-to-all-start.4
  456.6 59.5 %while.11 = (s32[]{:T(128)}, bf16[16,128,3584]{2,1,0:T(8,128)(2,1)}, bf16[16,256,128]{2,1,0:T(8,128)(2,1)S(1)}, bf16[256,3584]{1,0:T(8,128)(2,1)S(1)}, bf16[16,2...) while((s32[]{:T(128)}, bf16[16,128,3584]{2,1,0:T(8,128)(2,1)}, ...), condition=%wide.region_4.5_spmd.clone, body=%wide.region_3.4_spmd.sunk.clone | while | flops 470679552 | bytes 15729765 | solution.py:81
  457.0 1.1 copy-done.3
  458.1 2.2 fusion.54
  460.7 1.1 copy-done.3
  461.8 2.2 fusion.54
  464.4 1.1 copy-done.3
  465.5 2.2 fusion.54
  468.1 1.1 copy-done.3
  469.2 2.2 fusion.54
  471.8 1.1 copy-done.3
  472.9 2.2 fusion.54
  475.5 1.1 copy-done.3
  476.6 2.2 fusion.54
  479.2 1.1 copy-done.3
  480.3 2.2 fusion.54
  483.0 1.1 copy-done.3
  484.0 2.2 fusion.54
  486.7 1.1 copy-done.3
  487.7 2.2 fusion.54
  490.4 1.1 copy-done.3
  491.5 2.2 fusion.54
  494.1 1.1 copy-done.3
  495.2 2.2 fusion.54
  497.8 1.1 copy-done.3
  498.9 2.3 fusion.54
  501.6 1.1 copy-done.3
  502.7 2.3 fusion.54
  505.4 1.1 copy-done.3
  506.4 2.2 fusion.54
  509.1 1.1 copy-done.3
  510.1 2.2 fusion.54
  512.8 1.1 copy-done.3
  513.8 2.2 fusion.54
  516.1 5.7 all-to-all-start.3
  521.9 0.8 copy.45
  522.8 0.7 convolution_bitcast_fusion.1
  523.5 194.7 %all-to-all-done.3 = bf16[16,128,3584]{2,1,0:T(8,128)(2,1)} async-done(((bf16[16,128,3584]{2,1,0:T(8,128)(2,1)}), bf16[16,128,3584]{2,1,0:T(8,128)(2,1)}, u32[]{:S(2)}, u32[]{:S(2)}) %all-to-all-start.3) | async-done | bytes 14680096 | tf_op jit(solution)/shard_map/all_to_all | solution.py:85
  718.2 24.6 %fusion.10 = f32[4,128,3584]{2,0,1:T(4,128)} fusion(bf16[16,128,3584]{2,1,0:T(8,128)(2,1)} %all-to-all-done.3, s32[16]{0:T(128)S(1)} %get-tuple-element.51), kind=kOutput, calls=%fused_computation.13 | convolution fusion | flops 58720320 | bytes 22020160 | tf_op jit(solution)/shard_map/rk,rld->kld/dot_general | solution.py:89
  742.8 8.5 %copy.43 = f32[4,128,3584]{2,1,0:T(8,128)} copy(f32[4,128,3584]{2,0,1:T(4,128)} %fusion.10) | data formatting | bytes 14680064 | tf_op jit(solution)/shard_map/rk,rld->kld/dot_general | solution.py:89
  (63 shorter events, 8.2 us)
Async XLA Ops:
  7.2 24.3 %copy-start = (bf16[512]{0:T(512)(128)(2,1)S(1)}, bf16[512]{0:T(512)(128)(2,1)}, u32[]{:S(2)}) copy-start(bf16[512]{0:T(512)(128)(2,1)} %param.9) | copy-start | bytes 3076
  32.7 17.5 %all-to-all-start.2 = ((bf16[16,1,128]{2,1,0:T(2,128)(2,1)}), bf16[16,1,128]{2,1,0:T(2,128)(2,1)S(1)}, u32[]{:S(2)}, u32[]{:S(2)}) async-start(bf16[16,1,128]{2,1,0:T(2,128)(2,1)} %copy.39), calls=%async_computation.2 | async-start | bytes 16384 | tf_op jit(solution)/shard_map/all_to_all | solution.py:42
  50.2 202.2 %all-to-all-start.1 = ((bf16[16,128,3584]{2,1,0:T(8,128)(2,1)}), bf16[16,128,3584]{2,1,0:T(8,128)(2,1)}, u32[]{:S(2)}, u32[]{:S(2)}) async-start(bf16[16,128,3584]{2,1,0:T(8,128)(2,1)} %broadcast_select_fusion), calls=%async_computation.1 | async-start | bytes 29360128 | tf_op jit(solution)/shard_map/all_to_all | solution.py:41
  56.0 175.7 %copy-start.7 = (f32[3584]{0:T(1024)S(1)}, f32[3584]{0:T(1024)}, u32[]{:S(2)}) copy-start(f32[3584]{0:T(1024)} %param.10) | copy-start | bytes 43012
  56.0 171.9 %all-gather.2.cloned.1.call-start = ((), (), s32[]{:S(2)}) async-start(), calls=%async_computation.5 | async-start | bytes 2064384 | tf_op jit(solution)/shard_map/all_gather | solution.py:23
  56.8 382.2 %all-reduce.2.cloned.1.call-start = ((), (), s32[]{:S(2)}) async-start(), calls=%async_computation.6 | async-start | bytes 7340032 | tf_op jit(solution)/shard_map/psum | solution.py:59
  233.5 26.2 %copy-start.2 = (bf16[256,3584]{1,0:T(8,128)(2,1)}, bf16[256,3584]{1,0:T(8,128)(2,1)S(1)}, u32[]{:S(2)}) copy-start(bf16[256,3584]{1,0:T(8,128)(2,1)S(1)} %fusion.12) | copy-start | bytes 5505028
  259.7 1.3 copy-start.4
  272.1 1.6 copy-start.5
  438.9 3.2 copy-start.6
  451.0 65.1 %all-to-all-start.4 = ((bf16[16,1,128]{2,1,0:T(2,128)(2,1)}), bf16[16,1,128]{2,1,0:T(2,128)(2,1)S(1)}, u32[]{:S(2)}, u32[]{:S(2)}) async-start(bf16[16,1,128]{2,1,0:T(2,128)(2,1)} %copy.44), calls=%async_computation.4 | async-start | bytes 16384 | tf_op jit(solution)/shard_map/all_to_all | solution.py:86
  456.6 1.5 copy-start.3
  460.3 1.5 copy-start.3
  464.0 1.5 copy-start.3
  467.7 1.5 copy-start.3
  471.4 1.5 copy-start.3
  475.1 1.5 copy-start.3
  478.8 1.5 copy-start.3
  482.5 1.5 copy-start.3
  486.2 1.5 copy-start.3
  490.0 1.5 copy-start.3
  493.7 1.5 copy-start.3
  497.4 1.5 copy-start.3
  501.2 1.5 copy-start.3
  504.9 1.5 copy-start.3
  508.6 1.5 copy-start.3
  512.3 1.5 copy-start.3
  516.1 202.1 %all-to-all-start.3 = ((bf16[16,128,3584]{2,1,0:T(8,128)(2,1)}), bf16[16,128,3584]{2,1,0:T(8,128)(2,1)}, u32[]{:S(2)}, u32[]{:S(2)}) async-start(bf16[16,128,3584]{2,1,0:T(8,128)(2,1)} %get-tuple-element.35), calls=%async_computation.3 | async-start | bytes 29360128 | tf_op jit(solution)/shard_map/all_to_all | solution.py:85
  742.8 8.5 %copy-start.1 = (bf16[512]{0:T(512)(128)(2,1)S(1)}, bf16[512]{0:T(512)(128)(2,1)}, u32[]{:S(2)}) copy-start(bf16[512]{0:T(512)(128)(2,1)} %param.9) | copy-start | bytes 3076
Sparse Core Ops, SparseCore 0:
  59.2 168.7 all-gather.1
  272.2 166.6 all-reduce.1
where the time goes:
time: 763 us; the launch traced here: 758 us
  waiting for transfers between devices  550 us (72%)
  matrix products  94.4 us (12%)
  local copies, waits for them, and re-layouts  44.6 us (6%)
  other arithmetic  21.8 us (3%)
  starting transfers between devices  20.9 us (3%)
  between operations  14.2 us (2%)
  blocking collectives  12.6 us (2%)
    all_to_all x1, waiting for transfers between devices, shards(): lax.all_to_all(weight_terms, 'dp', split_axis=0, concat_axis=0, tiled=True)  195 us
    all_gather x1, waiting for transfers between devices, shards(): gathered = lax.all_gather(activations, 'dict', axis=1, tiled=True)  171 us
    psum x1, waiting for transfers between devices, shards(): summed = lax.psum(partial_product, 'dict')  165 us
    dot_general x16, matrix products, block_grad(): lax.dot_general(slope_one, mean_removed, (((0,), (0,)), ((), ())), prefer...  35.5 us
    dot_general x1, matrix products, shards(): jnp.einsum('rk,rld->kld', onehot, back_w, preferred_element_type=jnp.floa...  24.6 us
    all_to_all x1, waiting for transfers between devices, shards(): lax.all_to_all(send_w, 'dp', split_axis=0, concat_axis=0, tiled=True)  18.9 us
    while x32, local copies, waits for them, and re-layouts  17 us
    dot_general x2, matrix products, flat_dot(): lax.dot_general(left, right, (((1,), (1,)), ((), ())), preferred_element_...  15.5 us
  transfers between devices with their start and end apart: 6, of which 4 were waited for; matrix products, arithmetic and copies ran while one was open for 9% of the time, Pallas kernels for 0%

commit v1 on v0

v1 whole, which is shorter than its diff:
```python
import functools
import jax, jax.numpy as jnp
from jax import lax
from jax.experimental import pallas as pl
from jax.experimental.pallas import tpu as pltpu
from jax.sharding import Mesh, PartitionSpec as P

ROWS, TOK = 448, 256
C0 = (0, 144, 288)
CN = (144, 144, 160)
CH = (80, 64, 80)
ORDER = (("x", "y", "z"), ("y", "z", "x"), ("z", "x", "y"))


def coords():
    x, y = lax.axis_index("x"), lax.axis_index("y")
    z = lax.axis_index("zh") * 2 + lax.axis_index("zl")
    return {"x": x, "y": y, "z": z}


def shift(me, dim, by):
    return lax.rem(me[dim] + (by + 4), 4)


def device(dim, value):
    if dim == "z":
        return {"zh": value // 2, "zl": lax.rem(value, 2)}
    return {dim: value}


def region(ref, at, lo, n):
    z = at["z"]
    zl = slice(None) if z is None else lax.rem(z, 2)
    zh = slice(None) if z is None else z // 2
    y = slice(None) if at["y"] is None else at["y"]
    x = slice(None) if at["x"] is None else at["x"]
    return ref.at[zl, y, x, zh, pl.ds(lo, n), :]


def remote(src, dst, send, recv, dim, value):
    return pltpu.make_async_remote_copy(
        src_ref=src, dst_ref=dst, send_sem=send, recv_sem=recv,
        device_id=device(dim, value), device_id_type=pl.DeviceIdType.MESH)


def barrier(me):
    sem = pltpu.get_barrier_semaphore()
    for dim in ("x", "y", "z"):
        for by in (-1, 1):
            pl.semaphore_signal(sem, inc=1, device_id=device(dim, shift(me, dim, by)),
                                device_id_type=pl.DeviceIdType.MESH)
    pl.semaphore_wait(sem, 6)


def gather(me, own, out, local, send, recv):
    mine = pltpu.make_async_copy(own, region(out, me, 0, ROWS), local)
    mine.start()
    started = []
    for p in range(3):
        near = []
        for k in range(3):
            dim, prev = ORDER[k][p], ORDER[k][:p]
            at = {d: (None if d in prev else me[d]) for d in me}
            lo, n, h = C0[k], CN[k], CH[k]
            copies = []
            for s, by in enumerate((1, -1)):
                src = own.at[pl.ds(lo, n), :] if p == 0 else region(out, at, lo, n)
                c = remote(src, region(out, at, lo, n), send.at[k, p, s], recv.at[k, p, s], dim, shift(me, dim, by))
                c.start()
                copies.append(c)
            near.append(copies)
            started += copies
        far = []
        for k in range(3):
            dim, prev = ORDER[k][p], ORDER[k][:p]
            lo, n, h = C0[k], CN[k], CH[k]
            copies = []
            for s, by in enumerate((1, -1)):
                at = {d: (None if d in prev else me[d]) for d in me}
                at[dim] = shift(me, dim, -by)
                near[k][s].wait_recv()
                a, b = (lo, h) if s == 0 else (lo + h, n - h)
                c = remote(region(out, at, a, b), region(out, at, a, b), send.at[k, p, 2 + s], recv.at[k, p, 2 + s],
                           dim, shift(me, dim, by))
                c.start()
                copies.append(c)
            far.append(copies)
            started += copies
        for k in range(3):
            for c in far[k]:
                c.wait_recv()
        if p == 0:
            mine.wait()
    for c in started:
        c.wait_send()


def held(ref, dims, at, lo, n):
    index = []
    for name in ("zl", "y", "x", "zh"):
        dim = name[0]
        if dim not in dims:
            continue
        value = at[dim]
        if value is None:
            index.append(slice(None))
        elif name == "zl":
            index.append(lax.rem(value, 2))
        elif name == "zh":
            index.append(value // 2)
        else:
            index.append(value)
    return ref.at[(*index, pl.ds(lo, n), slice(None))]


def lead(dims):
    return tuple(s for name, s in (("zl", 2), ("y", 4), ("x", 4), ("zh", 2)) if name[0] in dims)


def each(shape, body):
    total = 1
    for s in shape:
        total *= s
    if total == 1:
        body(())
        return

    def step(i, carry):
        index = []
        for s in reversed(shape):
            index.append(lax.rem(i, s))
            i = i // s
        body(tuple(reversed(index)))
        return carry

    lax.fori_loop(0, total, step, 0)


def reduce_scratch():
    shapes = []
    for k in range(3):
        n, h = CN[k], CH[k]
        for q in range(3):
            dims = lead(ORDER[k][: 2 - q])
            for rows in (h, n - h, h, n - h, h, n - h):
                shapes.append(pltpu.VMEM((*dims, rows, TOK), jnp.bfloat16))
            if q < 2:
                shapes.append(pltpu.VMEM((*dims, n, TOK), jnp.bfloat16))
    return shapes


def reduce_error(me, parts, base, err, slots, send, recv):
    slots = list(slots)
    table = []
    for k in range(3):
        row = []
        for q in range(3):
            row.append([slots.pop(0) for _ in range(7 if q < 2 else 6)])
        table.append(row)
    started = []

    def source(k, q, at, lo, n):
        if q == 0:
            return region(parts, at, C0[k] + lo, n)
        return held(table[k][q - 1][6], ORDER[k][: 3 - q], at, lo, n)

    for q in range(3):
        first = []
        for k in range(3):
            dim, rest = ORDER[k][2 - q], ORDER[k][: 2 - q]
            n, h = CN[k], CH[k]
            at = {d: (None if d in rest else me[d]) for d in me}
            far = {**at, dim: shift(me, dim, 2)}
            up, down = shift(me, dim, 1), shift(me, dim, -1)
            opp_p, opp_m, sum_p, raw_p, raw_m, sum_m = table[k][q][:6]
            copies = [
                remote(source(k, q, far, 0, h), opp_p, send.at[k, q, 0], recv.at[k, q, 0], dim, up),
                remote(source(k, q, far, h, n - h), opp_m, send.at[k, q, 1], recv.at[k, q, 1], dim, down),
                remote(source(k, q, {**at, dim: up}, h, n - h), raw_p, send.at[k, q, 2], recv.at[k, q, 2], dim, up),
                remote(source(k, q, {**at, dim: down}, 0, h), raw_m, send.at[k, q, 3], recv.at[k, q, 3], dim, down),
            ]
            for c in copies:
                c.start()
            first.append(copies)
            started += copies
        second = []
        for k in range(3):
            dim, rest = ORDER[k][2 - q], ORDER[k][: 2 - q]
            n, h = CN[k], CH[k]
            at = {d: (None if d in rest else me[d]) for d in me}
            up, down = shift(me, dim, 1), shift(me, dim, -1)
            opp_p, opp_m, sum_p, raw_p, raw_m, sum_m = table[k][q][:6]
            copies = []
            for s, (slot, to, lo, rows, into) in enumerate(((opp_p, up, 0, h, sum_p), (opp_m, down, h, n - h, sum_m))):
                first[k][s].wait_recv()
                own = source(k, q, {**at, dim: to}, lo, rows)

                def add(index, slot=slot, own=own):
                    a = slot[index].astype(jnp.float32) + own[index].astype(jnp.float32)
                    slot[index] = a.astype(jnp.bfloat16)

                each(lead(rest), add)
                c = remote(slot, into, send.at[k, q, 4 + s], recv.at[k, q, 4 + s], dim, to)
                c.start()
                copies.append(c)
            second.append(copies)
            started += copies
        for k in range(3):
            dim, rest = ORDER[k][2 - q], ORDER[k][: 2 - q]
            n, h = CN[k], CH[k]
            at = {d: (None if d in rest else me[d]) for d in me}
            opp_p, opp_m, sum_p, raw_p, raw_m, sum_m = table[k][q][:6]
            first[k][2].wait_recv()
            first[k][3].wait_recv()
            second[k][0].wait_recv()
            second[k][1].wait_recv()
            for lo, rows, a, b in ((0, h, sum_p, raw_m), (h, n - h, raw_p, sum_m)):
                own = source(k, q, at, lo, rows)

                def add(index, own=own, a=a, b=b, lo=lo, rows=rows):
                    total = own[index].astype(jnp.float32) + a[index].astype(jnp.float32) + b[index].astype(jnp.float32)
                    if q < 2:
                        table[k][q][6][(*index, pl.ds(lo, rows), slice(None))] = total.astype(jnp.bfloat16)
                    else:
                        at_rows = pl.ds(C0[k] + lo, rows)
                        err[at_rows, :] = (total + base[at_rows, :]).astype(jnp.bfloat16)

                each(lead(rest), add)
    return started


def params(collective=None):
    return pltpu.CompilerParams(collective_id=collective, has_side_effects=collective is not None,
                                vmem_limit_bytes=60 * 1024 * 1024)


PIECES = (2, 4, 4, 2, ROWS, TOK)
VMEM = pl.BlockSpec(memory_space=pltpu.VMEM)
ANY = pl.BlockSpec(memory_space=pl.ANY)


def gather_kernel(own, out, local, send, recv):
    me = coords()
    barrier(me)
    gather(me, own, out, local, send, recv)


def gather_call(x):
    return pl.pallas_call(
        gather_kernel,
        out_shape=jax.ShapeDtypeStruct(PIECES, jnp.bfloat16),
        in_specs=[VMEM], out_specs=ANY,
        scratch_shapes=[pltpu.SemaphoreType.DMA, pltpu.SemaphoreType.DMA((3, 3, 4)), pltpu.SemaphoreType.DMA((3, 3, 4))],
        compiler_params=params(0), name="gather",
        cost_estimate=pl.CostEstimate(flops=0, bytes_accessed=150_000_000, transcendentals=0),
    )(x)


def error_kernel(parts, base, err, out, local, send, recv, rsend, rrecv, *slots):
    me = coords()
    barrier(me)
    started = reduce_error(me, parts, base, err, slots, rsend, rrecv)
    gather(me, err, out, local, send, recv)
    for c in started:
        c.wait_send()


def error_call(parts, base):
    dma = pltpu.SemaphoreType.DMA
    return pl.pallas_call(
        error_kernel,
        out_shape=(jax.ShapeDtypeStruct((ROWS, TOK), jnp.bfloat16), jax.ShapeDtypeStruct(PIECES, jnp.bfloat16)),
        in_specs=[VMEM, VMEM], out_specs=(VMEM, ANY),
        scratch_shapes=[dma, dma((3, 3, 4)), dma((3, 3, 4)), dma((3, 3, 6)), dma((3, 3, 6)), *reduce_scratch()],
        compiler_params=params(1), name="error",
    )(parts, base)


D = 3584
SPAN = 128
CHUNK = 896


def pick(sel, g, w, ws):
    for hh in range(2):
        ws[hh * SPAN : (hh + 1) * SPAN, :] = w[hh * 4 + sel[g, hh]]


def encode_kernel(sel, named, cen, w, bias, part, lat, mask, ws):
    g = pl.program_id(0)
    pick(sel, g, w, ws)
    pre = jnp.dot(ws[...], cen[0], preferred_element_type=jnp.float32)
    lane = lax.broadcasted_iota(jnp.int32, (SPAN, TOK), 1)
    for hh in range(2):
        rows = slice(hh * SPAN, (hh + 1) * SPAN)
        p = pre[rows] + bias[hh * 4 + sel[g, hh]]
        on = jnp.where(lane < SPAN, named[g, hh], named[g, 2 + hh])
        keep = (on > 0) & (p > 0)
        lat[0, rows] = jnp.where(keep, p, 0.0).astype(jnp.bfloat16)
        mask[0, rows] = jnp.where(keep, 1.0, 0.0).astype(jnp.bfloat16)
    for i in range(0, D, CHUNK):
        part[0, i : i + CHUNK] = lax.dot_general(
            ws[:, i : i + CHUNK], lat[0], (((0,), (0,)), ((), ())), preferred_element_type=jnp.float32
        ).astype(jnp.bfloat16)


def encode_call(sel, named, cen, w, bias):
    per = lambda *shape: pl.BlockSpec((1, *shape), lambda g, *_: (g, 0, 0))
    return pl.pallas_call(
        encode_kernel,
        out_shape=(
            jax.ShapeDtypeStruct((8, D, TOK), jnp.bfloat16),
            jax.ShapeDtypeStruct((8, 2 * SPAN, TOK), jnp.bfloat16),
            jax.ShapeDtypeStruct((8, 2 * SPAN, TOK), jnp.bfloat16),
        ),
        grid_spec=pltpu.PrefetchScalarGridSpec(
            num_scalar_prefetch=2, grid=(8,),
            in_specs=[per(D, TOK), VMEM, VMEM],
            out_specs=(per(D, TOK), per(2 * SPAN, TOK), per(2 * SPAN, TOK)),
            scratch_shapes=[pltpu.VMEM((2 * SPAN, D), jnp.bfloat16)],
        ),
        compiler_params=params(), name="encode",
    )(sel, named, cen, w, bias)


def grad_kernel(sel, err, cen, lat, mask, w, own, other, gb, ws, acc):
    g = pl.program_id(0)

    @pl.when(g == 0)
    def _():
        own[...] = jnp.zeros_like(own)
        acc[...] = jnp.zeros_like(acc)
        gb[...] = jnp.zeros_like(gb)

    pick(sel, g, w, ws)
    back = jnp.dot(ws[...], err[0], preferred_element_type=jnp.float32)
    slope = jnp.where(mask[0] > 0, back, 0.0).astype(jnp.bfloat16)
    ones = jnp.ones((TOK, SPAN), jnp.bfloat16)
    sums = jnp.dot(slope, ones, preferred_element_type=jnp.float32).astype(jnp.bfloat16).astype(jnp.float32)
    for hh in range(2):
        gb[hh * 4 + sel[g, hh]] += sums[hh * SPAN : (hh + 1) * SPAN]
    for i in range(0, D, CHUNK):
        nt = (((1,), (1,)), ((), ()))
        t = lax.dot_general(lat[0], err[0, i : i + CHUNK], nt, preferred_element_type=jnp.float32)
        t = t + lax.dot_general(slope, cen[0, i : i + CHUNK], nt, preferred_element_type=jnp.float32)
        t = t.astype(jnp.bfloat16).astype(jnp.float32)
        own[sel[g, 0], :, i : i + CHUNK] += t[:SPAN]
        acc[sel[g, 1], :, i : i + CHUNK] += t[SPAN:]

    @pl.when(g == 7)
    def _():
        for b in range(4):
            other[b] = acc[b].astype(jnp.bfloat16)


def grad_call(sel, err, cen, lat, mask, w):
    per = lambda *shape: pl.BlockSpec((1, *shape), lambda g, *_: (g, 0, 0))
    return pl.pallas_call(
        grad_kernel,
        out_shape=(
            jax.ShapeDtypeStruct((4, SPAN, D), jnp.float32),
            jax.ShapeDtypeStruct((4, SPAN, D), jnp.bfloat16),
            jax.ShapeDtypeStruct((8, SPAN, SPAN), jnp.float32),
        ),
        grid_spec=pltpu.PrefetchScalarGridSpec(
            num_scalar_prefetch=1, grid=(8,),
            in_specs=[per(D, TOK), per(D, TOK), per(2 * SPAN, TOK), per(2 * SPAN, TOK), VMEM],
            out_specs=(VMEM, VMEM, VMEM),
            scratch_shapes=[pltpu.VMEM((2 * SPAN, D), jnp.bfloat16), pltpu.VMEM((4, SPAN, D), jnp.float32)],
        ),
        compiler_params=params(), name="grad",
    )(sel, err, cen, lat, mask, w)


NAMES = ("x", "zh", "zl", "y", "c")
SWAP = [(0, 1), (1, 0)]


def step(activations, dictionary, enc_bias, dec_bias, block_codes):
    d = lax.axis_index("x") * 2 + lax.axis_index("zh")
    c = lax.axis_index("c")
    chip = lax.axis_index("zl") * 4 + lax.axis_index("y")
    mine = dictionary.reshape(4, SPAN, D)
    theirs = lax.ppermute(mine, "c", SWAP)
    bias_theirs = lax.ppermute(enc_bias, "c", SWAP)
    codes = lax.dynamic_index_in_dim(block_codes, d, axis=1, keepdims=False)
    codes = lax.all_gather(codes, ("zl", "y"), axis=0)
    act_t = activations.T.astype(jnp.float32)
    dec = lax.dynamic_slice_in_dim(dec_bias, d * ROWS, ROWS)[:, None]
    cen = gather_call((act_t - dec).astype(jnp.bfloat16)).reshape(8, D, TOK)
    first = d * 64 + (chip * 2 + jnp.stack([c, 1 - c])) * 4
    local = codes[:, :, None, :] - first[:, None]
    hit = (codes[:, :, None, :] >= 0) & (local >= 0) & (local < 4)
    named = jnp.any(hit, axis=3).astype(jnp.int32).reshape(8, 4)
    sel = jnp.max(jnp.where(hit, local, 0), axis=(1, 3)).astype(jnp.int32)
    w = jnp.concatenate([mine, theirs])
    bias = jnp.concatenate([enc_bias, bias_theirs]).astype(jnp.float32).reshape(8, SPAN, 1)
    part, lat, mask = encode_call(sel, named, cen, w, bias)
    err_own, err = error_call(part.reshape(PIECES), dec - act_t)
    own, other, gb = grad_call(sel, err.reshape(8, D, TOK), cen, lat, mask, w)
    gb = gb[:, :, 0]
    grad_w = own + lax.ppermute(other, "c", SWAP).astype(jnp.float32)
    grad_b = gb[:4] + lax.ppermute(gb[4:], "c", SWAP)
    return err_own.T, grad_w.reshape(4 * SPAN, D), grad_b.reshape(4 * SPAN)


def solution(mesh):
    split = Mesh(mesh.devices.reshape(4, 2, 2, 4, 2), NAMES)
    dict_, dp = ("x", "zh"), ("zl", "y", "c")
    rows = P((*dict_, *dp))
    return jax.shard_map(
        step, mesh=split,
        in_specs=(P(dp, dict_), P((*dict_, *dp), None), rows, P(), P(dp, None, None)),
        out_specs=(P(dp, dict_), P((*dict_, *dp), None), rows),
        check_vma=False,
    )
```

time: 763 us -> 307 us (0.40)
  waiting for transfers between devices: 550 us -> 4.92 us
  Pallas kernels: 0 us -> 243 us
  matrix products: 94.4 us -> 0 us
  local copies, waits for them, and re-layouts: 44.6 us -> 5.14 us
  between operations: 14.2 us -> 0.72 us
    pallas_call x0 -> x4, Pallas kernels: none -> 243 us  [the longest x1 121 us: error_call(): pl.pallas_call(error_kernel, out_shape=(jax.ShapeDtypeStruct((ROWS, TOK),...]
    all_to_all x4 -> x0, waiting for transfers between devices: 214 us -> none  [the longest x1 195 us: shards(): lax.all_to_all(weight_terms, 'dp', split_axis=0, concat_axis=0, tiled=True)]
    all_gather x1 -> x0, waiting for transfers between devices: 171 us -> none  [shards(): gathered = lax.all_gather(activations, 'dict', axis=1, tiled=True)]
    psum x1 -> x0, waiting for transfers between devices: 165 us -> none  [shards(): summed = lax.psum(partial_product, 'dict')]
    dot_general x37 -> x0, matrix products: 94.4 us -> none  [the longest x16 35.5 us: block_grad(): lax.dot_general(slope_one, mean_removed, (((0,), (0,)), ((), ())), prefer...]
    all_to_all x4 -> x0, starting transfers between devices: 20.8 us -> none  [the longest x1 5.79 us: shards(): lax.all_to_all(send_w, 'dp', split_axis=0, concat_axis=0, tiled=True)]
    ppermute x0 -> x4, starting transfers between devices: none -> 19.6 us  [the longest x1 18 us: step(): grad_w = own + lax.ppermute(other, 'c', SWAP).astype(jnp.float32)]
    while x32 -> x0, local copies, waits for them, and re-layouts: 17 us -> none
  transfers between devices with their start and end apart: 6 -> 4, of which waited for: 4 -> 1; matrix products, arithmetic and copies ran while one was open for 9% -> 2% of each run, Pallas kernels for 0% -> 21%
where the time goes in v1:
time: 307 us
  Pallas kernels  243 us (79%)
  starting transfers between devices  19.6 us (6%)
  other arithmetic  17.2 us (6%)
  blocking collectives  15.8 us (5%)
  local copies, waits for them, and re-layouts  5.14 us (2%)
  waiting for transfers between devices  4.92 us (2%)
    pallas_call x1, Pallas kernels, error_call(): pl.pallas_call(error_kernel, out_shape=(jax.ShapeDtypeStruct((ROWS, TOK),...  121 us
    pallas_call x1, Pallas kernels, gather_call(): pl.pallas_call(gather_kernel, out_shape=jax.ShapeDtypeStruct(PIECES, jnp....  64.1 us
    pallas_call x1, Pallas kernels, grad_call(): pl.pallas_call(grad_kernel, out_shape=(jax.ShapeDtypeStruct((4, SPAN, D),...  34.4 us
    pallas_call x1, Pallas kernels, encode_call(): pl.pallas_call(encode_kernel, out_shape=(jax.ShapeDtypeStruct((8, D, TOK)...  23.5 us
    ppermute x1, starting transfers between devices, step(): grad_w = own + lax.ppermute(other, 'c', SWAP).astype(jnp.float32)  18 us
    all_gather x1, blocking collectives, step(): codes = lax.all_gather(codes, ('zl', 'y'), axis=0)  15.8 us
    add x1, other arithmetic, step(): grad_w = own + lax.ppermute(other, 'c', SWAP).astype(jnp.float32)  7.35 us
    concatenate x1, other arithmetic, step(): w = jnp.concatenate([mine, theirs])  6.84 us
  transfers between devices with their start and end apart: 4, of which 1 were waited for; matrix products, arithmetic and copies ran while one was open for 2% of the time, Pallas kernels for 21%

profile of v1, /device:TPU:1, one launch (start us, length us, event | category | flops | bytes accessed | tf_op | source)
XLA Modules:
  0.0 306.7 jit_solution(2086785549456518206)
XLA Ops:
  0.6 0.0 copy-start
  0.6 1.5 collective-permute-start
  2.1 0.1 collective-permute-start.1
  2.2 0.0 copy-done
  2.2 15.8 %all-gather = s32[16,1,16]{2,1,0:T(1,128)S(1)} all-gather(s32[2,1,16]{2,1,0:T(1,128)S(1)} %constant_dynamic-slice_fusion), channel_id=2, replica_groups=mesh['x'=4,'zh'=2,'zl'=2,'y'=4,'c'=2] {'zl','y'}, dimensions={0}, use_global_device_ids=true | all-gather | bytes 1152 | tf_op jit(solution)/shard_map/all_gather | solution.py:387
  18.1 0.8 dynamic_slice.8
  18.8 0.1 fusion.8
  18.9 0.2 fusion.3
  19.1 1.9 fusion.1
  21.0 0.2 fusion.6
  21.2 0.7 copy.27.named
  21.9 0.7 copy.26.sel
  22.6 0.0 copy-start.3
  22.6 64.1 %gather.1 = bf16[2,4,4,2,448,256]{5,4,3,2,1,0:T(8,128)(2,1)} custom-call(bf16[448,256]{1,0:T(8,128)(2,1)} %get-tuple-element.22.own), custom_call_target="tpu_custom_call" | custom-call | bytes 150000000 | tf_op jit(solution)/shard_map/gather/pallas_call | solution.py:249
  86.7 0.0 collective-permute-done.1
  86.7 0.0 copy-done.3
  86.7 1.0 copy.28.bias
  87.8 0.0 collective-permute-done
  87.8 6.8 %pad_maximum_fusion.w = bf16[8,128,3584]{2,1,0:T(8,128)(2,1)} fusion(bf16[4,128,3584]{2,1,0:T(8,128)(2,1)} %collective-permute-done, bf16[4,128,3584]{2,1,0:T(8,128)(2,1)} %bitcast.24), kind=kLoop, calls=%fused_computation | loop fusion | flops 3670016 | bytes 14680064 | tf_op jit(solution)/shard_map/concatenate | solution.py:396
  94.6 23.5 %encode.1 = (bf16[8,3584,256]{2,1,0:T(8,128)(2,1)}, bf16[8,256,256]{2,1,0:T(8,128)(2,1)}, bf16[8,256,256]{2,1,0:T(8,128)(2,1)}) custom-call(s32[8,2]{1,0:T(8,128)} %copy.26.sel, s32[8,4]{1,0:T(8,128)} %copy.27.named, bf16[8,3584,256]{2,1,0:T(8,128)(2,1)} %bitcast.18, bf16[8,128,3584]{2,1,0:T(8,128)(2,1)} %pad_maximum_fusion.w, f32[8,128,1]{2,1,0:T(8,128)} %copy.28.bias), custom_call_target="tpu_custom_call" | custom-call | tf_op jit(solution)/shard_map/encode/pallas_call | solution.py:309
  118.1 121.3 %error.1 = (bf16[448,256]{1,0:T(8,128)(2,1)}, bf16[2,4,4,2,448,256]{5,4,3,2,1,0:T(8,128)(2,1)}) custom-call(bf16[2,4,4,2,448,256]{5,4,3,2,1,0:T(8,128)(2,1)} %bitcast.21, f32[448,256]{1,0:T(8,128)} %get-tuple-element.21.base), custom_call_target="tpu_custom_call" | custom-call | tf_op jit(solution)/shard_map/error/pallas_call | solution.py:270
  239.4 34.4 %grad.1 = (f32[4,128,3584]{2,1,0:T(8,128)}, bf16[4,128,3584]{2,1,0:T(8,128)(2,1)}, f32[8,128,128]{2,1,0:T(8,128)}) custom-call(s32[8,2]{1,0:T(8,128)} %copy.26.sel, bf16[8,3584,256]{2,1,0:T(8,128)(2,1)} %bitcast.20, bf16[8,3584,256]{2,1,0:T(8,128)(2,1)} %bitcast.19, bf16[8,256,256]{2,1,0:T(8,128)(2,1)} %get-tuple-element.14.lat, ...), custom_call_target="tpu_custom_call" | custom-call | tf_op jit(solution)/shard_map/grad/pallas_call | solution.py:358
  273.8 18.0 %collective-permute-start.2 = (bf16[4,128,3584]{2,1,0:T(8,128)(2,1)}, bf16[4,128,3584]{2,1,0:T(8,128)(2,1)S(1)}, u32[]{:S(2)}, u32[]{:S(2)}) collective-permute-start(bf16[4,128,3584]{2,1,0:T(8,128)(2,1)} %get-tuple-element.17), channel_id=1, source_target_pairs={{0,1},{1,0},{2,3},{3,2},{4,5},{5,4},{6,7},{7,6},{8,9},{9,8},{10,11... | collective-permute-start | bytes 11010056 | tf_op jit(solution)/shard_map/ppermute | solution.py:402
  291.8 1.2 slice_reduce_fusion
  293.0 0.1 collective-permute-start.3
  293.1 4.9 %collective-permute-done.3 = f32[4,128]{1,0:T(4,128)S(1)} collective-permute-done((f32[4,128]{1,0:T(4,128)S(1)}, f32[4,128]{1,0:T(4,128)S(1)}, u32[]{:S(2)}, u32[]{:S(2)}) %collective-permute-start.3) | collective-permute-done | bytes 2080 | tf_op jit(solution)/shard_map/ppermute | solution.py:403
  298.0 0.6 add_bitcast_fusion
  298.6 0.0 collective-permute-done.2
  298.6 0.0 copy-start.1
  298.6 0.0 copy-start.2
  298.6 7.3 %convert_add_fusion = f32[4,128,3584]{2,1,0:T(8,128)} fusion(f32[4,128,3584]{2,1,0:T(8,128)} %get-tuple-element.16, bf16[4,128,3584]{2,1,0:T(8,128)(2,1)S(1)} %collective-permute-done.2), kind=kLoop, calls=%fused_computation.1 | loop fusion | flops 3670016 | bytes 18350080 | tf_op jit(solution)/shard_map/add | solution.py:402
  306.0 0.0 copy-done.2
  306.0 0.7 copy.31
  306.7 0.0 copy-done.1
  (6 shorter events, 0.0 us)
Async XLA Ops:
  0.6 1.6 copy-start
  0.6 87.1 %collective-permute-start = (bf16[4,128,3584]{2,1,0:T(8,128)(2,1)}, bf16[4,128,3584]{2,1,0:T(8,128)(2,1)}, u32[]{:S(2)}, u32[]{:S(2)}) collective-permute-start(bf16[4,128,3584]{2,1,0:T(8,128)(2,1)} %bitcast.23), channel_id=1, source_target_pairs={{0,1},{1,0},{2,3},{3,2},{4,5},{5,4},{6,7},{7,6},{8,9},{9,8},{10,11... | collective-permute-start | bytes 11010056 | tf_op jit(solution)/shard_map/ppermute | solution.py:384
  2.1 84.6 %collective-permute-start.1 = (bf16[512]{0:T(512)(128)(2,1)}, bf16[512]{0:T(512)(128)(2,1)S(1)}, u32[]{:S(2)}, u32[]{:S(2)}) collective-permute-start(bf16[512]{0:T(512)(128)(2,1)} %param.7), channel_id=1, source_target_pairs={{0,1},{1,0},{2,3},{3,2},{4,5},{5,4},{6,7},{7,6},{8,9},{9,8},{10,11... | collective-permute-start | bytes 3080 | tf_op jit(solution)/shard_map/ppermute | solution.py:385
  22.6 64.1 %copy-start.3 = (bf16[512]{0:T(512)(128)(2,1)S(1)}, bf16[512]{0:T(512)(128)(2,1)}, u32[]{:S(2)}) copy-start(bf16[512]{0:T(512)(128)(2,1)} %param.7) | copy-start | bytes 3076
  273.8 24.8 %collective-permute-start.2 = (bf16[4,128,3584]{2,1,0:T(8,128)(2,1)}, bf16[4,128,3584]{2,1,0:T(8,128)(2,1)S(1)}, u32[]{:S(2)}, u32[]{:S(2)}) collective-permute-start(bf16[4,128,3584]{2,1,0:T(8,128)(2,1)} %get-tuple-element.17), channel_id=1, source_target_pairs={{0,1},{1,0},{2,3},{3,2},{4,5},{5,4},{6,7},{7,6},{8,9},{9,8},{10,11... | collective-permute-start | bytes 11010056 | tf_op jit(solution)/shard_map/ppermute | solution.py:402
  293.0 5.0 %collective-permute-start.3 = (f32[4,128]{1,0:T(4,128)S(1)}, f32[4,128]{1,0:T(4,128)S(1)}, u32[]{:S(2)}, u32[]{:S(2)}) collective-permute-start(f32[4,128]{1,0:T(4,128)S(1)} %get-tuple-element.19), channel_id=1, source_target_pairs={{0,1},{1,0},{2,3},{3,2},{4,5},{5,4},{6,7},{7,6},{8,9},{9,8},{10,11... | collective-permute-start | bytes 6152 | tf_op jit(solution)/shard_map/ppermute | solution.py:403
  298.6 8.0 %copy-start.1 = (s32[2,8,16]{2,1,0:T(8,128)S(1)}, s32[2,8,16]{2,1,0:T(8,128)}, u32[]{:S(2)}) copy-start(s32[2,8,16]{2,1,0:T(8,128)} %param.9) | copy-start | bytes 3076
  298.6 7.4 %copy-start.2 = (bf16[448,256]{1,0:T(8,128)(2,1)S(1)}, bf16[448,256]{1,0:T(8,128)(2,1)}, u32[]{:S(2)}) copy-start(bf16[448,256]{1,0:T(8,128)(2,1)} %get-tuple-element.12) | copy-start | bytes 688132

commit v2 on v1

--- a/solution.py
+++ b/solution.py
@@ -52,46 +52,100 @@
     pl.semaphore_wait(sem, 6)
 
 
-def gather(me, own, out, local, send, recv):
+NEAR = ((0, 1), (1, -1))
+
+
+def gather(me, own, out, local, send, recv, beside=iter(())):
     mine = pltpu.make_async_copy(own, region(out, me, 0, ROWS), local)
     mine.start()
-    started = []
-    for p in range(3):
-        near = []
+    copies = [{} for _ in range(3)]
+
+    def go(k, phase, name, at, by, lo=0, n=None, src=None):
+        order = ORDER[k]
+        where = {d: (None if i < phase - 1 else shift(me, d, at.get(i, 0))) for i, d in enumerate(order)}
+        part = region(out, where, C0[k] + lo, CN[k] if n is None else n)
+        dim = order[phase]
+        i = len(copies[k])
+        c = remote(part if src is None else src, part, send.at[k, i], recv.at[k, i], dim, shift(me, dim, by))
+        c.start()
+        copies[k][(phase, *name)] = c
+
+    def got(k, *name):
+        copies[k][name].wait_recv()
+
+    for k in range(3):
+        src = own.at[pl.ds(C0[k], CN[k]), :]
+        for s, by in NEAR:
+            go(k, 0, ("near", s), {}, by, src=src)
+        for s, by in NEAR:
+            go(k, 1, ("near", 0, s), {}, by, src=src)
+    next(beside, None)
+    for k in range(3):
+        for s, by in NEAR:
+            got(k, 0, "near", s)
+            lo, n = (0, CH[k]) if s == 0 else (CH[k], CN[k] - CH[k])
+            go(k, 0, ("far", s), {0: -by}, by, lo, n)
+        for j in (-1, 1):
+            for s, by in NEAR:
+                go(k, 1, ("near", j, s), {0: j}, by)
+    mine.wait()
+    next(beside, None)
+    for k in range(3):
+        got(k, 0, "far", 0)
+        got(k, 0, "far", 1)
+        for s, by in NEAR:
+            go(k, 1, ("near", 2, s), {0: 2}, by)
+        for s, by in NEAR:
+            go(k, 2, ("near", 0, s), {1: 0}, by)
+    for phase in (1, 2):
+        next(beside, None)
+        for j in (0, -1, 1, 2):
+            for k in range(3):
+                for s, by in NEAR:
+                    got(k, phase, "near", j, s)
+                    if (j in (0, 1)) == (s == 0):
+                        go(k, phase, ("far", j), {phase - 1: j, phase: -by}, by)
+        if phase == 1:
+            for k in range(3):
+                for j in (-1, 1):
+                    for s, by in NEAR:
+                        go(k, 2, ("near", j, s), {1: j}, by)
         for k in range(3):
-            dim, prev = ORDER[k][p], ORDER[k][:p]
-            at = {d: (None if d in prev else me[d]) for d in me}
-            lo, n, h = C0[k], CN[k], CH[k]
-            copies = []
-            for s, by in enumerate((1, -1)):
-                src = own.at[pl.ds(lo, n), :] if p == 0 else region(out, at, lo, n)
-                c = remote(src, region(out, at, lo, n), send.at[k, p, s], recv.at[k, p, s], dim, shift(me, dim, by))
-                c.start()
-                copies.append(c)
-            near.append(copies)
-            started += copies
-        far = []
-        for k in range(3):
-            dim, prev = ORDER[k][p], ORDER[k][:p]
-            lo, n, h = C0[k], CN[k], CH[k]
-            copies = []
-            for s, by in enumerate((1, -1)):
-                at = {d: (None if d in prev else me[d]) for d in me}
-                at[dim] = shift(me, dim, -by)
-                near[k][s].wait_recv()
-                a, b = (lo, h) if s == 0 else (lo + h, n - h)
-                c = remote(region(out, at, a, b), region(out, at, a, b), send.at[k, p, 2 + s], recv.at[k, p, 2 + s],
-                           dim, shift(me, dim, by))
-                c.start()
-                copies.append(c)
-            far.append(copies)
-            started += copies
-        for k in range(3):
-            for c in far[k]:
-                c.wait_recv()
-        if p == 0:
-            mine.wait()
-    for c in started:
+            for j in (0, -1, 1, 2):
+                got(k, phase, "far", j)
+            if phase == 1:
+                for s, by in NEAR:
+                    go(k, 2, ("near", 2, s), {1: 2}, by)
+    for k in range(3):
+        for c in copies[k].values():
+            c.wait_send()
+
+
+def gather_codes(me, own, out, send, recv):
+    zl = lax.rem(me["z"], 2)
+    out[zl, me["y"]] = own[...]
+    copies = []
+
+    def go(src, dst, device_id):
+        i = len(copies)
+        c = pltpu.make_async_remote_copy(src_ref=src, dst_ref=dst, send_sem=send.at[i], recv_sem=recv.at[i],
+                                         device_id=device_id, device_id_type=pl.DeviceIdType.MESH)
+        c.start()
+        copies.append(c)
+
+    for by in (1, -1):
+        go(own, out.at[zl, me["y"]], device("y", shift(me, "y", by)))
+    yield
+    copies[0].wait_recv()
+    back = out.at[zl, shift(me, "y", -1)]
+    go(back, back, device("y", shift(me, "y", 1)))
+    yield
+    copies[1].wait_recv()
+    copies[2].wait_recv()
+    go(out.at[zl], out.at[zl], {"zl": 1 - zl})
+    yield
+    copies[3].wait_recv()
+    for c in copies:
         c.wait_send()
 
 
@@ -239,21 +293,25 @@
 ANY = pl.BlockSpec(memory_space=pl.ANY)
 
 
-def gather_kernel(own, out, local, send, recv):
+def gather_kernel(own, codes, out, all_codes, local, send, recv, csend, crecv):
     me = coords()
     barrier(me)
-    gather(me, own, out, local, send, recv)
-
-
-def gather_call(x):
+    gather(me, own, out, local, send, recv, gather_codes(me, codes, all_codes, csend, crecv))
+
+
+DMA = pltpu.SemaphoreType.DMA
+COPIES = 28
+
+
+def gather_call(x, codes):
     return pl.pallas_call(
         gather_kernel,
-        out_shape=jax.ShapeDtypeStruct(PIECES, jnp.bfloat16),
-        in_specs=[VMEM], out_specs=ANY,
-        scratch_shapes=[pltpu.SemaphoreType.DMA, pltpu.SemaphoreType.DMA((3, 3, 4)), pltpu.SemaphoreType.DMA((3, 3, 4))],
+        out_shape=(jax.ShapeDtypeStruct(PIECES, jnp.bfloat16), jax.ShapeDtypeStruct((2, 4, 8, 128), jnp.int32)),
+        in_specs=[VMEM, VMEM], out_specs=(ANY, VMEM),
+        scratch_shapes=[DMA, DMA((3, COPIES)), DMA((3, COPIES)), DMA((4,)), DMA((4,))],
         compiler_params=params(0), name="gather",
         cost_estimate=pl.CostEstimate(flops=0, bytes_accessed=150_000_000, transcendentals=0),
-    )(x)
+    )(x, codes)
 
 
 def error_kernel(parts, base, err, out, local, send, recv, rsend, rrecv, *slots):
@@ -266,12 +324,11 @@
 
 
 def error_call(parts, base):
-    dma = pltpu.SemaphoreType.DMA
     return pl.pallas_call(
         error_kernel,
         out_shape=(jax.ShapeDtypeStruct((ROWS, TOK), jnp.bfloat16), jax.ShapeDtypeStruct(PIECES, jnp.bfloat16)),
         in_specs=[VMEM, VMEM], out_specs=(VMEM, ANY),
-        scratch_shapes=[dma, dma((3, 3, 4)), dma((3, 3, 4)), dma((3, 3, 6)), dma((3, 3, 6)), *reduce_scratch()],
+        scratch_shapes=[DMA, DMA((3, COPIES)), DMA((3, COPIES)), DMA((3, 3, 6)), DMA((3, 3, 6)), *reduce_scratch()],
         compiler_params=params(1), name="error",
     )(parts, base)
 
@@ -281,14 +338,14 @@
 CHUNK = 896
 
 
-def pick(sel, g, w, ws):
-    for hh in range(2):
-        ws[hh * SPAN : (hh + 1) * SPAN, :] = w[hh * 4 + sel[g, hh]]
-
-
-def encode_kernel(sel, named, cen, w, bias, part, lat, mask, ws):
+def pick(sel, g, mine, theirs, ws):
+    ws[:SPAN, :] = mine[sel[g, 0]]
+    ws[SPAN:, :] = theirs[sel[g, 1]]
+
+
+def encode_kernel(sel, named, cen, mine, theirs, bias, part, lat, mask, ws):
     g = pl.program_id(0)
-    pick(sel, g, w, ws)
+    pick(sel, g, mine, theirs, ws)
     pre = jnp.dot(ws[...], cen[0], preferred_element_type=jnp.float32)
     lane = lax.broadcasted_iota(jnp.int32, (SPAN, TOK), 1)
     for hh in range(2):
@@ -304,7 +361,7 @@
         ).astype(jnp.bfloat16)
 
 
-def encode_call(sel, named, cen, w, bias):
+def encode_call(sel, named, cen, mine, theirs, bias):
     per = lambda *shape: pl.BlockSpec((1, *shape), lambda g, *_: (g, 0, 0))
     return pl.pallas_call(
         encode_kernel,
@@ -315,15 +372,15 @@
         ),
         grid_spec=pltpu.PrefetchScalarGridSpec(
             num_scalar_prefetch=2, grid=(8,),
-            in_specs=[per(D, TOK), VMEM, VMEM],
+            in_specs=[per(D, TOK), VMEM, VMEM, VMEM],
             out_specs=(per(D, TOK), per(2 * SPAN, TOK), per(2 * SPAN, TOK)),
             scratch_shapes=[pltpu.VMEM((2 * SPAN, D), jnp.bfloat16)],
         ),
         compiler_params=params(), name="encode",
-    )(sel, named, cen, w, bias)
-
-
-def grad_kernel(sel, err, cen, lat, mask, w, own, other, gb, ws, acc):
+    )(sel, named, cen, mine, theirs, bias)
+
+
+def grad_kernel(sel, err, cen, lat, mask, mine, theirs, own, other, gb, ws, acc):
     g = pl.program_id(0)
 
     @pl.when(g == 0)
@@ -332,7 +389,7 @@
         acc[...] = jnp.zeros_like(acc)
         gb[...] = jnp.zeros_like(gb)
 
-    pick(sel, g, w, ws)
+    pick(sel, g, mine, theirs, ws)
     back = jnp.dot(ws[...], err[0], preferred_element_type=jnp.float32)
     slope = jnp.where(mask[0] > 0, back, 0.0).astype(jnp.bfloat16)
     ones = jnp.ones((TOK, SPAN), jnp.bfloat16)
@@ -353,7 +410,7 @@
             other[b] = acc[b].astype(jnp.bfloat16)
 
 
-def grad_call(sel, err, cen, lat, mask, w):
+def grad_call(sel, err, cen, lat, mask, mine, theirs):
     per = lambda *shape: pl.BlockSpec((1, *shape), lambda g, *_: (g, 0, 0))
     return pl.pallas_call(
         grad_kernel,
@@ -364,12 +421,12 @@
         ),
         grid_spec=pltpu.PrefetchScalarGridSpec(
             num_scalar_prefetch=1, grid=(8,),
-            in_specs=[per(D, TOK), per(D, TOK), per(2 * SPAN, TOK), per(2 * SPAN, TOK), VMEM],
+            in_specs=[per(D, TOK), per(D, TOK), per(2 * SPAN, TOK), per(2 * SPAN, TOK), VMEM, VMEM],
             out_specs=(VMEM, VMEM, VMEM),
             scratch_shapes=[pltpu.VMEM((2 * SPAN, D), jnp.bfloat16), pltpu.VMEM((4, SPAN, D), jnp.float32)],
         ),
         compiler_params=params(), name="grad",
-    )(sel, err, cen, lat, mask, w)
+    )(sel, err, cen, lat, mask, mine, theirs)
 
 
 NAMES = ("x", "zh", "zl", "y", "c")
@@ -384,20 +441,21 @@
     theirs = lax.ppermute(mine, "c", SWAP)
     bias_theirs = lax.ppermute(enc_bias, "c", SWAP)
     codes = lax.dynamic_index_in_dim(block_codes, d, axis=1, keepdims=False)
-    codes = lax.all_gather(codes, ("zl", "y"), axis=0)
+    codes = jnp.pad(codes.reshape(1, 32), ((0, 7), (0, 96)), constant_values=-1)
     act_t = activations.T.astype(jnp.float32)
     dec = lax.dynamic_slice_in_dim(dec_bias, d * ROWS, ROWS)[:, None]
-    cen = gather_call((act_t - dec).astype(jnp.bfloat16)).reshape(8, D, TOK)
+    cen, codes = gather_call((act_t - dec).astype(jnp.bfloat16), codes)
+    cen = cen.reshape(8, D, TOK)
+    codes = codes.reshape(8, 8, 128)[:, 0, :32].reshape(8, 2, 16)
     first = d * 64 + (chip * 2 + jnp.stack([c, 1 - c])) * 4
     local = codes[:, :, None, :] - first[:, None]
     hit = (codes[:, :, None, :] >= 0) & (local >= 0) & (local < 4)
     named = jnp.any(hit, axis=3).astype(jnp.int32).reshape(8, 4)
     sel = jnp.max(jnp.where(hit, local, 0), axis=(1, 3)).astype(jnp.int32)
-    w = jnp.concatenate([mine, theirs])
     bias = jnp.concatenate([enc_bias, bias_theirs]).astype(jnp.float32).reshape(8, SPAN, 1)
-    part, lat, mask = encode_call(sel, named, cen, w, bias)
+    part, lat, mask = encode_call(sel, named, cen, mine, theirs, bias)
     err_own, err = error_call(part.reshape(PIECES), dec - act_t)
-    own, other, gb = grad_call(sel, err.reshape(8, D, TOK), cen, lat, mask, w)
+    own, other, gb = grad_call(sel, err.reshape(8, D, TOK), cen, lat, mask, mine, theirs)
     gb = gb[:, :, 0]
     grad_w = own + lax.ppermute(other, "c", SWAP).astype(jnp.float32)
     grad_b = gb[:4] + lax.ppermute(gb[4:], "c", SWAP)

time: 307 us -> 280 us (0.912)
  blocking collectives: 15.8 us -> 0 us
  starting transfers between devices: 19.6 us -> 9.49 us
  other arithmetic: 17.2 us -> 11 us
    all_gather x1 -> x0, blocking collectives: 15.8 us -> none  [step(): codes = lax.all_gather(codes, ('zl', 'y'), axis=0)]
    ppermute x1, starting transfers between devices: 18 us -> 7.85 us  [step(): grad_w = own + lax.ppermute(other, 'c', SWAP).astype(jnp.float32)]
    concatenate x1 -> x0, other arithmetic: 6.84 us -> none  [step(): w = jnp.concatenate([mine, theirs])]
  transfers between devices with their start and end apart: 4 -> 4, of which waited for: 1 -> 1; matrix products, arithmetic and copies ran while one was open for 2% -> 3% of each run, Pallas kernels for 21% -> 23%
where the time goes in v2:
time: 280 us; the launch traced here: 279 us
  Pallas kernels  246 us (88%)
  other arithmetic  11 us (4%)
  starting transfers between devices  9.49 us (3%)
  local copies, waits for them, and re-layouts  6.65 us (2%)
  waiting for transfers between devices  4.92 us (2%)
    pallas_call x1, Pallas kernels, error_call(): pl.pallas_call(error_kernel, out_shape=(jax.ShapeDtypeStruct((ROWS, TOK),...  123 us
    pallas_call x1, Pallas kernels, gather_call(): pl.pallas_call(gather_kernel, out_shape=(jax.ShapeDtypeStruct(PIECES, jnp...  65.2 us
    pallas_call x1, Pallas kernels, grad_call(): pl.pallas_call(grad_kernel, out_shape=(jax.ShapeDtypeStruct((4, SPAN, D),...  34.6 us
    pallas_call x1, Pallas kernels, encode_call(): pl.pallas_call(encode_kernel, out_shape=(jax.ShapeDtypeStruct((8, D, TOK)...  23.6 us
    ppermute x1, starting transfers between devices, step(): grad_w = own + lax.ppermute(other, 'c', SWAP).astype(jnp.float32)  7.85 us
    add x1, other arithmetic, step(): grad_w = own + lax.ppermute(other, 'c', SWAP).astype(jnp.float32)  7.35 us
  transfers between devices with their start and end apart: 4, of which 1 were waited for; matrix products, arithmetic and copies ran while one was open for 3% of the time, Pallas kernels for 23%

profile of v2, /device:TPU:1, one launch (start us, length us, event | category | flops | bytes accessed | tf_op | source)
XLA Modules:
  0.0 279.1 jit_solution(778502095398109063)
XLA Ops:
  0.6 0.0 copy-start
  0.6 1.5 collective-permute-start
  2.1 0.1 collective-permute-start.1
  2.2 0.0 copy-done
  2.2 0.1 reshape.95
  2.3 0.8 dynamic_slice.7
  3.1 0.6 pad.4.codes
  3.7 1.9 fusion.1
  5.6 65.2 %gather.1 = (bf16[2,4,4,2,448,256]{5,4,3,2,1,0:T(8,128)(2,1)}, s32[2,4,8,128]{3,2,1,0:T(8,128)}) custom-call(bf16[448,256]{1,0:T(8,128)(2,1)} %get-tuple-element.26.own, s32[8,128]{1,0:T(8,128)} %pad.4.codes), custom_call_target="tpu_custom_call" | custom-call | bytes 150000000 | tf_op jit(solution)/shard_map/gather/pallas_call | solution.py:307
  70.8 0.8 slice_reduce_fusion.2
  71.6 0.1 broadcast_in_dim_reshape_squeeze.4
  71.7 0.1 fusion.8
  71.8 0.2 fusion.3
  72.0 0.2 fusion.6
  72.2 0.7 copy.27.named
  72.9 0.7 copy.26.sel
  73.5 0.0 collective-permute-done.1
  73.5 0.7 maximum_convert_fusion
  74.2 1.0 copy.28.bias
  75.3 0.0 collective-permute-done.theirs
  75.3 23.6 %encode.1 = (bf16[8,3584,256]{2,1,0:T(8,128)(2,1)}, bf16[8,256,256]{2,1,0:T(8,128)(2,1)}, bf16[8,256,256]{2,1,0:T(8,128)(2,1)}) custom-call(s32[8,2]{1,0:T(8,128)} %copy.26.sel, s32[8,4]{1,0:T(8,128)} %copy.27.named, bf16[8,3584,256]{2,1,0:T(8,128)(2,1)} %bitcast.18, bf16[4,128,3584]{2,1,0:T(8,128)(2,1)} %bitcast.21, ...), custom_call_target="tpu_custom_call" | custom-call | tf_op jit(solution)/shard_map/encode/pallas_call | solution.py:366
  98.8 122.9 %error.1 = (bf16[448,256]{1,0:T(8,128)(2,1)}, bf16[2,4,4,2,448,256]{5,4,3,2,1,0:T(8,128)(2,1)}) custom-call(bf16[2,4,4,2,448,256]{5,4,3,2,1,0:T(8,128)(2,1)} %bitcast.24, f32[448,256]{1,0:T(8,128)} %get-tuple-element.25.base), custom_call_target="tpu_custom_call" | custom-call | tf_op jit(solution)/shard_map/error/pallas_call | solution.py:327
  221.7 34.6 %grad.1 = (f32[4,128,3584]{2,1,0:T(8,128)}, bf16[4,128,3584]{2,1,0:T(8,128)(2,1)}, f32[8,128,128]{2,1,0:T(8,128)}) custom-call(s32[8,2]{1,0:T(8,128)} %copy.26.sel, bf16[8,3584,256]{2,1,0:T(8,128)(2,1)} %bitcast.23, bf16[8,3584,256]{2,1,0:T(8,128)(2,1)} %bitcast.19, bf16[8,256,256]{2,1,0:T(8,128)(2,1)} %get-tuple-element.18.lat, ...), custom_call_target="tpu_custom_call" | custom-call | tf_op jit(solution)/shard_map/grad/pallas_call | solution.py:415
  256.3 7.8 %collective-permute-start.2 = (bf16[4,128,3584]{2,1,0:T(8,128)(2,1)}, bf16[4,128,3584]{2,1,0:T(8,128)(2,1)S(1)}, u32[]{:S(2)}, u32[]{:S(2)}) collective-permute-start(bf16[4,128,3584]{2,1,0:T(8,128)(2,1)} %get-tuple-element.21), channel_id=1, source_target_pairs={{0,1},{1,0},{2,3},{3,2},{4,5},{5,4},{6,7},{7,6},{8,9},{9,8},{10,11... | collective-permute-start | bytes 11010056 | tf_op jit(solution)/shard_map/ppermute | solution.py:460
  264.2 1.2 slice_reduce_fusion
  265.4 0.1 collective-permute-start.3
  265.5 4.9 %collective-permute-done.3 = f32[4,128]{1,0:T(4,128)S(1)} collective-permute-done((f32[4,128]{1,0:T(4,128)S(1)}, f32[4,128]{1,0:T(4,128)S(1)}, u32[]{:S(2)}, u32[]{:S(2)}) %collective-permute-start.3) | collective-permute-done | bytes 2080 | tf_op jit(solution)/shard_map/ppermute | solution.py:461
  270.4 0.6 add_bitcast_fusion
  271.0 0.0 collective-permute-done.2
  271.0 0.0 copy-start.1
  271.0 0.0 copy-start.2
  271.0 7.3 %convert_add_fusion = f32[4,128,3584]{2,1,0:T(8,128)} fusion(f32[4,128,3584]{2,1,0:T(8,128)} %get-tuple-element.20, bf16[4,128,3584]{2,1,0:T(8,128)(2,1)S(1)} %collective-permute-done.2), kind=kLoop, calls=%fused_computation | loop fusion | flops 3670016 | bytes 18350080 | tf_op jit(solution)/shard_map/add | solution.py:460
  278.4 0.0 copy-done.2
  278.4 0.7 copy.32
  279.1 0.0 copy-done.1
  (4 shorter events, 0.0 us)
Async XLA Ops:
  0.6 1.6 copy-start
  0.6 74.6 %collective-permute-start = (bf16[4,128,3584]{2,1,0:T(8,128)(2,1)}, bf16[4,128,3584]{2,1,0:T(8,128)(2,1)}, u32[]{:S(2)}, u32[]{:S(2)}) collective-permute-start(bf16[4,128,3584]{2,1,0:T(8,128)(2,1)} %bitcast.20), channel_id=1, source_target_pairs={{0,1},{1,0},{2,3},{3,2},{4,5},{5,4},{6,7},{7,6},{8,9},{9,8},{10,11... | collective-permute-start | bytes 11010056 | tf_op jit(solution)/shard_map/ppermute | solution.py:441
  2.1 71.4 %collective-permute-start.1 = (bf16[512]{0:T(512)(128)(2,1)}, bf16[512]{0:T(512)(128)(2,1)S(1)}, u32[]{:S(2)}, u32[]{:S(2)}) collective-permute-start(bf16[512]{0:T(512)(128)(2,1)} %param.7), channel_id=1, source_target_pairs={{0,1},{1,0},{2,3},{3,2},{4,5},{5,4},{6,7},{7,6},{8,9},{9,8},{10,11... | collective-permute-start | bytes 3080 | tf_op jit(solution)/shard_map/ppermute | solution.py:442
  256.3 14.7 %collective-permute-start.2 = (bf16[4,128,3584]{2,1,0:T(8,128)(2,1)}, bf16[4,128,3584]{2,1,0:T(8,128)(2,1)S(1)}, u32[]{:S(2)}, u32[]{:S(2)}) collective-permute-start(bf16[4,128,3584]{2,1,0:T(8,128)(2,1)} %get-tuple-element.21), channel_id=1, source_target_pairs={{0,1},{1,0},{2,3},{3,2},{4,5},{5,4},{6,7},{7,6},{8,9},{9,8},{10,11... | collective-permute-start | bytes 11010056 | tf_op jit(solution)/shard_map/ppermute | solution.py:460
  265.4 5.0 %collective-permute-start.3 = (f32[4,128]{1,0:T(4,128)S(1)}, f32[4,128]{1,0:T(4,128)S(1)}, u32[]{:S(2)}, u32[]{:S(2)}) collective-permute-start(f32[4,128]{1,0:T(4,128)S(1)} %get-tuple-element.23), channel_id=1, source_target_pairs={{0,1},{1,0},{2,3},{3,2},{4,5},{5,4},{6,7},{7,6},{8,9},{9,8},{10,11... | collective-permute-start | bytes 6152 | tf_op jit(solution)/shard_map/ppermute | solution.py:461
  271.0 8.0 %copy-start.1 = (s32[2,8,16]{2,1,0:T(8,128)S(1)}, s32[2,8,16]{2,1,0:T(8,128)}, u32[]{:S(2)}) copy-start(s32[2,8,16]{2,1,0:T(8,128)} %param.9) | copy-start | bytes 3076
  271.0 7.4 %copy-start.2 = (bf16[448,256]{1,0:T(8,128)(2,1)S(1)}, bf16[448,256]{1,0:T(8,128)(2,1)}, u32[]{:S(2)}) copy-start(bf16[448,256]{1,0:T(8,128)(2,1)} %get-tuple-element.16) | copy-start | bytes 688132

commit v3 on v2

--- a/solution.py
+++ b/solution.py
@@ -6,6 +6,7 @@
 from jax.sharding import Mesh, PartitionSpec as P
 
 ROWS, TOK = 448, 256
+D, SPAN = 3584, 128
 C0 = (0, 144, 288)
 CN = (144, 144, 160)
 CH = (80, 64, 80)
@@ -43,13 +44,15 @@
         device_id=device(dim, value), device_id_type=pl.DeviceIdType.MESH)
 
 
-def barrier(me):
+def barrier(me, cores=False):
     sem = pltpu.get_barrier_semaphore()
     for dim in ("x", "y", "z"):
         for by in (-1, 1):
             pl.semaphore_signal(sem, inc=1, device_id=device(dim, shift(me, dim, by)),
                                 device_id_type=pl.DeviceIdType.MESH)
-    pl.semaphore_wait(sem, 6)
+    if cores:
+        pl.semaphore_signal(sem, inc=1, device_id={"c": 1 - lax.axis_index("c")}, device_id_type=pl.DeviceIdType.MESH)
+    pl.semaphore_wait(sem, 7 if cores else 6)
 
 
 NEAR = ((0, 1), (1, -1))
@@ -110,6 +113,7 @@
                 for j in (-1, 1):
                     for s, by in NEAR:
                         go(k, 2, ("near", j, s), {1: j}, by)
+        next(beside, None)
         for k in range(3):
             for j in (0, -1, 1, 2):
                 got(k, phase, "far", j)
@@ -203,7 +207,23 @@
     return shapes
 
 
-def reduce_error(me, parts, base, err, slots, send, recv):
+def fill(k, at, sel, wt, lat, parts):
+    dims = [d for d in ("z", "y", "x") if at[d] is None]
+    lo, n = C0[k], CN[k]
+
+    def one(index):
+        where = {**at, **dict(zip(dims, index, strict=True))}
+        zl, zh = lax.rem(where["z"], 2), where["z"] // 2
+        g = zl * 4 + where["y"]
+        rows = pl.ds(pl.multiple_of((where["x"] * 2 + zh) * ROWS + lo, 16), n)
+        w = jnp.concatenate([wt[sel[g, 0], rows, :], wt[4 + sel[g, 1], rows, :]], axis=1)
+        part = jnp.dot(w, lat[g], preferred_element_type=jnp.float32)
+        parts[zl, where["y"], where["x"], zh, pl.ds(lo, n), :] = part.astype(jnp.bfloat16)
+
+    each((4,) * len(dims), one)
+
+
+def reduce_error(me, make, parts, base, err, slots, send, recv):
     slots = list(slots)
     table = []
     for k in range(3):
@@ -227,16 +247,35 @@
             far = {**at, dim: shift(me, dim, 2)}
             up, down = shift(me, dim, 1), shift(me, dim, -1)
             opp_p, opp_m, sum_p, raw_p, raw_m, sum_m = table[k][q][:6]
+            if q == 0:
+                make(k, far)
             copies = [
                 remote(source(k, q, far, 0, h), opp_p, send.at[k, q, 0], recv.at[k, q, 0], dim, up),
                 remote(source(k, q, far, h, n - h), opp_m, send.at[k, q, 1], recv.at[k, q, 1], dim, down),
+            ]
+            for c in copies:
+                c.start()
+            first.append(copies)
+        for k in range(3):
+            dim, rest = ORDER[k][2 - q], ORDER[k][: 2 - q]
+            n, h = CN[k], CH[k]
+            at = {d: (None if d in rest else me[d]) for d in me}
+            up, down = shift(me, dim, 1), shift(me, dim, -1)
+            opp_p, opp_m, sum_p, raw_p, raw_m, sum_m = table[k][q][:6]
+            if q == 0:
+                make(k, {**at, dim: up})
+                make(k, {**at, dim: down})
+            copies = [
                 remote(source(k, q, {**at, dim: up}, h, n - h), raw_p, send.at[k, q, 2], recv.at[k, q, 2], dim, up),
                 remote(source(k, q, {**at, dim: down}, 0, h), raw_m, send.at[k, q, 3], recv.at[k, q, 3], dim, down),
             ]
             for c in copies:
                 c.start()
-            first.append(copies)
-            started += copies
+            first[k] += copies
+            started += first[k]
+        if q == 0:
+            for k in range(3):
+                make(k, {d: (None if d in ORDER[k][:2] else me[d]) for d in me})
         second = []
         for k in range(3):
             dim, rest = ORDER[k][2 - q], ORDER[k][: 2 - q]
@@ -293,48 +332,101 @@
 ANY = pl.BlockSpec(memory_space=pl.ANY)
 
 
-def gather_kernel(own, codes, out, all_codes, local, send, recv, csend, crecv):
+def turn(mine, wt, held_w, turned, sems, send, recv):
+    load = pltpu.make_async_copy(mine, held_w, sems.at[0])
+    load.start()
+    yield
+    yield
+    yield
+    load.wait()
+    yield
+
+    def block(i, carry):
+        b, j = i // (D // SPAN), pl.multiple_of(lax.rem(i, D // SPAN) * SPAN, SPAN)
+        turned[b, pl.ds(j, SPAN), :] = held_w[b, :, pl.ds(j, SPAN)].T
+        return carry
+
+    lax.fori_loop(0, 4 * (D // SPAN), block, 0)
+    yield
+    keep = pltpu.make_async_copy(turned, wt.at[pl.ds(0, 4)], sems.at[1])
+    give = pltpu.make_async_remote_copy(
+        src_ref=turned, dst_ref=wt.at[pl.ds(4, 4)], send_sem=send, recv_sem=recv,
+        device_id={"c": 1 - lax.axis_index("c")}, device_id_type=pl.DeviceIdType.MESH)
+    keep.start()
+    give.start()
+    yield
+    keep.wait()
+    give.wait()
+
+
+def both(*steps):
+    while True:
+        done = [next(s, "end") for s in steps]
+        if all(d == "end" for d in done):
+            return
+        yield
+
+
+def gather_kernel(own, codes, mine, out, all_codes, wt, local, send, recv, csend, crecv, held_w, turned, sems, wsend, wrecv):
     me = coords()
-    barrier(me)
-    gather(me, own, out, local, send, recv, gather_codes(me, codes, all_codes, csend, crecv))
+    barrier(me, True)
+    steps = both(gather_codes(me, codes, all_codes, csend, crecv), turn(mine, wt, held_w, turned, sems, wsend, wrecv))
+    gather(me, own, out, local, send, recv, steps)
+    for _ in steps:
+        pass
 
 
 DMA = pltpu.SemaphoreType.DMA
 COPIES = 28
 
 
-def gather_call(x, codes):
+def gather_call(x, codes, mine):
     return pl.pallas_call(
         gather_kernel,
-        out_shape=(jax.ShapeDtypeStruct(PIECES, jnp.bfloat16), jax.ShapeDtypeStruct((2, 4, 8, 128), jnp.int32)),
-        in_specs=[VMEM, VMEM], out_specs=(ANY, VMEM),
-        scratch_shapes=[DMA, DMA((3, COPIES)), DMA((3, COPIES)), DMA((4,)), DMA((4,))],
+        out_shape=(
+            jax.ShapeDtypeStruct(PIECES, jnp.bfloat16),
+            jax.ShapeDtypeStruct((2, 4, 8, 128), jnp.int32),
+            jax.ShapeDtypeStruct((8, D, SPAN), jnp.bfloat16),
+        ),
+        in_specs=[VMEM, VMEM, ANY], out_specs=(ANY, VMEM, ANY),
+        scratch_shapes=[
+            DMA, DMA((3, COPIES)), DMA((3, COPIES)), DMA((4,)), DMA((4,)),
+            pltpu.VMEM((4, SPAN, D), jnp.bfloat16), pltpu.VMEM((4, D, SPAN), jnp.bfloat16), DMA((2,)), DMA, DMA,
+        ],
         compiler_params=params(0), name="gather",
         cost_estimate=pl.CostEstimate(flops=0, bytes_accessed=150_000_000, transcendentals=0),
-    )(x, codes)
-
-
-def error_kernel(parts, base, err, out, local, send, recv, rsend, rrecv, *slots):
+    )(x, codes, mine)
+
+
+def error_kernel(sel, wt_hbm, lat, base, err, out, local, send, recv, rsend, rrecv, wt, wt_sem, parts, *slots):
     me = coords()
+    load = pltpu.make_async_copy(wt_hbm, wt, wt_sem)
+    load.start()
     barrier(me)
-    started = reduce_error(me, parts, base, err, slots, rsend, rrecv)
+    load.wait()
+
+    def make(k, at):
+        fill(k, at, sel, wt, lat, parts)
+
+    started = reduce_error(me, make, parts, base, err, slots, rsend, rrecv)
     gather(me, err, out, local, send, recv)
     for c in started:
         c.wait_send()
 
 
-def error_call(parts, base):
+def error_call(sel, wt, lat, base):
     return pl.pallas_call(
         error_kernel,
         out_shape=(jax.ShapeDtypeStruct((ROWS, TOK), jnp.bfloat16), jax.ShapeDtypeStruct(PIECES, jnp.bfloat16)),
-        in_specs=[VMEM, VMEM], out_specs=(VMEM, ANY),
-        scratch_shapes=[DMA, DMA((3, COPIES)), DMA((3, COPIES)), DMA((3, 3, 6)), DMA((3, 3, 6)), *reduce_scratch()],
+        in_specs=[pl.BlockSpec(memory_space=pltpu.SMEM), ANY, VMEM, VMEM], out_specs=(VMEM, ANY),
+        scratch_shapes=[
+            DMA, DMA((3, COPIES)), DMA((3, COPIES)), DMA((3, 3, 6)), DMA((3, 3, 6)),
+            pltpu.VMEM((8, D, SPAN), jnp.bfloat16), DMA, pltpu.VMEM(PIECES, jnp.bfloat16), *reduce_scratch(),
+        ],
         compiler_params=params(1), name="error",
-    )(parts, base)
-
-
-D = 3584
-SPAN = 128
+    )(sel, wt, lat, base)
+
+
 CHUNK = 896
 
 
@@ -343,7 +435,7 @@
     ws[SPAN:, :] = theirs[sel[g, 1]]
 
 
-def encode_kernel(sel, named, cen, mine, theirs, bias, part, lat, mask, ws):
+def encode_kernel(sel, named, cen, mine, theirs, bias, lat, mask, ws):
     g = pl.program_id(0)
     pick(sel, g, mine, theirs, ws)
     pre = jnp.dot(ws[...], cen[0], preferred_element_type=jnp.float32)
@@ -355,10 +447,6 @@
         keep = (on > 0) & (p > 0)
         lat[0, rows] = jnp.where(keep, p, 0.0).astype(jnp.bfloat16)
         mask[0, rows] = jnp.where(keep, 1.0, 0.0).astype(jnp.bfloat16)
-    for i in range(0, D, CHUNK):
-        part[0, i : i + CHUNK] = lax.dot_general(
-            ws[:, i : i + CHUNK], lat[0], (((0,), (0,)), ((), ())), preferred_element_type=jnp.float32
-        ).astype(jnp.bfloat16)
 
 
 def encode_call(sel, named, cen, mine, theirs, bias):
@@ -366,14 +454,13 @@
     return pl.pallas_call(
         encode_kernel,
         out_shape=(
-            jax.ShapeDtypeStruct((8, D, TOK), jnp.bfloat16),
             jax.ShapeDtypeStruct((8, 2 * SPAN, TOK), jnp.bfloat16),
             jax.ShapeDtypeStruct((8, 2 * SPAN, TOK), jnp.bfloat16),
         ),
         grid_spec=pltpu.PrefetchScalarGridSpec(
             num_scalar_prefetch=2, grid=(8,),
             in_specs=[per(D, TOK), VMEM, VMEM, VMEM],
-            out_specs=(per(D, TOK), per(2 * SPAN, TOK), per(2 * SPAN, TOK)),
+            out_specs=(per(2 * SPAN, TOK), per(2 * SPAN, TOK)),
             scratch_shapes=[pltpu.VMEM((2 * SPAN, D), jnp.bfloat16)],
         ),
         compiler_params=params(), name="encode",
@@ -444,7 +531,7 @@
     codes = jnp.pad(codes.reshape(1, 32), ((0, 7), (0, 96)), constant_values=-1)
     act_t = activations.T.astype(jnp.float32)
     dec = lax.dynamic_slice_in_dim(dec_bias, d * ROWS, ROWS)[:, None]
-    cen, codes = gather_call((act_t - dec).astype(jnp.bfloat16), codes)
+    cen, codes, wt = gather_call((act_t - dec).astype(jnp.bfloat16), codes, mine)
     cen = cen.reshape(8, D, TOK)
     codes = codes.reshape(8, 8, 128)[:, 0, :32].reshape(8, 2, 16)
     first = d * 64 + (chip * 2 + jnp.stack([c, 1 - c])) * 4
@@ -453,8 +540,8 @@
     named = jnp.any(hit, axis=3).astype(jnp.int32).reshape(8, 4)
     sel = jnp.max(jnp.where(hit, local, 0), axis=(1, 3)).astype(jnp.int32)
     bias = jnp.concatenate([enc_bias, bias_theirs]).astype(jnp.float32).reshape(8, SPAN, 1)
-    part, lat, mask = encode_call(sel, named, cen, mine, theirs, bias)
-    err_own, err = error_call(part.reshape(PIECES), dec - act_t)
+    lat, mask = encode_call(sel, named, cen, mine, theirs, bias)
+    err_own, err = error_call(sel, wt, lat, dec - act_t)
     own, other, gb = grad_call(sel, err.reshape(8, D, TOK), cen, lat, mask, mine, theirs)
     gb = gb[:, :, 0]
     grad_w = own + lax.ppermute(other, "c", SWAP).astype(jnp.float32)

time: 280 us -> 279 us (level)
    pallas_call x1, Pallas kernels: 23.6 us -> 13.8 us  [encode_call(): pl.pallas_call(encode_kernel, out_shape=(jax.ShapeDtypeStruct((8, 2 * SPA...]
    pallas_call x1, Pallas kernels: 123 us -> 131 us  [error_call(): pl.pallas_call(error_kernel, out_shape=(jax.ShapeDtypeStruct((ROWS, TOK),...]
where the time goes in v3:
time: 279 us; the launch traced here: 278 us
  Pallas kernels  245 us (88%)
  other arithmetic  11 us (4%)
  starting transfers between devices  10.1 us (4%)
  local copies, waits for them, and re-layouts  6.65 us (2%)
  waiting for transfers between devices  4.92 us (2%)
    pallas_call x1, Pallas kernels, error_call(): pl.pallas_call(error_kernel, out_shape=(jax.ShapeDtypeStruct((ROWS, TOK),...  131 us
    pallas_call x1, Pallas kernels, gather_call(): pl.pallas_call(gather_kernel, out_shape=(jax.ShapeDtypeStruct(PIECES, jnp...  65.3 us
    pallas_call x1, Pallas kernels, grad_call(): pl.pallas_call(grad_kernel, out_shape=(jax.ShapeDtypeStruct((4, SPAN, D),...  34.6 us
    pallas_call x1, Pallas kernels, encode_call(): pl.pallas_call(encode_kernel, out_shape=(jax.ShapeDtypeStruct((8, 2 * SPA...  13.8 us
    ppermute x1, starting transfers between devices, step(): grad_w = own + lax.ppermute(other, 'c', SWAP).astype(jnp.float32)  8.5 us
    add x1, other arithmetic, step(): grad_w = own + lax.ppermute(other, 'c', SWAP).astype(jnp.float32)  7.35 us
  transfers between devices with their start and end apart: 4, of which 1 were waited for; matrix products, arithmetic and copies ran while one was open for 3% of the time, Pallas kernels for 23%

profile of v3, /device:TPU:1, one launch (start us, length us, event | category | flops | bytes accessed | tf_op | source)
XLA Modules:
  0.0 278.3 jit_solution(8216978558246095778)
XLA Ops:
  0.6 0.0 copy-start
  0.6 1.5 collective-permute-start
  2.1 0.1 collective-permute-start.1
  2.2 0.0 copy-done
  2.2 0.1 reshape.92
  2.3 0.8 dynamic_slice.7
  3.1 0.6 pad.4.codes
  3.7 1.9 fusion.1
  5.6 65.3 %gather.1 = (bf16[2,4,4,2,448,256]{5,4,3,2,1,0:T(8,128)(2,1)}, s32[2,4,8,128]{3,2,1,0:T(8,128)}, bf16[8,3584,128]{2,1,0:T(8,128)(2,1)}) custom-call(bf16[448,256]{1,0:T(8,128)(2,1)} %get-tuple-element.26.own, s32[8,128]{1,0:T(8,128)} %pad.4.codes, bf16[4,128,3584]{2,1,0:T(8,128)(2,1)} %bitcast.20), custom_call_target="tpu_custom_call" | custom-call | bytes 150000000 | tf_op jit(solution)/shard_map/gather/pallas_call | solution.py:384
  70.9 0.8 slice_reduce_fusion.2
  71.6 0.1 broadcast_in_dim_reshape_squeeze.4
  71.7 0.1 fusion.8
  71.8 0.2 fusion.3
  72.0 0.2 fusion.6
  72.2 0.7 copy.28.named
  72.9 0.7 copy.30.sel
  73.6 0.0 collective-permute-done.1
  73.6 0.7 maximum_convert_fusion
  74.3 1.0 copy.29.bias
  75.3 0.0 collective-permute-done.theirs
  75.3 13.8 %encode.1 = (bf16[8,256,256]{2,1,0:T(8,128)(2,1)}, bf16[8,256,256]{2,1,0:T(8,128)(2,1)}) custom-call(s32[8,2]{1,0:T(8,128)} %copy.30.sel, s32[8,4]{1,0:T(8,128)} %copy.28.named, bf16[8,3584,256]{2,1,0:T(8,128)(2,1)} %bitcast.17, bf16[4,128,3584]{2,1,0:T(8,128)(2,1)} %bitcast.21, bf16[4,128,3584]{2,1,0:T(8,128)(2,1)} %collective-permute-done.theirs, ...), custom_call_target="tpu_custom_call" | custom-call | tf_op jit(solution)/shard_map/encode/pallas_call | solution.py:454
  89.1 131.2 %error.1 = (bf16[448,256]{1,0:T(8,128)(2,1)}, bf16[2,4,4,2,448,256]{5,4,3,2,1,0:T(8,128)(2,1)}) custom-call(s32[8,2]{1,0:T(8,128)} %copy.30.sel, bf16[8,3584,128]{2,1,0:T(8,128)(2,1)} %get-tuple-element.14.wt_hbm, bf16[8,256,256]{2,1,0:T(8,128)(2,1)} %get-tuple-element.16.lat, f32[448,256]{1,0:T(8,128)} %get-tuple-element.25.base), custom_call_target="tpu_custom_call" | custom-call | tf_op jit(solution)/shard_map/error/pallas_call | solution.py:418
  220.3 34.6 %grad.1 = (f32[4,128,3584]{2,1,0:T(8,128)}, bf16[4,128,3584]{2,1,0:T(8,128)(2,1)}, f32[8,128,128]{2,1,0:T(8,128)}) custom-call(s32[8,2]{1,0:T(8,128)} %copy.30.sel, bf16[8,3584,256]{2,1,0:T(8,128)(2,1)} %bitcast.23, bf16[8,3584,256]{2,1,0:T(8,128)(2,1)} %bitcast.18, bf16[8,256,256]{2,1,0:T(8,128)(2,1)} %get-tuple-element.16.lat, ...), custom_call_target="tpu_custom_call" | custom-call | tf_op jit(solution)/shard_map/grad/pallas_call | solution.py:502
  254.9 8.5 %collective-permute-start.2 = (bf16[4,128,3584]{2,1,0:T(8,128)(2,1)}, bf16[4,128,3584]{2,1,0:T(8,128)(2,1)S(1)}, u32[]{:S(2)}, u32[]{:S(2)}) collective-permute-start(bf16[4,128,3584]{2,1,0:T(8,128)(2,1)} %get-tuple-element.21), channel_id=1, source_target_pairs={{0,1},{1,0},{2,3},{3,2},{4,5},{5,4},{6,7},{7,6},{8,9},{9,8},{10,11... | collective-permute-start | bytes 11010056 | tf_op jit(solution)/shard_map/ppermute | solution.py:547
  263.4 1.2 slice_reduce_fusion
  264.7 0.1 collective-permute-start.3
  264.8 4.9 %collective-permute-done.3 = f32[4,128]{1,0:T(4,128)S(1)} collective-permute-done((f32[4,128]{1,0:T(4,128)S(1)}, f32[4,128]{1,0:T(4,128)S(1)}, u32[]{:S(2)}, u32[]{:S(2)}) %collective-permute-start.3) | collective-permute-done | bytes 2080 | tf_op jit(solution)/shard_map/ppermute | solution.py:548
  269.7 0.6 add_bitcast_fusion
  270.3 0.0 collective-permute-done.2
  270.3 0.0 copy-start.1
  270.3 0.0 copy-start.2
  270.3 7.3 %convert_add_fusion = f32[4,128,3584]{2,1,0:T(8,128)} fusion(f32[4,128,3584]{2,1,0:T(8,128)} %get-tuple-element.20, bf16[4,128,3584]{2,1,0:T(8,128)(2,1)S(1)} %collective-permute-done.2), kind=kLoop, calls=%fused_computation | loop fusion | flops 3670016 | bytes 18350080 | tf_op jit(solution)/shard_map/add | solution.py:547
  277.6 0.0 copy-done.2
  277.6 0.7 copy.34
  278.3 0.0 copy-done.1
  (4 shorter events, 0.0 us)
Async XLA Ops:
  0.6 1.6 copy-start
  0.6 74.6 %collective-permute-start = (bf16[4,128,3584]{2,1,0:T(8,128)(2,1)}, bf16[4,128,3584]{2,1,0:T(8,128)(2,1)}, u32[]{:S(2)}, u32[]{:S(2)}) collective-permute-start(bf16[4,128,3584]{2,1,0:T(8,128)(2,1)} %bitcast.19), channel_id=1, source_target_pairs={{0,1},{1,0},{2,3},{3,2},{4,5},{5,4},{6,7},{7,6},{8,9},{9,8},{10,11... | collective-permute-start | bytes 11010056 | tf_op jit(solution)/shard_map/ppermute | solution.py:528
  2.1 71.5 %collective-permute-start.1 = (bf16[512]{0:T(512)(128)(2,1)}, bf16[512]{0:T(512)(128)(2,1)S(1)}, u32[]{:S(2)}, u32[]{:S(2)}) collective-permute-start(bf16[512]{0:T(512)(128)(2,1)} %param.7), channel_id=1, source_target_pairs={{0,1},{1,0},{2,3},{3,2},{4,5},{5,4},{6,7},{7,6},{8,9},{9,8},{10,11... | collective-permute-start | bytes 3080 | tf_op jit(solution)/shard_map/ppermute | solution.py:529
  254.9 15.3 %collective-permute-start.2 = (bf16[4,128,3584]{2,1,0:T(8,128)(2,1)}, bf16[4,128,3584]{2,1,0:T(8,128)(2,1)S(1)}, u32[]{:S(2)}, u32[]{:S(2)}) collective-permute-start(bf16[4,128,3584]{2,1,0:T(8,128)(2,1)} %get-tuple-element.21), channel_id=1, source_target_pairs={{0,1},{1,0},{2,3},{3,2},{4,5},{5,4},{6,7},{7,6},{8,9},{9,8},{10,11... | collective-permute-start | bytes 11010056 | tf_op jit(solution)/shard_map/ppermute | solution.py:547
  264.7 5.0 %collective-permute-start.3 = (f32[4,128]{1,0:T(4,128)S(1)}, f32[4,128]{1,0:T(4,128)S(1)}, u32[]{:S(2)}, u32[]{:S(2)}) collective-permute-start(f32[4,128]{1,0:T(4,128)S(1)} %get-tuple-element.23), channel_id=1, source_target_pairs={{0,1},{1,0},{2,3},{3,2},{4,5},{5,4},{6,7},{7,6},{8,9},{9,8},{10,11... | collective-permute-start | bytes 6152 | tf_op jit(solution)/shard_map/ppermute | solution.py:548
  270.3 8.0 %copy-start.1 = (s32[2,8,16]{2,1,0:T(8,128)S(1)}, s32[2,8,16]{2,1,0:T(8,128)}, u32[]{:S(2)}) copy-start(s32[2,8,16]{2,1,0:T(8,128)} %param.9) | copy-start | bytes 3076
  270.3 7.4 %copy-start.2 = (bf16[448,256]{1,0:T(8,128)(2,1)S(1)}, bf16[448,256]{1,0:T(8,128)(2,1)}, u32[]{:S(2)}) copy-start(bf16[448,256]{1,0:T(8,128)(2,1)} %get-tuple-element.17) | copy-start | bytes 688132

commit v4 on v3

--- a/solution.py
+++ b/solution.py
@@ -208,19 +208,21 @@
 
 
 def fill(k, at, sel, wt, lat, parts):
-    dims = [d for d in ("z", "y", "x") if at[d] is None]
     lo, n = C0[k], CN[k]
 
-    def one(index):
-        where = {**at, **dict(zip(dims, index, strict=True))}
-        zl, zh = lax.rem(where["z"], 2), where["z"] // 2
-        g = zl * 4 + where["y"]
-        rows = pl.ds(pl.multiple_of((where["x"] * 2 + zh) * ROWS + lo, 16), n)
-        w = jnp.concatenate([wt[sel[g, 0], rows, :], wt[4 + sel[g, 1], rows, :]], axis=1)
-        part = jnp.dot(w, lat[g], preferred_element_type=jnp.float32)
-        parts[zl, where["y"], where["x"], zh, pl.ds(lo, n), :] = part.astype(jnp.bfloat16)
-
-    each((4,) * len(dims), one)
+    def group(index):
+        index = list(index)
+        zl = index.pop(0) if at["z"] is None else lax.rem(at["z"], 2)
+        y = index.pop(0) if at["y"] is None else at["y"]
+        g = zl * 4 + y
+        for zh in (0, 1) if at["z"] is None else (at["z"] // 2,):
+            for x in range(4) if at["x"] is None else (at["x"],):
+                rows = pl.ds(pl.multiple_of((x * 2 + zh) * ROWS + lo, 16), n)
+                w = jnp.concatenate([wt[sel[g, 0], rows, :], wt[4 + sel[g, 1], rows, :]], axis=1)
+                part = jnp.dot(w, lat[g], preferred_element_type=jnp.float32)
+                parts[zl, y, x, zh, pl.ds(lo, n), :] = part.astype(jnp.bfloat16)
+
+    each((2,) * (at["z"] is None) + (4,) * (at["y"] is None), group)
 
 
 def reduce_error(me, make, parts, base, err, slots, send, recv):
@@ -273,9 +275,6 @@
                 c.start()
             first[k] += copies
             started += first[k]
-        if q == 0:
-            for k in range(3):
-                make(k, {d: (None if d in ORDER[k][:2] else me[d]) for d in me})
         second = []
         for k in range(3):
             dim, rest = ORDER[k][2 - q], ORDER[k][: 2 - q]
@@ -298,6 +297,8 @@
                 copies.append(c)
             second.append(copies)
             started += copies
+        for k in range(3) if q == 0 else ():
+            make(k, {d: (None if d in ORDER[k][:2] else me[d]) for d in me})
         for k in range(3):
             dim, rest = ORDER[k][2 - q], ORDER[k][: 2 - q]
             n, h = CN[k], CH[k]
@@ -332,9 +333,18 @@
 ANY = pl.BlockSpec(memory_space=pl.ANY)
 
 
-def turn(mine, wt, held_w, turned, sems, send, recv):
+def turn(mine, bias, theirs, biases, wt, held_w, turned, sems, send, recv):
+    def give(i, src, dst):
+        c = pltpu.make_async_remote_copy(
+            src_ref=src, dst_ref=dst, send_sem=send.at[i], recv_sem=recv.at[i],
+            device_id={"c": 1 - lax.axis_index("c")}, device_id_type=pl.DeviceIdType.MESH)
+        c.start()
+        return c
+
     load = pltpu.make_async_copy(mine, held_w, sems.at[0])
     load.start()
+    given = [give(0, mine, theirs), give(1, bias, biases.at[1])]
+    biases[0] = bias[...]
     yield
     yield
     yield
@@ -349,14 +359,12 @@
     lax.fori_loop(0, 4 * (D // SPAN), block, 0)
     yield
     keep = pltpu.make_async_copy(turned, wt.at[pl.ds(0, 4)], sems.at[1])
-    give = pltpu.make_async_remote_copy(
-        src_ref=turned, dst_ref=wt.at[pl.ds(4, 4)], send_sem=send, recv_sem=recv,
-        device_id={"c": 1 - lax.axis_index("c")}, device_id_type=pl.DeviceIdType.MESH)
     keep.start()
-    give.start()
+    given.append(give(2, turned, wt.at[pl.ds(4, 4)]))
     yield
     keep.wait()
-    give.wait()
+    for c in given:
+        c.wait()
 
 
 def both(*steps):
@@ -367,10 +375,10 @@
         yield
 
 
-def gather_kernel(own, codes, mine, out, all_codes, wt, local, send, recv, csend, crecv, held_w, turned, sems, wsend, wrecv):
+def gather_kernel(own, codes, bias, mine, out, all_codes, biases, theirs, wt, local, send, recv, csend, crecv, held_w, turned, sems, wsend, wrecv):
     me = coords()
     barrier(me, True)
-    steps = both(gather_codes(me, codes, all_codes, csend, crecv), turn(mine, wt, held_w, turned, sems, wsend, wrecv))
+    steps = both(gather_codes(me, codes, all_codes, csend, crecv), turn(mine, bias, theirs, biases, wt, held_w, turned, sems, wsend, wrecv))
     gather(me, own, out, local, send, recv, steps)
     for _ in steps:
         pass
@@ -380,22 +388,24 @@
 COPIES = 28
 
 
-def gather_call(x, codes, mine):
+def gather_call(x, codes, bias, mine):
     return pl.pallas_call(
         gather_kernel,
         out_shape=(
             jax.ShapeDtypeStruct(PIECES, jnp.bfloat16),
             jax.ShapeDtypeStruct((2, 4, 8, 128), jnp.int32),
+            jax.ShapeDtypeStruct((2, 8, SPAN), jnp.float32),
+            jax.ShapeDtypeStruct((4, SPAN, D), jnp.bfloat16),
             jax.ShapeDtypeStruct((8, D, SPAN), jnp.bfloat16),
         ),
-        in_specs=[VMEM, VMEM, ANY], out_specs=(ANY, VMEM, ANY),
+        in_specs=[VMEM, VMEM, VMEM, ANY], out_specs=(ANY, VMEM, VMEM, ANY, ANY),
         scratch_shapes=[
             DMA, DMA((3, COPIES)), DMA((3, COPIES)), DMA((4,)), DMA((4,)),
-            pltpu.VMEM((4, SPAN, D), jnp.bfloat16), pltpu.VMEM((4, D, SPAN), jnp.bfloat16), DMA((2,)), DMA, DMA,
+            pltpu.VMEM((4, SPAN, D), jnp.bfloat16), pltpu.VMEM((4, D, SPAN), jnp.bfloat16), DMA((2,)), DMA((3,)), DMA((3,)),
         ],
         compiler_params=params(0), name="gather",
         cost_estimate=pl.CostEstimate(flops=0, bytes_accessed=150_000_000, transcendentals=0),
-    )(x, codes, mine)
+    )(x, codes, bias, mine)
 
 
 def error_kernel(sel, wt_hbm, lat, base, err, out, local, send, recv, rsend, rrecv, wt, wt_sem, parts, *slots):
@@ -430,27 +440,31 @@
 CHUNK = 896
 
 
-def pick(sel, g, mine, theirs, ws):
-    ws[:SPAN, :] = mine[sel[g, 0]]
-    ws[SPAN:, :] = theirs[sel[g, 1]]
-
-
-def encode_kernel(sel, named, cen, mine, theirs, bias, lat, mask, ws):
+def pick(mine, theirs, ws):
+    ws[:SPAN, :] = mine[0]
+    ws[SPAN:, :] = theirs[0]
+
+
+def encode_kernel(table, cen, mine, theirs, bias, lat, mask, ws):
     g = pl.program_id(0)
-    pick(sel, g, mine, theirs, ws)
+    pick(mine, theirs, ws)
     pre = jnp.dot(ws[...], cen[0], preferred_element_type=jnp.float32)
     lane = lax.broadcasted_iota(jnp.int32, (SPAN, TOK), 1)
     for hh in range(2):
         rows = slice(hh * SPAN, (hh + 1) * SPAN)
-        p = pre[rows] + bias[hh * 4 + sel[g, hh]]
-        on = jnp.where(lane < SPAN, named[g, hh], named[g, 2 + hh])
+        chosen = lax.broadcasted_iota(jnp.int32, (8, TOK), 0) == table[g, hh]
+        p = pre[rows] + lax.dot_general(
+            bias[hh].astype(jnp.bfloat16), jnp.where(chosen, 1.0, 0.0).astype(jnp.bfloat16),
+            (((0,), (0,)), ((), ())), preferred_element_type=jnp.float32)
+        on = jnp.where(lane < SPAN, table[g, 2 + hh], table[g, 4 + hh])
         keep = (on > 0) & (p > 0)
         lat[0, rows] = jnp.where(keep, p, 0.0).astype(jnp.bfloat16)
         mask[0, rows] = jnp.where(keep, 1.0, 0.0).astype(jnp.bfloat16)
 
 
-def encode_call(sel, named, cen, mine, theirs, bias):
+def encode_call(table, cen, mine, theirs, bias):
     per = lambda *shape: pl.BlockSpec((1, *shape), lambda g, *_: (g, 0, 0))
+    block = lambda hh: pl.BlockSpec((1, SPAN, D), lambda g, t: (t[g, hh], 0, 0))
     return pl.pallas_call(
         encode_kernel,
         out_shape=(
@@ -458,13 +472,13 @@
             jax.ShapeDtypeStruct((8, 2 * SPAN, TOK), jnp.bfloat16),
         ),
         grid_spec=pltpu.PrefetchScalarGridSpec(
-            num_scalar_prefetch=2, grid=(8,),
-            in_specs=[per(D, TOK), VMEM, VMEM, VMEM],
+            num_scalar_prefetch=1, grid=(8,),
+            in_specs=[per(D, TOK), block(0), block(1), VMEM],
             out_specs=(per(2 * SPAN, TOK), per(2 * SPAN, TOK)),
             scratch_shapes=[pltpu.VMEM((2 * SPAN, D), jnp.bfloat16)],
         ),
         compiler_params=params(), name="encode",
-    )(sel, named, cen, mine, theirs, bias)
+    )(table, cen, mine, theirs, bias)
 
 
 def grad_kernel(sel, err, cen, lat, mask, mine, theirs, own, other, gb, ws, acc):
@@ -476,13 +490,14 @@
         acc[...] = jnp.zeros_like(acc)
         gb[...] = jnp.zeros_like(gb)
 
-    pick(sel, g, mine, theirs, ws)
+    pick(mine, theirs, ws)
     back = jnp.dot(ws[...], err[0], preferred_element_type=jnp.float32)
     slope = jnp.where(mask[0] > 0, back, 0.0).astype(jnp.bfloat16)
-    ones = jnp.ones((TOK, SPAN), jnp.bfloat16)
-    sums = jnp.dot(slope, ones, preferred_element_type=jnp.float32).astype(jnp.bfloat16).astype(jnp.float32)
+    sums = lax.dot_general(jnp.ones((8, TOK), jnp.bfloat16), slope, (((1,), (1,)), ((), ())), preferred_element_type=jnp.float32)
+    sums = sums.astype(jnp.bfloat16).astype(jnp.float32)
+    row = lax.broadcasted_iota(jnp.int32, (8, SPAN), 0)
     for hh in range(2):
-        gb[hh * 4 + sel[g, hh]] += sums[hh * SPAN : (hh + 1) * SPAN]
+        gb[hh] += jnp.where(row == sel[g, hh], sums[:, hh * SPAN : (hh + 1) * SPAN], 0.0)
     for i in range(0, D, CHUNK):
         nt = (((1,), (1,)), ((), ()))
         t = lax.dot_general(lat[0], err[0, i : i + CHUNK], nt, preferred_element_type=jnp.float32)
@@ -499,16 +514,17 @@
 
 def grad_call(sel, err, cen, lat, mask, mine, theirs):
     per = lambda *shape: pl.BlockSpec((1, *shape), lambda g, *_: (g, 0, 0))
+    block = lambda hh: pl.BlockSpec((1, SPAN, D), lambda g, t: (t[g, hh], 0, 0))
     return pl.pallas_call(
         grad_kernel,
         out_shape=(
             jax.ShapeDtypeStruct((4, SPAN, D), jnp.float32),
             jax.ShapeDtypeStruct((4, SPAN, D), jnp.bfloat16),
-            jax.ShapeDtypeStruct((8, SPAN, SPAN), jnp.float32),
+            jax.ShapeDtypeStruct((2, 8, SPAN), jnp.float32),
         ),
         grid_spec=pltpu.PrefetchScalarGridSpec(
             num_scalar_prefetch=1, grid=(8,),
-            in_specs=[per(D, TOK), per(D, TOK), per(2 * SPAN, TOK), per(2 * SPAN, TOK), VMEM, VMEM],
+            in_specs=[per(D, TOK), per(D, TOK), per(2 * SPAN, TOK), per(2 * SPAN, TOK), block(0), block(1)],
             out_specs=(VMEM, VMEM, VMEM),
             scratch_shapes=[pltpu.VMEM((2 * SPAN, D), jnp.bfloat16), pltpu.VMEM((4, SPAN, D), jnp.float32)],
         ),
@@ -525,27 +541,24 @@
     c = lax.axis_index("c")
     chip = lax.axis_index("zl") * 4 + lax.axis_index("y")
     mine = dictionary.reshape(4, SPAN, D)
-    theirs = lax.ppermute(mine, "c", SWAP)
-    bias_theirs = lax.ppermute(enc_bias, "c", SWAP)
     codes = lax.dynamic_index_in_dim(block_codes, d, axis=1, keepdims=False)
     codes = jnp.pad(codes.reshape(1, 32), ((0, 7), (0, 96)), constant_values=-1)
     act_t = activations.T.astype(jnp.float32)
     dec = lax.dynamic_slice_in_dim(dec_bias, d * ROWS, ROWS)[:, None]
-    cen, codes, wt = gather_call((act_t - dec).astype(jnp.bfloat16), codes, mine)
+    bias = jnp.pad(enc_bias.astype(jnp.float32).reshape(4, SPAN), ((0, 4), (0, 0)))
+    cen, codes, biases, theirs, wt = gather_call((act_t - dec).astype(jnp.bfloat16), codes, bias, mine)
     cen = cen.reshape(8, D, TOK)
     codes = codes.reshape(8, 8, 128)[:, 0, :32].reshape(8, 2, 16)
     first = d * 64 + (chip * 2 + jnp.stack([c, 1 - c])) * 4
     local = codes[:, :, None, :] - first[:, None]
     hit = (codes[:, :, None, :] >= 0) & (local >= 0) & (local < 4)
-    named = jnp.any(hit, axis=3).astype(jnp.int32).reshape(8, 4)
-    sel = jnp.max(jnp.where(hit, local, 0), axis=(1, 3)).astype(jnp.int32)
-    bias = jnp.concatenate([enc_bias, bias_theirs]).astype(jnp.float32).reshape(8, SPAN, 1)
-    lat, mask = encode_call(sel, named, cen, mine, theirs, bias)
-    err_own, err = error_call(sel, wt, lat, dec - act_t)
-    own, other, gb = grad_call(sel, err.reshape(8, D, TOK), cen, lat, mask, mine, theirs)
-    gb = gb[:, :, 0]
+    local = jnp.max(jnp.where(hit, local, -1), axis=3)
+    table = jnp.concatenate([jnp.maximum(jnp.max(local, axis=1), 0), (local >= 0).astype(jnp.int32).reshape(8, 4)], axis=1)
+    lat, mask = encode_call(table, cen, mine, theirs, biases)
+    err_own, err = error_call(table, wt, lat, dec - act_t)
+    own, other, gb = grad_call(table, err.reshape(8, D, TOK), cen, lat, mask, mine, theirs)
     grad_w = own + lax.ppermute(other, "c", SWAP).astype(jnp.float32)
-    grad_b = gb[:4] + lax.ppermute(gb[4:], "c", SWAP)
+    grad_b = (gb[0] + lax.ppermute(gb[1], "c", SWAP))[:4]
     return err_own.T, grad_w.reshape(4 * SPAN, D), grad_b.reshape(4 * SPAN)
 
 

time: 279 us -> 267 us (0.957)
  Pallas kernels: 245 us -> 234 us
    pallas_call x1, Pallas kernels: 131 us -> 122 us  [error_call(): pl.pallas_call(error_kernel, out_shape=(jax.ShapeDtypeStruct((ROWS, TOK),...]
  transfers between devices with their start and end apart: 4 -> 2, of which waited for: 1 -> 1; matrix products, arithmetic and copies ran while one was open for 3% -> 1% of each run, Pallas kernels for 23% -> 0%
where the time goes in v4:
time: 267 us
  Pallas kernels  234 us (88%)
  other arithmetic  12.2 us (5%)
  starting transfers between devices  8.85 us (3%)
  waiting for transfers between devices  5.55 us (2%)
  local copies, waits for them, and re-layouts  5.14 us (2%)
    pallas_call x1, Pallas kernels, error_call(): pl.pallas_call(error_kernel, out_shape=(jax.ShapeDtypeStruct((ROWS, TOK),...  122 us
    pallas_call x1, Pallas kernels, gather_call(): pl.pallas_call(gather_kernel, out_shape=(jax.ShapeDtypeStruct(PIECES, jnp...  65.8 us
    pallas_call x1, Pallas kernels, grad_call(): pl.pallas_call(grad_kernel, out_shape=(jax.ShapeDtypeStruct((4, SPAN, D),...  32 us
    pallas_call x1, Pallas kernels, encode_call(): pl.pallas_call(encode_kernel, out_shape=(jax.ShapeDtypeStruct((8, 2 * SPA...  14 us
    ppermute x1, starting transfers between devices, step(): grad_w = own + lax.ppermute(other, 'c', SWAP).astype(jnp.float32)  8.84 us
    add x1, other arithmetic, step(): grad_w = own + lax.ppermute(other, 'c', SWAP).astype(jnp.float32)  7.35 us
    ppermute x1, waiting for transfers between devices, step(): grad_b = (gb[0] + lax.ppermute(gb[1], 'c', SWAP))[:4]  5.55 us
  transfers between devices with their start and end apart: 2, of which 1 were waited for; matrix products, arithmetic and copies ran while one was open for 1% of the time, Pallas kernels for 0%

profile of v4, /device:TPU:1, one launch (start us, length us, event | category | flops | bytes accessed | tf_op | source)
XLA Modules:
  0.0 266.7 jit_solution(13516682861837501291)
XLA Ops:
  0.6 0.0 copy-start
  0.7 0.7 copy-done
  1.4 0.1 reshape.66
  1.4 1.3 pad_convert_fusion.bias
  2.7 0.8 dynamic_slice.7
  3.5 0.6 pad.10.codes
  4.1 1.9 fusion.1
  6.0 65.8 %gather.1 = (bf16[2,4,4,2,448,256]{5,4,3,2,1,0:T(8,128)(2,1)}, s32[2,4,8,128]{3,2,1,0:T(8,128)}, f32[2,8,128]{2,1,0:T(8,128)}, bf16[4,128,3584]{2,1,0:T(8,128)(2,1)}, bf16[8,3584,128]{2,1,0:T(8,128)(2,1)}) custom-call(bf16[448,256]{1,0:T(8,128)(2,1)} %get-tuple-element.30.own, s32[8,128]{1,0:T(8,128)} %pad.10.codes, f32[8,128]{1,0:T(8,128)} %pad_convert_fusion.bias, ...), custom_call_target="tpu_custom_call" | custom-call | bytes 150000000 | tf_op jit(solution)/shard_map/gather/pallas_call | solution.py:392
  71.8 0.8 slice_reduce_fusion
  72.6 0.1 broadcast_in_dim_reshape_squeeze.4
  72.7 0.1 fusion.8
  72.8 0.3 fusion.4
  73.1 0.1 copy.13
  73.2 0.1 copy.12
  73.2 0.7 pad_add_fusion.table.sel
  73.9 14.0 %encode.1 = (bf16[8,256,256]{2,1,0:T(8,128)(2,1)}, bf16[8,256,256]{2,1,0:T(8,128)(2,1)}) custom-call(s32[8,6]{1,0:T(8,128)} %pad_add_fusion.table.sel, bf16[8,3584,256]{2,1,0:T(8,128)(2,1)} %bitcast.20, bf16[4,128,3584]{2,1,0:T(8,128)(2,1)} %bitcast.23, bf16[4,128,3584]{2,1,0:T(8,128)(2,1)} %get-tuple-element.18.theirs, f32[2,8,128]{2,1,0:T(8,128)} %get-tuple-element.19.bias), custom_call_target="tpu_custom_call" | custom-call | tf_op jit(solution)/shard_map/encode/pallas_call | solution.py:468
  87.9 122.3 %error.1 = (bf16[448,256]{1,0:T(8,128)(2,1)}, bf16[2,4,4,2,448,256]{5,4,3,2,1,0:T(8,128)(2,1)}) custom-call(s32[8,6]{1,0:T(8,128)} %pad_add_fusion.table.sel, bf16[8,3584,128]{2,1,0:T(8,128)(2,1)} %get-tuple-element.16.wt_hbm, bf16[8,256,256]{2,1,0:T(8,128)(2,1)} %get-tuple-element.20.lat, f32[448,256]{1,0:T(8,128)} %get-tuple-element.29.base), custom_call_target="tpu_custom_call" | custom-call | tf_op jit(solution)/shard_map/error/pallas_call | solution.py:428
  210.3 32.0 %grad.1 = (f32[4,128,3584]{2,1,0:T(8,128)}, bf16[4,128,3584]{2,1,0:T(8,128)(2,1)}, f32[2,8,128]{2,1,0:T(8,128)}) custom-call(s32[8,6]{1,0:T(8,128)} %pad_add_fusion.table.sel, bf16[8,3584,256]{2,1,0:T(8,128)(2,1)} %bitcast.25, bf16[8,3584,256]{2,1,0:T(8,128)(2,1)} %bitcast.21, bf16[8,256,256]{2,1,0:T(8,128)(2,1)} %get-tuple-element.20.lat, ...), custom_call_target="tpu_custom_call" | custom-call | tf_op jit(solution)/shard_map/grad/pallas_call | solution.py:518
  242.3 8.8 %collective-permute-start = (bf16[4,128,3584]{2,1,0:T(8,128)(2,1)}, bf16[4,128,3584]{2,1,0:T(8,128)(2,1)S(1)}, u32[]{:S(2)}, u32[]{:S(2)}) collective-permute-start(bf16[4,128,3584]{2,1,0:T(8,128)(2,1)} %get-tuple-element.25), channel_id=1, source_target_pairs={{0,1},{1,0},{2,3},{3,2},{4,5},{5,4},{6,7},{7,6},{8,9},{9,8},{10,11... | collective-permute-start | bytes 11010056 | tf_op jit(solution)/shard_map/ppermute | solution.py:560
  251.1 0.7 slice_bitcast_fusion
  251.8 0.0 collective-permute-start.1
  251.8 5.6 %collective-permute-done.1 = f32[8,128]{1,0:T(8,128)S(1)} collective-permute-done((f32[8,128]{1,0:T(8,128)S(1)}, f32[8,128]{1,0:T(8,128)S(1)}, u32[]{:S(2)}, u32[]{:S(2)}) %collective-permute-start.1) | collective-permute-done | bytes 4128 | tf_op jit(solution)/shard_map/ppermute | solution.py:561
  257.4 0.7 bitcast_add_fusion
  258.1 0.6 slice_bitcast_fusion.1
  258.7 0.0 collective-permute-done
  258.7 0.0 copy-start.1
  258.7 0.0 copy-start.2
  258.7 7.3 %convert_add_fusion = f32[4,128,3584]{2,1,0:T(8,128)} fusion(f32[4,128,3584]{2,1,0:T(8,128)} %get-tuple-element.24, bf16[4,128,3584]{2,1,0:T(8,128)(2,1)S(1)} %collective-permute-done), kind=kLoop, calls=%fused_computation | loop fusion | flops 3670016 | bytes 18350080 | tf_op jit(solution)/shard_map/add | solution.py:560
  266.0 0.0 copy-done.2
  266.0 0.7 copy.16
  266.7 0.0 copy-done.1
  (5 shorter events, 0.0 us)
Async XLA Ops:
  0.6 0.7 copy-start
  242.3 16.4 %collective-permute-start = (bf16[4,128,3584]{2,1,0:T(8,128)(2,1)}, bf16[4,128,3584]{2,1,0:T(8,128)(2,1)S(1)}, u32[]{:S(2)}, u32[]{:S(2)}) collective-permute-start(bf16[4,128,3584]{2,1,0:T(8,128)(2,1)} %get-tuple-element.25), channel_id=1, source_target_pairs={{0,1},{1,0},{2,3},{3,2},{4,5},{5,4},{6,7},{7,6},{8,9},{9,8},{10,11... | collective-permute-start | bytes 11010056 | tf_op jit(solution)/shard_map/ppermute | solution.py:560
  251.8 5.6 %collective-permute-start.1 = (f32[8,128]{1,0:T(8,128)S(1)}, f32[8,128]{1,0:T(8,128)S(1)}, u32[]{:S(2)}, u32[]{:S(2)}) collective-permute-start(f32[8,128]{1,0:T(8,128)S(1)} %slice_bitcast_fusion), channel_id=1, source_target_pairs={{0,1},{1,0},{2,3},{3,2},{4,5},{5,4},{6,7},{7,6},{8,9},{9,8},{10,11... | collective-permute-start | bytes 12296 | tf_op jit(solution)/shard_map/ppermute | solution.py:561
  258.7 8.0 %copy-start.1 = (s32[2,8,16]{2,1,0:T(8,128)S(1)}, s32[2,8,16]{2,1,0:T(8,128)}, u32[]{:S(2)}) copy-start(s32[2,8,16]{2,1,0:T(8,128)} %param.9) | copy-start | bytes 3076
  258.7 7.4 %copy-start.2 = (bf16[448,256]{1,0:T(8,128)(2,1)S(1)}, bf16[448,256]{1,0:T(8,128)(2,1)}, u32[]{:S(2)}) copy-start(bf16[448,256]{1,0:T(8,128)(2,1)} %get-tuple-element.21) | copy-start | bytes 688132

commit v5 on v4

--- a/solution.py
+++ b/solution.py
@@ -58,9 +58,8 @@
 NEAR = ((0, 1), (1, -1))
 
 
-def gather(me, own, out, local, send, recv, beside=iter(())):
+def gather(me, own, out, local, send, recv, beside=iter(()), ready=lambda k: None):
     mine = pltpu.make_async_copy(own, region(out, me, 0, ROWS), local)
-    mine.start()
     copies = [{} for _ in range(3)]
 
     def go(k, phase, name, at, by, lo=0, n=None, src=None):
@@ -77,11 +76,13 @@
         copies[k][name].wait_recv()
 
     for k in range(3):
+        ready(k)
         src = own.at[pl.ds(C0[k], CN[k]), :]
         for s, by in NEAR:
             go(k, 0, ("near", s), {}, by, src=src)
         for s, by in NEAR:
             go(k, 1, ("near", 0, s), {}, by, src=src)
+    mine.start()
     next(beside, None)
     for k in range(3):
         for s, by in NEAR:
@@ -153,24 +154,6 @@
         c.wait_send()
 
 
-def held(ref, dims, at, lo, n):
-    index = []
-    for name in ("zl", "y", "x", "zh"):
-        dim = name[0]
-        if dim not in dims:
-            continue
-        value = at[dim]
-        if value is None:
-            index.append(slice(None))
-        elif name == "zl":
-            index.append(lax.rem(value, 2))
-        elif name == "zh":
-            index.append(value // 2)
-        else:
-            index.append(value)
-    return ref.at[(*index, pl.ds(lo, n), slice(None))]
-
-
 def lead(dims):
     return tuple(s for name, s in (("zl", 2), ("y", 4), ("x", 4), ("zh", 2)) if name[0] in dims)
 
@@ -194,17 +177,76 @@
     lax.fori_loop(0, total, step, 0)
 
 
+SUBS = (2, -1, 1, 0)
+
+
 def reduce_scratch():
     shapes = []
     for k in range(3):
         n, h = CN[k], CH[k]
-        for q in range(3):
-            dims = lead(ORDER[k][: 2 - q])
+        for q in (0, 0, 0, 0, 1, 2):
+            dims = lead(ORDER[k][:1] if q < 2 else ())
             for rows in (h, n - h, h, n - h, h, n - h):
                 shapes.append(pltpu.VMEM((*dims, rows, TOK), jnp.bfloat16))
-            if q < 2:
-                shapes.append(pltpu.VMEM((*dims, n, TOK), jnp.bfloat16))
     return shapes
+
+
+class Reduction:
+    def __init__(self, me, k, dim, at, parts, slots, send, recv, base):
+        self.me, self.k, self.dim, self.at, self.parts, self.slots = me, k, dim, at, parts, slots
+        self.send, self.recv, self.base = send, recv, base
+        self.copies = {}
+        self.lead = lead(tuple(d for d in at if d != dim and at[d] is None))
+        self.halves = ((0, CH[k]), (CH[k], CN[k] - CH[k]))
+
+    def source(self, by, half):
+        lo, n = self.halves[half]
+        return region(self.parts, {**self.at, self.dim: shift(self.me, self.dim, by)}, C0[self.k] + lo, n)
+
+    def go(self, i, src, by):
+        c = remote(src, self.slots[i], self.send.at[self.k, self.base + i], self.recv.at[self.k, self.base + i],
+                   self.dim, shift(self.me, self.dim, by))
+        c.start()
+        self.copies[i] = c
+
+    def far(self):
+        self.go(0, self.source(2, 0), 1)
+        self.go(1, self.source(2, 1), -1)
+
+    def near(self):
+        self.go(3, self.source(1, 1), 1)
+        self.go(4, self.source(-1, 0), -1)
+
+    def forward(self):
+        for i, by in ((0, 1), (1, -1)):
+            self.copies[i].wait_recv()
+            slot, own = self.slots[i], self.source(by, i)
+
+            def add(index, slot=slot, own=own):
+                a = slot[index].astype(jnp.float32) + own[index].astype(jnp.float32)
+                slot[index] = a.astype(jnp.bfloat16)
+
+            each(self.lead, add)
+            self.go(2 if i == 0 else 5, slot, by)
+
+    def finish(self, store=None):
+        for i in (3, 4, 2, 5):
+            self.copies[i].wait_recv()
+        for half, (i, j) in enumerate(((2, 4), (3, 5))):
+            a, b, own = self.slots[i], self.slots[j], self.source(0, half)
+
+            def add(index, a=a, b=b, own=own, half=half):
+                total = own[index].astype(jnp.float32) + a[index].astype(jnp.float32) + b[index].astype(jnp.float32)
+                if store is None:
+                    own[index] = total.astype(jnp.bfloat16)
+                else:
+                    store(self.halves[half], total)
+
+            each(self.lead, add)
+
+    def drain(self):
+        for c in self.copies.values():
+            c.wait_send()
 
 
 def fill(k, at, sel, wt, lat, parts):
@@ -226,101 +268,61 @@
 
 
 def reduce_error(me, make, parts, base, err, slots, send, recv):
-    slots = list(slots)
-    table = []
-    for k in range(3):
-        row = []
-        for q in range(3):
-            row.append([slots.pop(0) for _ in range(7 if q < 2 else 6)])
-        table.append(row)
-    started = []
-
-    def source(k, q, at, lo, n):
-        if q == 0:
-            return region(parts, at, C0[k] + lo, n)
-        return held(table[k][q - 1][6], ORDER[k][: 3 - q], at, lo, n)
-
-    for q in range(3):
-        first = []
+    first, second, third = [], [], []
+    for k in range(3):
+        a, b, c = ORDER[k]
+        mine = slots[36 * k : 36 * (k + 1)]
+        at = {a: None, b: me[b], c: me[c]}
+
+        def new(dim, at, i, k=k, mine=mine):
+            return Reduction(me, k, dim, at, parts, mine[6 * i : 6 * i + 6], send, recv, 6 * i)
+
+        first.append({m: new(c, {**at, b: shift(me, b, m)}, i) for i, m in enumerate(SUBS)})
+        second.append(new(b, at, 4))
+        third.append(new(a, {**at, a: me[a]}, 5))
+
+    def whole(k, by):
+        a, b, c = ORDER[k]
+        make(k, {a: None, b: None, c: shift(me, c, by)})
+
+    for k in range(3):
+        whole(k, 2)
+        for m in SUBS:
+            first[k][m].far()
+    for k in range(3):
+        whole(k, 1)
+        whole(k, -1)
+        for m in SUBS:
+            first[k][m].near()
+    for m in SUBS:
         for k in range(3):
-            dim, rest = ORDER[k][2 - q], ORDER[k][: 2 - q]
-            n, h = CN[k], CH[k]
-            at = {d: (None if d in rest else me[d]) for d in me}
-            far = {**at, dim: shift(me, dim, 2)}
-            up, down = shift(me, dim, 1), shift(me, dim, -1)
-            opp_p, opp_m, sum_p, raw_p, raw_m, sum_m = table[k][q][:6]
-            if q == 0:
-                make(k, far)
-            copies = [
-                remote(source(k, q, far, 0, h), opp_p, send.at[k, q, 0], recv.at[k, q, 0], dim, up),
-                remote(source(k, q, far, h, n - h), opp_m, send.at[k, q, 1], recv.at[k, q, 1], dim, down),
-            ]
-            for c in copies:
-                c.start()
-            first.append(copies)
+            first[k][m].forward()
+    for k in range(3):
+        whole(k, 0)
+    for m in SUBS:
         for k in range(3):
-            dim, rest = ORDER[k][2 - q], ORDER[k][: 2 - q]
-            n, h = CN[k], CH[k]
-            at = {d: (None if d in rest else me[d]) for d in me}
-            up, down = shift(me, dim, 1), shift(me, dim, -1)
-            opp_p, opp_m, sum_p, raw_p, raw_m, sum_m = table[k][q][:6]
-            if q == 0:
-                make(k, {**at, dim: up})
-                make(k, {**at, dim: down})
-            copies = [
-                remote(source(k, q, {**at, dim: up}, h, n - h), raw_p, send.at[k, q, 2], recv.at[k, q, 2], dim, up),
-                remote(source(k, q, {**at, dim: down}, 0, h), raw_m, send.at[k, q, 3], recv.at[k, q, 3], dim, down),
-            ]
-            for c in copies:
-                c.start()
-            first[k] += copies
-            started += first[k]
-        second = []
-        for k in range(3):
-            dim, rest = ORDER[k][2 - q], ORDER[k][: 2 - q]
-            n, h = CN[k], CH[k]
-            at = {d: (None if d in rest else me[d]) for d in me}
-            up, down = shift(me, dim, 1), shift(me, dim, -1)
-            opp_p, opp_m, sum_p, raw_p, raw_m, sum_m = table[k][q][:6]
-            copies = []
-            for s, (slot, to, lo, rows, into) in enumerate(((opp_p, up, 0, h, sum_p), (opp_m, down, h, n - h, sum_m))):
-                first[k][s].wait_recv()
-                own = source(k, q, {**at, dim: to}, lo, rows)
-
-                def add(index, slot=slot, own=own):
-                    a = slot[index].astype(jnp.float32) + own[index].astype(jnp.float32)
-                    slot[index] = a.astype(jnp.bfloat16)
-
-                each(lead(rest), add)
-                c = remote(slot, into, send.at[k, q, 4 + s], recv.at[k, q, 4 + s], dim, to)
-                c.start()
-                copies.append(c)
-            second.append(copies)
-            started += copies
-        for k in range(3) if q == 0 else ():
-            make(k, {d: (None if d in ORDER[k][:2] else me[d]) for d in me})
-        for k in range(3):
-            dim, rest = ORDER[k][2 - q], ORDER[k][: 2 - q]
-            n, h = CN[k], CH[k]
-            at = {d: (None if d in rest else me[d]) for d in me}
-            opp_p, opp_m, sum_p, raw_p, raw_m, sum_m = table[k][q][:6]
-            first[k][2].wait_recv()
-            first[k][3].wait_recv()
-            second[k][0].wait_recv()
-            second[k][1].wait_recv()
-            for lo, rows, a, b in ((0, h, sum_p, raw_m), (h, n - h, raw_p, sum_m)):
-                own = source(k, q, at, lo, rows)
-
-                def add(index, own=own, a=a, b=b, lo=lo, rows=rows):
-                    total = own[index].astype(jnp.float32) + a[index].astype(jnp.float32) + b[index].astype(jnp.float32)
-                    if q < 2:
-                        table[k][q][6][(*index, pl.ds(lo, rows), slice(None))] = total.astype(jnp.bfloat16)
-                    else:
-                        at_rows = pl.ds(C0[k] + lo, rows)
-                        err[at_rows, :] = (total + base[at_rows, :]).astype(jnp.bfloat16)
-
-                each(lead(rest), add)
-    return started
+            first[k][m].finish()
+            if m == 2:
+                second[k].far()
+            elif m == 1:
+                second[k].near()
+    for k in range(3):
+        second[k].forward()
+    for k in range(3):
+        second[k].finish()
+        third[k].far()
+        third[k].near()
+    for k in range(3):
+        third[k].forward()
+
+    def last(k):
+        def store(half, total):
+            rows = pl.ds(C0[k] + half[0], half[1])
+            err[rows, :] = (total + base[rows, :]).astype(jnp.bfloat16)
+
+        third[k].finish(store)
+
+    return last, [r for k in range(3) for r in (*first[k].values(), second[k], third[k])]
 
 
 def params(collective=None):
@@ -418,10 +420,10 @@
     def make(k, at):
         fill(k, at, sel, wt, lat, parts)
 
-    started = reduce_error(me, make, parts, base, err, slots, rsend, rrecv)
-    gather(me, err, out, local, send, recv)
-    for c in started:
-        c.wait_send()
+    last, reductions = reduce_error(me, make, parts, base, err, slots, rsend, rrecv)
+    gather(me, err, out, local, send, recv, ready=last)
+    for r in reductions:
+        r.drain()
 
 
 def error_call(sel, wt, lat, base):
@@ -430,7 +432,7 @@
         out_shape=(jax.ShapeDtypeStruct((ROWS, TOK), jnp.bfloat16), jax.ShapeDtypeStruct(PIECES, jnp.bfloat16)),
         in_specs=[pl.BlockSpec(memory_space=pltpu.SMEM), ANY, VMEM, VMEM], out_specs=(VMEM, ANY),
         scratch_shapes=[
-            DMA, DMA((3, COPIES)), DMA((3, COPIES)), DMA((3, 3, 6)), DMA((3, 3, 6)),
+            DMA, DMA((3, COPIES)), DMA((3, COPIES)), DMA((3, 36)), DMA((3, 36)),
             pltpu.VMEM((8, D, SPAN), jnp.bfloat16), DMA, pltpu.VMEM(PIECES, jnp.bfloat16), *reduce_scratch(),
         ],
         compiler_params=params(1), name="error",
@@ -481,12 +483,12 @@
     )(table, cen, mine, theirs, bias)
 
 
-def grad_kernel(sel, err, cen, lat, mask, mine, theirs, own, other, gb, ws, acc):
+def grad_kernel(sel, err, cen, lat, mask, mine, theirs, own, other, gb, ws, mine_acc, acc):
     g = pl.program_id(0)
 
     @pl.when(g == 0)
     def _():
-        own[...] = jnp.zeros_like(own)
+        mine_acc[...] = jnp.zeros_like(mine_acc)
         acc[...] = jnp.zeros_like(acc)
         gb[...] = jnp.zeros_like(gb)
 
@@ -503,12 +505,13 @@
         t = lax.dot_general(lat[0], err[0, i : i + CHUNK], nt, preferred_element_type=jnp.float32)
         t = t + lax.dot_general(slope, cen[0, i : i + CHUNK], nt, preferred_element_type=jnp.float32)
         t = t.astype(jnp.bfloat16).astype(jnp.float32)
-        own[sel[g, 0], :, i : i + CHUNK] += t[:SPAN]
+        mine_acc[sel[g, 0], :, i : i + CHUNK] += t[:SPAN]
         acc[sel[g, 1], :, i : i + CHUNK] += t[SPAN:]
 
     @pl.when(g == 7)
     def _():
         for b in range(4):
+            own[b] = mine_acc[b].astype(jnp.bfloat16)
             other[b] = acc[b].astype(jnp.bfloat16)
 
 
@@ -518,7 +521,7 @@
     return pl.pallas_call(
         grad_kernel,
         out_shape=(
-            jax.ShapeDtypeStruct((4, SPAN, D), jnp.float32),
+            jax.ShapeDtypeStruct((4, SPAN, D), jnp.bfloat16),
             jax.ShapeDtypeStruct((4, SPAN, D), jnp.bfloat16),
             jax.ShapeDtypeStruct((2, 8, SPAN), jnp.float32),
         ),
@@ -526,7 +529,7 @@
             num_scalar_prefetch=1, grid=(8,),
             in_specs=[per(D, TOK), per(D, TOK), per(2 * SPAN, TOK), per(2 * SPAN, TOK), block(0), block(1)],
             out_specs=(VMEM, VMEM, VMEM),
-            scratch_shapes=[pltpu.VMEM((2 * SPAN, D), jnp.bfloat16), pltpu.VMEM((4, SPAN, D), jnp.float32)],
+            scratch_shapes=[pltpu.VMEM((2 * SPAN, D), jnp.bfloat16)] + [pltpu.VMEM((4, SPAN, D), jnp.float32)] * 2,
         ),
         compiler_params=params(), name="grad",
     )(sel, err, cen, lat, mask, mine, theirs)
@@ -557,7 +560,7 @@
     lat, mask = encode_call(table, cen, mine, theirs, biases)
     err_own, err = error_call(table, wt, lat, dec - act_t)
     own, other, gb = grad_call(table, err.reshape(8, D, TOK), cen, lat, mask, mine, theirs)
-    grad_w = own + lax.ppermute(other, "c", SWAP).astype(jnp.float32)
+    grad_w = own.astype(jnp.float32) + lax.ppermute(other, "c", SWAP).astype(jnp.float32)
     grad_b = (gb[0] + lax.ppermute(gb[1], "c", SWAP))[:4]
     return err_own.T, grad_w.reshape(4 * SPAN, D), grad_b.reshape(4 * SPAN)
 

time: 267 us -> 265 us (level)
  no operation moved by 1% of the time
where the time goes in v5:
time: 265 us; the launch traced here: 264 us
  Pallas kernels  234 us (88%)
  other arithmetic  11.1 us (4%)
  starting transfers between devices  7.88 us (3%)
  waiting for transfers between devices  5.55 us (2%)
  local copies, waits for them, and re-layouts  5.13 us (2%)
    pallas_call x1, Pallas kernels, error_call(): pl.pallas_call(error_kernel, out_shape=(jax.ShapeDtypeStruct((ROWS, TOK),...  123 us
    pallas_call x1, Pallas kernels, gather_call(): pl.pallas_call(gather_kernel, out_shape=(jax.ShapeDtypeStruct(PIECES, jnp...  65.8 us
    pallas_call x1, Pallas kernels, grad_call(): pl.pallas_call(grad_kernel, out_shape=(jax.ShapeDtypeStruct((4, SPAN, D),...  31.1 us
    pallas_call x1, Pallas kernels, encode_call(): pl.pallas_call(encode_kernel, out_shape=(jax.ShapeDtypeStruct((8, 2 * SPA...  14.1 us
    ppermute x1, starting transfers between devices, step(): lax.ppermute(other, 'c', SWAP).astype(jnp.float32)  7.87 us
    add x1, other arithmetic, step(): own.astype(jnp.float32) + lax.ppermute(other, 'c', SWAP).astype(jnp.float32)  6.22 us
    ppermute x1, waiting for transfers between devices, step(): grad_b = (gb[0] + lax.ppermute(gb[1], 'c', SWAP))[:4]  5.55 us
  transfers between devices with their start and end apart: 2, of which 1 were waited for; matrix products, arithmetic and copies ran while one was open for 1% of the time, Pallas kernels for 0%

profile of v5, /device:TPU:1, one launch (start us, length us, event | category | flops | bytes accessed | tf_op | source)
XLA Modules:
  0.0 264.3 jit_solution(12520091333535521211)
XLA Ops:
  0.6 0.0 copy-start
  0.7 0.7 copy-done
  1.4 0.1 reshape.66
  1.4 1.3 pad_convert_fusion.bias
  2.7 0.8 dynamic_slice.7
  3.5 0.6 pad.10.codes
  4.1 1.9 fusion.1
  6.0 65.8 %gather.1 = (bf16[2,4,4,2,448,256]{5,4,3,2,1,0:T(8,128)(2,1)}, s32[2,4,8,128]{3,2,1,0:T(8,128)}, f32[2,8,128]{2,1,0:T(8,128)}, bf16[4,128,3584]{2,1,0:T(8,128)(2,1)}, bf16[8,3584,128]{2,1,0:T(8,128)(2,1)}) custom-call(bf16[448,256]{1,0:T(8,128)(2,1)} %get-tuple-element.30.own, s32[8,128]{1,0:T(8,128)} %pad.10.codes, f32[8,128]{1,0:T(8,128)} %pad_convert_fusion.bias, ...), custom_call_target="tpu_custom_call" | custom-call | bytes 150000000 | tf_op jit(solution)/shard_map/gather/pallas_call | solution.py:394
  71.8 0.8 slice_reduce_fusion
  72.6 0.1 broadcast_in_dim_reshape_squeeze.4
  72.7 0.1 fusion.8
  72.8 0.3 fusion.4
  73.1 0.1 copy.13
  73.2 0.1 copy.12
  73.2 0.7 pad_add_fusion.table.sel
  73.9 14.1 %encode.1 = (bf16[8,256,256]{2,1,0:T(8,128)(2,1)}, bf16[8,256,256]{2,1,0:T(8,128)(2,1)}) custom-call(s32[8,6]{1,0:T(8,128)} %pad_add_fusion.table.sel, bf16[8,3584,256]{2,1,0:T(8,128)(2,1)} %bitcast.20, bf16[4,128,3584]{2,1,0:T(8,128)(2,1)} %bitcast.23, bf16[4,128,3584]{2,1,0:T(8,128)(2,1)} %get-tuple-element.18.theirs, f32[2,8,128]{2,1,0:T(8,128)} %get-tuple-element.19.bias), custom_call_target="tpu_custom_call" | custom-call | tf_op jit(solution)/shard_map/encode/pallas_call | solution.py:470
  88.0 122.8 %error.1 = (bf16[448,256]{1,0:T(8,128)(2,1)}, bf16[2,4,4,2,448,256]{5,4,3,2,1,0:T(8,128)(2,1)}) custom-call(s32[8,6]{1,0:T(8,128)} %pad_add_fusion.table.sel, bf16[8,3584,128]{2,1,0:T(8,128)(2,1)} %get-tuple-element.16.wt_hbm, bf16[8,256,256]{2,1,0:T(8,128)(2,1)} %get-tuple-element.20.lat, f32[448,256]{1,0:T(8,128)} %get-tuple-element.29.base), custom_call_target="tpu_custom_call" | custom-call | tf_op jit(solution)/shard_map/error/pallas_call | solution.py:430
  210.8 31.1 %grad.1 = (bf16[4,128,3584]{2,1,0:T(8,128)(2,1)}, bf16[4,128,3584]{2,1,0:T(8,128)(2,1)}, f32[2,8,128]{2,1,0:T(8,128)}) custom-call(s32[8,6]{1,0:T(8,128)} %pad_add_fusion.table.sel, bf16[8,3584,256]{2,1,0:T(8,128)(2,1)} %bitcast.25, bf16[8,3584,256]{2,1,0:T(8,128)(2,1)} %bitcast.21, bf16[8,256,256]{2,1,0:T(8,128)(2,1)} %get-tuple-element.20.lat, ...), custom_call_target="tpu_custom_call" | custom-call | tf_op jit(solution)/shard_map/grad/pallas_call | solution.py:521
  242.0 7.9 %collective-permute-start = (bf16[4,128,3584]{2,1,0:T(8,128)(2,1)}, bf16[4,128,3584]{2,1,0:T(8,128)(2,1)S(1)}, u32[]{:S(2)}, u32[]{:S(2)}) collective-permute-start(bf16[4,128,3584]{2,1,0:T(8,128)(2,1)} %get-tuple-element.25), channel_id=1, source_target_pairs={{0,1},{1,0},{2,3},{3,2},{4,5},{5,4},{6,7},{7,6},{8,9},{9,8},{10,11... | collective-permute-start | bytes 11010056 | tf_op jit(solution)/shard_map/ppermute | solution.py:563
  249.8 0.7 slice_bitcast_fusion
  250.5 0.0 collective-permute-start.1
  250.5 5.6 %collective-permute-done.1 = f32[8,128]{1,0:T(8,128)S(1)} collective-permute-done((f32[8,128]{1,0:T(8,128)S(1)}, f32[8,128]{1,0:T(8,128)S(1)}, u32[]{:S(2)}, u32[]{:S(2)}) %collective-permute-start.1) | collective-permute-done | bytes 4128 | tf_op jit(solution)/shard_map/ppermute | solution.py:564
  256.1 0.7 bitcast_add_fusion
  256.8 0.6 slice_bitcast_fusion.1
  257.4 0.0 collective-permute-done
  257.4 0.0 copy-start.1
  257.4 6.2 %convert_add_fusion = f32[4,128,3584]{2,1,0:T(8,128)} fusion(bf16[4,128,3584]{2,1,0:T(8,128)(2,1)S(1)} %collective-permute-done, bf16[4,128,3584]{2,1,0:T(8,128)(2,1)} %get-tuple-element.24), kind=kLoop, calls=%fused_computation | loop fusion | flops 5505024 | bytes 14680064 | tf_op jit(solution)/shard_map/add | solution.py:563
  263.6 0.0 copy-done.1
  263.6 0.7 copy.16
  (5 shorter events, 0.0 us)
Async XLA Ops:
  0.6 0.7 copy-start
  242.0 15.4 %collective-permute-start = (bf16[4,128,3584]{2,1,0:T(8,128)(2,1)}, bf16[4,128,3584]{2,1,0:T(8,128)(2,1)S(1)}, u32[]{:S(2)}, u32[]{:S(2)}) collective-permute-start(bf16[4,128,3584]{2,1,0:T(8,128)(2,1)} %get-tuple-element.25), channel_id=1, source_target_pairs={{0,1},{1,0},{2,3},{3,2},{4,5},{5,4},{6,7},{7,6},{8,9},{9,8},{10,11... | collective-permute-start | bytes 11010056 | tf_op jit(solution)/shard_map/ppermute | solution.py:563
  250.5 5.6 %collective-permute-start.1 = (f32[8,128]{1,0:T(8,128)S(1)}, f32[8,128]{1,0:T(8,128)S(1)}, u32[]{:S(2)}, u32[]{:S(2)}) collective-permute-start(f32[8,128]{1,0:T(8,128)S(1)} %slice_bitcast_fusion), channel_id=1, source_target_pairs={{0,1},{1,0},{2,3},{3,2},{4,5},{5,4},{6,7},{7,6},{8,9},{9,8},{10,11... | collective-permute-start | bytes 12296 | tf_op jit(solution)/shard_map/ppermute | solution.py:564
  257.4 6.2 %copy-start.1 = (bf16[448,256]{1,0:T(8,128)(2,1)S(1)}, bf16[448,256]{1,0:T(8,128)(2,1)}, u32[]{:S(2)}) copy-start(bf16[448,256]{1,0:T(8,128)(2,1)} %get-tuple-element.21) | copy-start | bytes 688132

commit v6 on v5

--- a/solution.py
+++ b/solution.py
@@ -285,29 +285,37 @@
         a, b, c = ORDER[k]
         make(k, {a: None, b: None, c: shift(me, c, by)})
 
-    for k in range(3):
-        whole(k, 2)
-        for m in SUBS:
+    def push(m):
+        for k in range(3):
+            first[k][m].near()
+            first[k][m].forward()
+
+    for m in SUBS:
+        for k in range(3):
+            a, b, c = ORDER[k]
+            make(k, {a: None, b: shift(me, b, m), c: shift(me, c, 2)})
             first[k][m].far()
     for k in range(3):
         whole(k, 1)
         whole(k, -1)
-        for m in SUBS:
-            first[k][m].near()
-    for m in SUBS:
-        for k in range(3):
-            first[k][m].forward()
+    push(2)
+    push(-1)
     for k in range(3):
         whole(k, 0)
-    for m in SUBS:
-        for k in range(3):
-            first[k][m].finish()
-            if m == 2:
-                second[k].far()
-            elif m == 1:
-                second[k].near()
+    for k in range(3):
+        first[k][2].finish()
+        second[k].far()
+    push(1)
+    for k in range(3):
+        first[k][-1].finish()
+    push(0)
+    for k in range(3):
+        first[k][1].finish()
+        second[k].near()
     for k in range(3):
         second[k].forward()
+    for k in range(3):
+        first[k][0].finish()
     for k in range(3):
         second[k].finish()
         third[k].far()
@@ -395,7 +403,7 @@
         gather_kernel,
         out_shape=(
             jax.ShapeDtypeStruct(PIECES, jnp.bfloat16),
-            jax.ShapeDtypeStruct((2, 4, 8, 128), jnp.int32),
+            jax.ShapeDtypeStruct((2, 4, 2, 8, 16), jnp.int32),
             jax.ShapeDtypeStruct((2, 8, SPAN), jnp.float32),
             jax.ShapeDtypeStruct((4, SPAN, D), jnp.bfloat16),
             jax.ShapeDtypeStruct((8, D, SPAN), jnp.bfloat16),
@@ -412,10 +420,12 @@
 
 def error_kernel(sel, wt_hbm, lat, base, err, out, local, send, recv, rsend, rrecv, wt, wt_sem, parts, *slots):
     me = coords()
-    load = pltpu.make_async_copy(wt_hbm, wt, wt_sem)
-    load.start()
+    loads = [pltpu.make_async_copy(wt_hbm.at[i], wt.at[i], wt_sem.at[i]) for i in range(8)]
+    for c in loads:
+        c.start()
     barrier(me)
-    load.wait()
+    for c in loads:
+        c.wait()
 
     def make(k, at):
         fill(k, at, sel, wt, lat, parts)
@@ -433,7 +443,7 @@
         in_specs=[pl.BlockSpec(memory_space=pltpu.SMEM), ANY, VMEM, VMEM], out_specs=(VMEM, ANY),
         scratch_shapes=[
             DMA, DMA((3, COPIES)), DMA((3, COPIES)), DMA((3, 36)), DMA((3, 36)),
-            pltpu.VMEM((8, D, SPAN), jnp.bfloat16), DMA, pltpu.VMEM(PIECES, jnp.bfloat16), *reduce_scratch(),
+            pltpu.VMEM((8, D, SPAN), jnp.bfloat16), DMA((8,)), pltpu.VMEM(PIECES, jnp.bfloat16), *reduce_scratch(),
         ],
         compiler_params=params(1), name="error",
     )(sel, wt, lat, base)
@@ -483,14 +493,15 @@
     )(table, cen, mine, theirs, bias)
 
 
-def grad_kernel(sel, err, cen, lat, mask, mine, theirs, own, other, gb, ws, mine_acc, acc):
+def grad_kernel(sel, err, cen, lat, mask, mine, theirs, own, other, own_b, other_b, ws, mine_acc, acc):
     g = pl.program_id(0)
 
     @pl.when(g == 0)
     def _():
         mine_acc[...] = jnp.zeros_like(mine_acc)
         acc[...] = jnp.zeros_like(acc)
-        gb[...] = jnp.zeros_like(gb)
+        own_b[...] = jnp.zeros_like(own_b)
+        other_b[...] = jnp.zeros_like(other_b)
 
     pick(mine, theirs, ws)
     back = jnp.dot(ws[...], err[0], preferred_element_type=jnp.float32)
@@ -498,8 +509,8 @@
     sums = lax.dot_general(jnp.ones((8, TOK), jnp.bfloat16), slope, (((1,), (1,)), ((), ())), preferred_element_type=jnp.float32)
     sums = sums.astype(jnp.bfloat16).astype(jnp.float32)
     row = lax.broadcasted_iota(jnp.int32, (8, SPAN), 0)
-    for hh in range(2):
-        gb[hh] += jnp.where(row == sel[g, hh], sums[:, hh * SPAN : (hh + 1) * SPAN], 0.0)
+    for hh, into in enumerate((own_b, other_b)):
+        into[...] += jnp.where(row == sel[g, hh], sums[:, hh * SPAN : (hh + 1) * SPAN], 0.0)
     for i in range(0, D, CHUNK):
         nt = (((1,), (1,)), ((), ()))
         t = lax.dot_general(lat[0], err[0, i : i + CHUNK], nt, preferred_element_type=jnp.float32)
@@ -523,12 +534,13 @@
         out_shape=(
             jax.ShapeDtypeStruct((4, SPAN, D), jnp.bfloat16),
             jax.ShapeDtypeStruct((4, SPAN, D), jnp.bfloat16),
-            jax.ShapeDtypeStruct((2, 8, SPAN), jnp.float32),
+            jax.ShapeDtypeStruct((8, SPAN), jnp.float32),
+            jax.ShapeDtypeStruct((8, SPAN), jnp.float32),
         ),
         grid_spec=pltpu.PrefetchScalarGridSpec(
             num_scalar_prefetch=1, grid=(8,),
             in_specs=[per(D, TOK), per(D, TOK), per(2 * SPAN, TOK), per(2 * SPAN, TOK), block(0), block(1)],
-            out_specs=(VMEM, VMEM, VMEM),
+            out_specs=(VMEM, VMEM, VMEM, VMEM),
             scratch_shapes=[pltpu.VMEM((2 * SPAN, D), jnp.bfloat16)] + [pltpu.VMEM((4, SPAN, D), jnp.float32)] * 2,
         ),
         compiler_params=params(), name="grad",
@@ -544,14 +556,12 @@
     c = lax.axis_index("c")
     chip = lax.axis_index("zl") * 4 + lax.axis_index("y")
     mine = dictionary.reshape(4, SPAN, D)
-    codes = lax.dynamic_index_in_dim(block_codes, d, axis=1, keepdims=False)
-    codes = jnp.pad(codes.reshape(1, 32), ((0, 7), (0, 96)), constant_values=-1)
     act_t = activations.T.astype(jnp.float32)
     dec = lax.dynamic_slice_in_dim(dec_bias, d * ROWS, ROWS)[:, None]
     bias = jnp.pad(enc_bias.astype(jnp.float32).reshape(4, SPAN), ((0, 4), (0, 0)))
-    cen, codes, biases, theirs, wt = gather_call((act_t - dec).astype(jnp.bfloat16), codes, bias, mine)
+    cen, codes, biases, theirs, wt = gather_call((act_t - dec).astype(jnp.bfloat16), block_codes, bias, mine)
     cen = cen.reshape(8, D, TOK)
-    codes = codes.reshape(8, 8, 128)[:, 0, :32].reshape(8, 2, 16)
+    codes = lax.dynamic_index_in_dim(codes.reshape(8, 2, 8, 16), d, axis=2, keepdims=False)
     first = d * 64 + (chip * 2 + jnp.stack([c, 1 - c])) * 4
     local = codes[:, :, None, :] - first[:, None]
     hit = (codes[:, :, None, :] >= 0) & (local >= 0) & (local < 4)
@@ -559,9 +569,9 @@
     table = jnp.concatenate([jnp.maximum(jnp.max(local, axis=1), 0), (local >= 0).astype(jnp.int32).reshape(8, 4)], axis=1)
     lat, mask = encode_call(table, cen, mine, theirs, biases)
     err_own, err = error_call(table, wt, lat, dec - act_t)
-    own, other, gb = grad_call(table, err.reshape(8, D, TOK), cen, lat, mask, mine, theirs)
+    own, other, own_b, other_b = grad_call(table, err.reshape(8, D, TOK), cen, lat, mask, mine, theirs)
     grad_w = own.astype(jnp.float32) + lax.ppermute(other, "c", SWAP).astype(jnp.float32)
-    grad_b = (gb[0] + lax.ppermute(gb[1], "c", SWAP))[:4]
+    grad_b = (own_b + lax.ppermute(other_b, "c", SWAP))[:4]
     return err_own.T, grad_w.reshape(4 * SPAN, D), grad_b.reshape(4 * SPAN)
 
 

time: 265 us -> 261 us (0.985)
  transfers between devices with their start and end apart: 2 -> 2, of which waited for: 1 -> 1; matrix products, arithmetic and copies ran while one was open for 1% -> 0% of each run, Pallas kernels for 0% -> 0%
where the time goes in v6:
time: 261 us; the launch traced here: 260 us
  Pallas kernels  233 us (89%)
  other arithmetic  11.1 us (4%)
  starting transfers between devices  6.17 us (2%)
  waiting for transfers between devices  6.16 us (2%)
  local copies, waits for them, and re-layouts  3.06 us (1%)
    pallas_call x1, Pallas kernels, error_call(): pl.pallas_call(error_kernel, out_shape=(jax.ShapeDtypeStruct((ROWS, TOK),...  123 us
    pallas_call x1, Pallas kernels, gather_call(): pl.pallas_call(gather_kernel, out_shape=(jax.ShapeDtypeStruct(PIECES, jnp...  65.8 us
    pallas_call x1, Pallas kernels, grad_call(): pl.pallas_call(grad_kernel, out_shape=(jax.ShapeDtypeStruct((4, SPAN, D),...  30.5 us
    pallas_call x1, Pallas kernels, encode_call(): pl.pallas_call(encode_kernel, out_shape=(jax.ShapeDtypeStruct((8, 2 * SPA...  14.1 us
    add x1, other arithmetic, step(): own.astype(jnp.float32) + lax.ppermute(other, 'c', SWAP).astype(jnp.float32)  6.22 us
    ppermute x1, waiting for transfers between devices, step(): grad_b = (own_b + lax.ppermute(other_b, 'c', SWAP))[:4]  6.16 us
    ppermute x1, starting transfers between devices, step(): lax.ppermute(other, 'c', SWAP).astype(jnp.float32)  6.08 us
  transfers between devices with their start and end apart: 2, of which 1 were waited for; matrix products, arithmetic and copies ran while one was open for 0% of the time, Pallas kernels for 0%

profile of v6, /device:TPU:1, one launch (start us, length us, event | category | flops | bytes accessed | tf_op | source)
XLA Modules:
  0.0 260.0 jit_solution(2668781559851605084)
XLA Ops:
  0.6 1.3 pad_convert_fusion.bias
  1.9 0.8 dynamic_slice.7
  2.7 1.9 fusion.1
  4.6 65.8 %gather.1 = (bf16[2,4,4,2,448,256]{5,4,3,2,1,0:T(8,128)(2,1)}, s32[2,4,2,8,16]{4,3,2,1,0:T(8,128)}, f32[2,8,128]{2,1,0:T(8,128)}, bf16[4,128,3584]{2,1,0:T(8,128)(2,1)}, bf16[8,3584,128]{2,1,0:T(8,128)(2,1)}) custom-call(bf16[448,256]{1,0:T(8,128)(2,1)} %get-tuple-element.32.own, s32[2,8,16]{2,1,0:T(8,128)} %codes.1, f32[8,128]{1,0:T(8,128)} %pad_convert_fusion.bias, ...), custom_call_target="tpu_custom_call" | custom-call | bytes 150000000 | tf_op jit(solution)/shard_map/gather/pallas_call | solution.py:402
  70.4 0.9 constant_dynamic-slice_fusion
  71.3 0.1 fusion.8
  71.4 0.3 fusion.4
  71.6 0.1 copy.18
  71.7 0.1 copy.17
  71.8 0.7 pad_add_fusion.table.sel
  72.5 14.1 %encode.1 = (bf16[8,256,256]{2,1,0:T(8,128)(2,1)}, bf16[8,256,256]{2,1,0:T(8,128)(2,1)}) custom-call(s32[8,6]{1,0:T(8,128)} %pad_add_fusion.table.sel, bf16[8,3584,256]{2,1,0:T(8,128)(2,1)} %bitcast.21, bf16[4,128,3584]{2,1,0:T(8,128)(2,1)} %bitcast.24, bf16[4,128,3584]{2,1,0:T(8,128)(2,1)} %get-tuple-element.19.theirs, f32[2,8,128]{2,1,0:T(8,128)} %get-tuple-element.20.bias), custom_call_target="tpu_custom_call" | custom-call | tf_op jit(solution)/shard_map/encode/pallas_call | solution.py:480
  86.6 122.5 %error.1 = (bf16[448,256]{1,0:T(8,128)(2,1)}, bf16[2,4,4,2,448,256]{5,4,3,2,1,0:T(8,128)(2,1)}) custom-call(s32[8,6]{1,0:T(8,128)} %pad_add_fusion.table.sel, bf16[8,3584,128]{2,1,0:T(8,128)(2,1)} %get-tuple-element.17.wt_hbm, bf16[8,256,256]{2,1,0:T(8,128)(2,1)} %get-tuple-element.21.lat, f32[448,256]{1,0:T(8,128)} %get-tuple-element.31.base), custom_call_target="tpu_custom_call" | custom-call | tf_op jit(solution)/shard_map/error/pallas_call | solution.py:440
  209.1 30.5 %grad.1 = (bf16[4,128,3584]{2,1,0:T(8,128)(2,1)}, bf16[4,128,3584]{2,1,0:T(8,128)(2,1)}, f32[8,128]{1,0:T(8,128)}, f32[8,128]{1,0:T(8,128)}) custom-call(s32[8,6]{1,0:T(8,128)} %pad_add_fusion.table.sel, bf16[8,3584,256]{2,1,0:T(8,128)(2,1)} %bitcast.26, bf16[8,3584,256]{2,1,0:T(8,128)(2,1)} %bitcast.22, bf16[8,256,256]{2,1,0:T(8,128)(2,1)} %get-tuple-element.21.lat, ...), custom_call_target="tpu_custom_call" | custom-call | tf_op jit(solution)/shard_map/grad/pallas_call | solution.py:532
  239.5 6.1 %collective-permute-start = (bf16[4,128,3584]{2,1,0:T(8,128)(2,1)}, bf16[4,128,3584]{2,1,0:T(8,128)(2,1)S(1)}, u32[]{:S(2)}, u32[]{:S(2)}) collective-permute-start(bf16[4,128,3584]{2,1,0:T(8,128)(2,1)} %get-tuple-element.26), channel_id=1, source_target_pairs={{0,1},{1,0},{2,3},{3,2},{4,5},{5,4},{6,7},{7,6},{8,9},{9,8},{10,11... | collective-permute-start | bytes 11010056 | tf_op jit(solution)/shard_map/ppermute | solution.py:573
  245.6 0.1 collective-permute-start.1
  245.7 6.2 %collective-permute-done.1 = f32[8,128]{1,0:T(8,128)S(1)} collective-permute-done((f32[8,128]{1,0:T(8,128)}, f32[8,128]{1,0:T(8,128)S(1)}, u32[]{:S(2)}, u32[]{:S(2)}) %collective-permute-start.1) | collective-permute-done | bytes 4128 | tf_op jit(solution)/shard_map/ppermute | solution.py:574
  251.9 0.7 add.50
  252.5 0.6 slice_bitcast_fusion
  253.1 0.0 collective-permute-done
  253.1 0.0 copy-start
  253.1 6.2 %convert_add_fusion = f32[4,128,3584]{2,1,0:T(8,128)} fusion(bf16[4,128,3584]{2,1,0:T(8,128)(2,1)S(1)} %collective-permute-done, bf16[4,128,3584]{2,1,0:T(8,128)(2,1)} %get-tuple-element.25), kind=kLoop, calls=%fused_computation | loop fusion | flops 5505024 | bytes 14680064 | tf_op jit(solution)/shard_map/add | solution.py:573
  259.4 0.0 copy-done
  259.4 0.7 copy.24
  (4 shorter events, 0.0 us)
Async XLA Ops:
  239.5 13.6 %collective-permute-start = (bf16[4,128,3584]{2,1,0:T(8,128)(2,1)}, bf16[4,128,3584]{2,1,0:T(8,128)(2,1)S(1)}, u32[]{:S(2)}, u32[]{:S(2)}) collective-permute-start(bf16[4,128,3584]{2,1,0:T(8,128)(2,1)} %get-tuple-element.26), channel_id=1, source_target_pairs={{0,1},{1,0},{2,3},{3,2},{4,5},{5,4},{6,7},{7,6},{8,9},{9,8},{10,11... | collective-permute-start | bytes 11010056 | tf_op jit(solution)/shard_map/ppermute | solution.py:573
  245.6 6.3 %collective-permute-start.1 = (f32[8,128]{1,0:T(8,128)}, f32[8,128]{1,0:T(8,128)S(1)}, u32[]{:S(2)}, u32[]{:S(2)}) collective-permute-start(f32[8,128]{1,0:T(8,128)} %get-tuple-element.28), channel_id=1, source_target_pairs={{0,1},{1,0},{2,3},{3,2},{4,5},{5,4},{6,7},{7,6},{8,9},{9,8},{10,11... | collective-permute-start | bytes 12296 | tf_op jit(solution)/shard_map/ppermute | solution.py:574
  253.1 6.2 %copy-start = (bf16[448,256]{1,0:T(8,128)(2,1)S(1)}, bf16[448,256]{1,0:T(8,128)(2,1)}, u32[]{:S(2)}) copy-start(bf16[448,256]{1,0:T(8,128)(2,1)} %get-tuple-element.22) | copy-start | bytes 688132

commit v7 on v6

--- a/solution.py
+++ b/solution.py
@@ -58,9 +58,18 @@
 NEAR = ((0, 1), (1, -1))
 
 
-def gather(me, own, out, local, send, recv, beside=iter(()), ready=lambda k: None):
+def gather(me, own, out, local, send, recv, beside=iter(()), ready=lambda k: None, use=None):
     mine = pltpu.make_async_copy(own, region(out, me, 0, ROWS), local)
     copies = [{} for _ in range(3)]
+
+    def arrived(k, by_b, by_c=0):
+        if use is not None:
+            a, b, c = ORDER[k]
+            use.arrived(k, {a: None, b: shift(me, b, by_b), c: shift(me, c, by_c)})
+
+    def work():
+        if use is not None:
+            use.work()
 
     def go(k, phase, name, at, by, lo=0, n=None, src=None):
         order = ORDER[k]
@@ -101,6 +110,7 @@
             go(k, 1, ("near", 2, s), {0: 2}, by)
         for s, by in NEAR:
             go(k, 2, ("near", 0, s), {1: 0}, by)
+        arrived(k, 0)
     for phase in (1, 2):
         next(beside, None)
         for j in (0, -1, 1, 2):
@@ -109,18 +119,32 @@
                     got(k, phase, "near", j, s)
                     if (j in (0, 1)) == (s == 0):
                         go(k, phase, ("far", j), {phase - 1: j, phase: -by}, by)
+                    if phase == 2:
+                        arrived(k, j, -by)
+            if phase == 2:
+                work()
         if phase == 1:
             for k in range(3):
                 for j in (-1, 1):
                     for s, by in NEAR:
                         go(k, 2, ("near", j, s), {1: j}, by)
+                    arrived(k, j)
         next(beside, None)
-        for k in range(3):
-            for j in (0, -1, 1, 2):
+        for j in (0, -1, 1, 2):
+            for k in range(3):
                 got(k, phase, "far", j)
-            if phase == 1:
+                if phase == 2:
+                    arrived(k, j, 2)
+            if phase == 2:
+                work()
+        if phase == 1:
+            for k in range(3):
                 for s, by in NEAR:
                     go(k, 2, ("near", 2, s), {1: 2}, by)
+                arrived(k, 2)
+            work()
+    work()
+    work()
     for k in range(3):
         for c in copies[k].values():
             c.wait_send()
@@ -249,22 +273,60 @@
             c.wait_send()
 
 
-def fill(k, at, sel, wt, lat, parts):
-    lo, n = C0[k], CN[k]
-
+def pieces(at, body):
     def group(index):
         index = list(index)
         zl = index.pop(0) if at["z"] is None else lax.rem(at["z"], 2)
         y = index.pop(0) if at["y"] is None else at["y"]
-        g = zl * 4 + y
-        for zh in (0, 1) if at["z"] is None else (at["z"] // 2,):
-            for x in range(4) if at["x"] is None else (at["x"],):
-                rows = pl.ds(pl.multiple_of((x * 2 + zh) * ROWS + lo, 16), n)
-                w = jnp.concatenate([wt[sel[g, 0], rows, :], wt[4 + sel[g, 1], rows, :]], axis=1)
-                part = jnp.dot(w, lat[g], preferred_element_type=jnp.float32)
-                parts[zl, y, x, zh, pl.ds(lo, n), :] = part.astype(jnp.bfloat16)
+        body(zl * 4 + y, [
+            (zl, y, x, zh)
+            for zh in ((0, 1) if at["z"] is None else (at["z"] // 2,))
+            for x in (range(4) if at["x"] is None else (at["x"],))
+        ])
 
     each((2,) * (at["z"] is None) + (4,) * (at["y"] is None), group)
+
+
+def turned_rows(wt, sel, g, piece, lo, n):
+    rows = pl.ds(pl.multiple_of((piece[2] * 2 + piece[3]) * ROWS + lo, 16), n)
+    return jnp.concatenate([wt[sel[g, 0], rows, :], wt[4 + sel[g, 1], rows, :]], axis=1)
+
+
+class Back:
+    def __init__(self, sel, wt, out, held_e, back, sems):
+        self.sel, self.wt, self.out, self.held, self.back, self.sems = sel, wt, out, held_e, back, sems
+        self.count, self.old, self.new = 0, [], []
+
+    def arrived(self, k, at):
+        src, dst = (region(r, at, C0[k], CN[k]) for r in (self.out, self.held))
+        copy = pltpu.make_async_copy(src, dst, self.sems.at[self.count])
+        self.count += 1
+        copy.start()
+        self.new.append((k, at, copy))
+
+    def work(self):
+        todo, self.old, self.new = self.old, self.new, []
+        for k, at, copy in todo:
+            copy.wait()
+            rows = pl.ds(C0[k], CN[k])
+
+            def add(g, group, k=k, rows=rows):
+                w = jnp.concatenate([turned_rows(self.wt, self.sel, g, piece, C0[k], CN[k]) for piece in group], axis=0)
+                e = jnp.concatenate([self.held[(*piece, rows, slice(None))] for piece in group], axis=0)
+                self.back[g] += lax.dot_general(w, e, (((0,), (0,)), ((), ())), preferred_element_type=jnp.float32)
+
+            pieces(at, add)
+
+
+def fill(k, at, sel, wt, lat, parts):
+    lo, n = C0[k], CN[k]
+
+    def group(g, found):
+        for piece in found:
+            part = jnp.dot(turned_rows(wt, sel, g, piece, lo, n), lat[g], preferred_element_type=jnp.float32)
+            parts[(*piece, pl.ds(lo, n), slice(None))] = part.astype(jnp.bfloat16)
+
+    pieces(at, group)
 
 
 def reduce_error(me, make, parts, base, err, slots, send, recv):
@@ -418,7 +480,7 @@
     )(x, codes, bias, mine)
 
 
-def error_kernel(sel, wt_hbm, lat, base, err, out, local, send, recv, rsend, rrecv, wt, wt_sem, parts, *slots):
+def error_kernel(sel, wt_hbm, lat, mask, base, err, out, slope, local, send, recv, rsend, rrecv, wt, wt_sem, parts, held_e, back, sems, *slots):
     me = coords()
     loads = [pltpu.make_async_copy(wt_hbm.at[i], wt.at[i], wt_sem.at[i]) for i in range(8)]
     for c in loads:
@@ -431,22 +493,34 @@
         fill(k, at, sel, wt, lat, parts)
 
     last, reductions = reduce_error(me, make, parts, base, err, slots, rsend, rrecv)
-    gather(me, err, out, local, send, recv, ready=last)
+    back[...] = jnp.zeros_like(back)
+    gather(me, err, out, local, send, recv, ready=last, use=Back(sel, wt, out, held_e, back, sems))
+
+    def round_off(g, carry):
+        slope[g] = jnp.where(mask[g] > 0, back[g], 0.0).astype(jnp.bfloat16)
+        return carry
+
+    lax.fori_loop(0, 8, round_off, 0)
     for r in reductions:
         r.drain()
 
 
-def error_call(sel, wt, lat, base):
+def error_call(sel, wt, lat, mask, base):
     return pl.pallas_call(
         error_kernel,
-        out_shape=(jax.ShapeDtypeStruct((ROWS, TOK), jnp.bfloat16), jax.ShapeDtypeStruct(PIECES, jnp.bfloat16)),
-        in_specs=[pl.BlockSpec(memory_space=pltpu.SMEM), ANY, VMEM, VMEM], out_specs=(VMEM, ANY),
+        out_shape=(
+            jax.ShapeDtypeStruct((ROWS, TOK), jnp.bfloat16),
+            jax.ShapeDtypeStruct(PIECES, jnp.bfloat16),
+            jax.ShapeDtypeStruct((8, 2 * SPAN, TOK), jnp.bfloat16),
+        ),
+        in_specs=[pl.BlockSpec(memory_space=pltpu.SMEM), ANY, VMEM, VMEM, VMEM], out_specs=(VMEM, ANY, VMEM),
         scratch_shapes=[
             DMA, DMA((3, COPIES)), DMA((3, COPIES)), DMA((3, 36)), DMA((3, 36)),
-            pltpu.VMEM((8, D, SPAN), jnp.bfloat16), DMA((8,)), pltpu.VMEM(PIECES, jnp.bfloat16), *reduce_scratch(),
+            pltpu.VMEM((8, D, SPAN), jnp.bfloat16), DMA((8,)), pltpu.VMEM(PIECES, jnp.bfloat16), pltpu.VMEM(PIECES, jnp.bfloat16),
+            pltpu.VMEM((8, 2 * SPAN, TOK), jnp.float32), DMA((48,)), *reduce_scratch(),
         ],
         compiler_params=params(1), name="error",
-    )(sel, wt, lat, base)
+    )(sel, wt, lat, mask, base)
 
 
 CHUNK = 896
@@ -493,7 +567,7 @@
     )(table, cen, mine, theirs, bias)
 
 
-def grad_kernel(sel, err, cen, lat, mask, mine, theirs, own, other, own_b, other_b, ws, mine_acc, acc):
+def grad_kernel(sel, err, cen, lat, slopes, own, other, own_b, other_b, mine_acc, acc):
     g = pl.program_id(0)
 
     @pl.when(g == 0)
@@ -503,9 +577,7 @@
         own_b[...] = jnp.zeros_like(own_b)
         other_b[...] = jnp.zeros_like(other_b)
 
-    pick(mine, theirs, ws)
-    back = jnp.dot(ws[...], err[0], preferred_element_type=jnp.float32)
-    slope = jnp.where(mask[0] > 0, back, 0.0).astype(jnp.bfloat16)
+    slope = slopes[0]
     sums = lax.dot_general(jnp.ones((8, TOK), jnp.bfloat16), slope, (((1,), (1,)), ((), ())), preferred_element_type=jnp.float32)
     sums = sums.astype(jnp.bfloat16).astype(jnp.float32)
     row = lax.broadcasted_iota(jnp.int32, (8, SPAN), 0)
@@ -526,9 +598,8 @@
             other[b] = acc[b].astype(jnp.bfloat16)
 
 
-def grad_call(sel, err, cen, lat, mask, mine, theirs):
+def grad_call(sel, err, cen, lat, slope):
     per = lambda *shape: pl.BlockSpec((1, *shape), lambda g, *_: (g, 0, 0))
-    block = lambda hh: pl.BlockSpec((1, SPAN, D), lambda g, t: (t[g, hh], 0, 0))
     return pl.pallas_call(
         grad_kernel,
         out_shape=(
@@ -539,12 +610,12 @@
         ),
         grid_spec=pltpu.PrefetchScalarGridSpec(
             num_scalar_prefetch=1, grid=(8,),
-            in_specs=[per(D, TOK), per(D, TOK), per(2 * SPAN, TOK), per(2 * SPAN, TOK), block(0), block(1)],
+            in_specs=[per(D, TOK), per(D, TOK), per(2 * SPAN, TOK), per(2 * SPAN, TOK)],
             out_specs=(VMEM, VMEM, VMEM, VMEM),
-            scratch_shapes=[pltpu.VMEM((2 * SPAN, D), jnp.bfloat16)] + [pltpu.VMEM((4, SPAN, D), jnp.float32)] * 2,
+            scratch_shapes=[pltpu.VMEM((4, SPAN, D), jnp.float32)] * 2,
         ),
         compiler_params=params(), name="grad",
-    )(sel, err, cen, lat, mask, mine, theirs)
+    )(sel, err, cen, lat, slope)
 
 
 NAMES = ("x", "zh", "zl", "y", "c")
@@ -568,8 +639,8 @@
     local = jnp.max(jnp.where(hit, local, -1), axis=3)
     table = jnp.concatenate([jnp.maximum(jnp.max(local, axis=1), 0), (local >= 0).astype(jnp.int32).reshape(8, 4)], axis=1)
     lat, mask = encode_call(table, cen, mine, theirs, biases)
-    err_own, err = error_call(table, wt, lat, dec - act_t)
-    own, other, own_b, other_b = grad_call(table, err.reshape(8, D, TOK), cen, lat, mask, mine, theirs)
+    err_own, err, slope = error_call(table, wt, lat, mask, dec - act_t)
+    own, other, own_b, other_b = grad_call(table, err.reshape(8, D, TOK), cen, lat, slope)
     grad_w = own.astype(jnp.float32) + lax.ppermute(other, "c", SWAP).astype(jnp.float32)
     grad_b = (own_b + lax.ppermute(other_b, "c", SWAP))[:4]
     return err_own.T, grad_w.reshape(4 * SPAN, D), grad_b.reshape(4 * SPAN)

time: 261 us -> 260 us (level)
  Pallas kernels: 233 us -> 228 us
  starting transfers between devices: 6.17 us -> 10 us
    pallas_call x1, Pallas kernels: 30.5 us -> 20.8 us  [grad_call(): pl.pallas_call(grad_kernel, out_shape=(jax.ShapeDtypeStruct((4, SPAN, D),...]
    pallas_call x1, Pallas kernels: 123 us -> 128 us  [error_call(): pl.pallas_call(error_kernel, out_shape=(jax.ShapeDtypeStruct((ROWS, TOK),...]
    ppermute x1, starting transfers between devices: 6.08 us -> 9.94 us  [step(): lax.ppermute(other, 'c', SWAP).astype(jnp.float32)]
where the time goes in v7:
time: 260 us; the launch traced here: 259 us
  Pallas kernels  228 us (88%)
  other arithmetic  11.1 us (4%)
  starting transfers between devices  10 us (4%)
  waiting for transfers between devices  6.17 us (2%)
  local copies, waits for them, and re-layouts  3.06 us (1%)
    pallas_call x1, Pallas kernels, error_call(): pl.pallas_call(error_kernel, out_shape=(jax.ShapeDtypeStruct((ROWS, TOK),...  128 us
    pallas_call x1, Pallas kernels, gather_call(): pl.pallas_call(gather_kernel, out_shape=(jax.ShapeDtypeStruct(PIECES, jnp...  65.8 us
    pallas_call x1, Pallas kernels, grad_call(): pl.pallas_call(grad_kernel, out_shape=(jax.ShapeDtypeStruct((4, SPAN, D),...  20.8 us
    pallas_call x1, Pallas kernels, encode_call(): pl.pallas_call(encode_kernel, out_shape=(jax.ShapeDtypeStruct((8, 2 * SPA...  13.9 us
    ppermute x1, starting transfers between devices, step(): lax.ppermute(other, 'c', SWAP).astype(jnp.float32)  9.94 us
    add x1, other arithmetic, step(): own.astype(jnp.float32) + lax.ppermute(other, 'c', SWAP).astype(jnp.float32)  6.22 us
    ppermute x1, waiting for transfers between devices, step(): grad_b = (own_b + lax.ppermute(other_b, 'c', SWAP))[:4]  6.17 us
  transfers between devices with their start and end apart: 2, of which 1 were waited for; matrix products, arithmetic and copies ran while one was open for 0% of the time, Pallas kernels for 0%

profile of v7, /device:TPU:1, one launch (start us, length us, event | category | flops | bytes accessed | tf_op | source)
XLA Modules:
  0.0 259.2 jit_solution(855597278926148466)
XLA Ops:
  0.6 1.3 pad_convert_fusion.bias
  1.9 0.8 dynamic_slice.7
  2.7 1.9 fusion.1
  4.6 65.8 %gather.1 = (bf16[2,4,4,2,448,256]{5,4,3,2,1,0:T(8,128)(2,1)}, s32[2,4,2,8,16]{4,3,2,1,0:T(8,128)}, f32[2,8,128]{2,1,0:T(8,128)}, bf16[4,128,3584]{2,1,0:T(8,128)(2,1)}, bf16[8,3584,128]{2,1,0:T(8,128)(2,1)}) custom-call(bf16[448,256]{1,0:T(8,128)(2,1)} %get-tuple-element.34.own, s32[2,8,16]{2,1,0:T(8,128)} %codes.1, f32[8,128]{1,0:T(8,128)} %pad_convert_fusion.bias, ...), custom_call_target="tpu_custom_call" | custom-call | bytes 150000000 | tf_op jit(solution)/shard_map/gather/pallas_call | solution.py:464
  70.4 0.9 constant_dynamic-slice_fusion
  71.3 0.1 fusion.8
  71.3 0.3 fusion.4
  71.6 0.1 copy.18
  71.7 0.1 copy.17
  71.8 0.7 pad_add_fusion.table.sel
  72.5 13.9 %encode.1 = (bf16[8,256,256]{2,1,0:T(8,128)(2,1)}, bf16[8,256,256]{2,1,0:T(8,128)(2,1)}) custom-call(s32[8,6]{1,0:T(8,128)} %pad_add_fusion.table.sel, bf16[8,3584,256]{2,1,0:T(8,128)(2,1)} %bitcast.21, bf16[4,128,3584]{2,1,0:T(8,128)(2,1)} %bitcast.25, bf16[4,128,3584]{2,1,0:T(8,128)(2,1)} %get-tuple-element.20.theirs, f32[2,8,128]{2,1,0:T(8,128)} %get-tuple-element.21.bias), custom_call_target="tpu_custom_call" | custom-call | tf_op jit(solution)/shard_map/encode/pallas_call | solution.py:554
  86.3 127.7 %error.1 = (bf16[448,256]{1,0:T(8,128)(2,1)}, bf16[2,4,4,2,448,256]{5,4,3,2,1,0:T(8,128)(2,1)}, bf16[8,256,256]{2,1,0:T(8,128)(2,1)}) custom-call(s32[8,6]{1,0:T(8,128)} %pad_add_fusion.table.sel, bf16[8,3584,128]{2,1,0:T(8,128)(2,1)} %get-tuple-element.18.wt_hbm, bf16[8,256,256]{2,1,0:T(8,128)(2,1)} %get-tuple-element.22.lat, ...), custom_call_target="tpu_custom_call" | custom-call | tf_op jit(solution)/shard_map/error/pallas_call | solution.py:509
  214.1 20.8 %grad.1 = (bf16[4,128,3584]{2,1,0:T(8,128)(2,1)}, bf16[4,128,3584]{2,1,0:T(8,128)(2,1)}, f32[8,128]{1,0:T(8,128)}, f32[8,128]{1,0:T(8,128)}) custom-call(s32[8,6]{1,0:T(8,128)} %pad_add_fusion.table.sel, bf16[8,3584,256]{2,1,0:T(8,128)(2,1)} %bitcast.23, bf16[8,3584,256]{2,1,0:T(8,128)(2,1)} %bitcast.22, bf16[8,256,256]{2,1,0:T(8,128)(2,1)} %get-tuple-element.22.lat, ...), custom_call_target="tpu_custom_call" | custom-call | tf_op jit(solution)/shard_map/grad/pallas_call | solution.py:603
  234.8 9.9 %collective-permute-start = (bf16[4,128,3584]{2,1,0:T(8,128)(2,1)}, bf16[4,128,3584]{2,1,0:T(8,128)(2,1)S(1)}, u32[]{:S(2)}, u32[]{:S(2)}) collective-permute-start(bf16[4,128,3584]{2,1,0:T(8,128)(2,1)} %get-tuple-element.28), channel_id=1, source_target_pairs={{0,1},{1,0},{2,3},{3,2},{4,5},{5,4},{6,7},{7,6},{8,9},{9,8},{10,11... | collective-permute-start | bytes 11010056 | tf_op jit(solution)/shard_map/ppermute | solution.py:644
  244.8 0.1 collective-permute-start.1
  244.9 6.2 %collective-permute-done.1 = f32[8,128]{1,0:T(8,128)S(1)} collective-permute-done((f32[8,128]{1,0:T(8,128)}, f32[8,128]{1,0:T(8,128)S(1)}, u32[]{:S(2)}, u32[]{:S(2)}) %collective-permute-start.1) | collective-permute-done | bytes 4128 | tf_op jit(solution)/shard_map/ppermute | solution.py:645
  251.0 0.7 add.50
  251.7 0.6 slice_bitcast_fusion
  252.3 0.0 collective-permute-done
  252.3 0.0 copy-start
  252.3 6.2 %convert_add_fusion = f32[4,128,3584]{2,1,0:T(8,128)} fusion(bf16[4,128,3584]{2,1,0:T(8,128)(2,1)S(1)} %collective-permute-done, bf16[4,128,3584]{2,1,0:T(8,128)(2,1)} %get-tuple-element.27), kind=kLoop, calls=%fused_computation | loop fusion | flops 5505024 | bytes 14680064 | tf_op jit(solution)/shard_map/add | solution.py:644
  258.5 0.0 copy-done
  258.5 0.7 copy.24
  (4 shorter events, 0.0 us)
Async XLA Ops:
  234.8 17.5 %collective-permute-start = (bf16[4,128,3584]{2,1,0:T(8,128)(2,1)}, bf16[4,128,3584]{2,1,0:T(8,128)(2,1)S(1)}, u32[]{:S(2)}, u32[]{:S(2)}) collective-permute-start(bf16[4,128,3584]{2,1,0:T(8,128)(2,1)} %get-tuple-element.28), channel_id=1, source_target_pairs={{0,1},{1,0},{2,3},{3,2},{4,5},{5,4},{6,7},{7,6},{8,9},{9,8},{10,11... | collective-permute-start | bytes 11010056 | tf_op jit(solution)/shard_map/ppermute | solution.py:644
  244.8 6.3 %collective-permute-start.1 = (f32[8,128]{1,0:T(8,128)}, f32[8,128]{1,0:T(8,128)S(1)}, u32[]{:S(2)}, u32[]{:S(2)}) collective-permute-start(f32[8,128]{1,0:T(8,128)} %get-tuple-element.30), channel_id=1, source_target_pairs={{0,1},{1,0},{2,3},{3,2},{4,5},{5,4},{6,7},{7,6},{8,9},{9,8},{10,11... | collective-permute-start | bytes 12296 | tf_op jit(solution)/shard_map/ppermute | solution.py:645
  252.3 6.2 %copy-start = (bf16[448,256]{1,0:T(8,128)(2,1)S(1)}, bf16[448,256]{1,0:T(8,128)(2,1)}, u32[]{:S(2)}) copy-start(bf16[448,256]{1,0:T(8,128)(2,1)} %get-tuple-element.24) | copy-start | bytes 688132

commit v8 on v7

--- a/solution.py
+++ b/solution.py
@@ -485,6 +485,7 @@
     loads = [pltpu.make_async_copy(wt_hbm.at[i], wt.at[i], wt_sem.at[i]) for i in range(8)]
     for c in loads:
         c.start()
+    back[...] = jnp.zeros_like(back)
     barrier(me)
     for c in loads:
         c.wait()
@@ -493,7 +494,6 @@
         fill(k, at, sel, wt, lat, parts)
 
     last, reductions = reduce_error(me, make, parts, base, err, slots, rsend, rrecv)
-    back[...] = jnp.zeros_like(back)
     gather(me, err, out, local, send, recv, ready=last, use=Back(sel, wt, out, held_e, back, sems))
 
     def round_off(g, carry):
@@ -523,18 +523,15 @@
     )(sel, wt, lat, mask, base)
 
 
-CHUNK = 896
-
-
-def pick(mine, theirs, ws):
-    ws[:SPAN, :] = mine[0]
-    ws[SPAN:, :] = theirs[0]
-
-
-def encode_kernel(table, cen, mine, theirs, bias, lat, mask, ws):
+CHUNK = DEPTH = 512
+
+
+def encode_kernel(table, cen, mine, theirs, bias, lat, mask):
     g = pl.program_id(0)
-    pick(mine, theirs, ws)
-    pre = jnp.dot(ws[...], cen[0], preferred_element_type=jnp.float32)
+    pre = jnp.zeros((2 * SPAN, TOK), jnp.float32)
+    for i in range(0, D, DEPTH):
+        w = jnp.concatenate([mine[0, :, i : i + DEPTH], theirs[0, :, i : i + DEPTH]], axis=0)
+        pre = pre + jnp.dot(w, cen[0, i : i + DEPTH], preferred_element_type=jnp.float32)
     lane = lax.broadcasted_iota(jnp.int32, (SPAN, TOK), 1)
     for hh in range(2):
         rows = slice(hh * SPAN, (hh + 1) * SPAN)
@@ -561,7 +558,6 @@
             num_scalar_prefetch=1, grid=(8,),
             in_specs=[per(D, TOK), block(0), block(1), VMEM],
             out_specs=(per(2 * SPAN, TOK), per(2 * SPAN, TOK)),
-            scratch_shapes=[pltpu.VMEM((2 * SPAN, D), jnp.bfloat16)],
         ),
         compiler_params=params(), name="encode",
     )(table, cen, mine, theirs, bias)

time: 260 us -> 259 us (level)
  no operation moved by 1% of the time
where the time goes in v8:
time: 259 us; the launch traced here: 258 us
  Pallas kernels  228 us (88%)
  other arithmetic  11.1 us (4%)
  starting transfers between devices  9.06 us (3%)
  waiting for transfers between devices  6.17 us (2%)
  local copies, waits for them, and re-layouts  3.06 us (1%)
    pallas_call x1, Pallas kernels, error_call(): pl.pallas_call(error_kernel, out_shape=(jax.ShapeDtypeStruct((ROWS, TOK),...  128 us
    pallas_call x1, Pallas kernels, gather_call(): pl.pallas_call(gather_kernel, out_shape=(jax.ShapeDtypeStruct(PIECES, jnp...  65.8 us
    pallas_call x1, Pallas kernels, grad_call(): pl.pallas_call(grad_kernel, out_shape=(jax.ShapeDtypeStruct((4, SPAN, D),...  20.2 us
    pallas_call x1, Pallas kernels, encode_call(): pl.pallas_call(encode_kernel, out_shape=(jax.ShapeDtypeStruct((8, 2 * SPA...  13.5 us
    ppermute x1, starting transfers between devices, step(): lax.ppermute(other, 'c', SWAP).astype(jnp.float32)  8.99 us
    add x1, other arithmetic, step(): own.astype(jnp.float32) + lax.ppermute(other, 'c', SWAP).astype(jnp.float32)  6.22 us
    ppermute x1, waiting for transfers between devices, step(): grad_b = (own_b + lax.ppermute(other_b, 'c', SWAP))[:4]  6.17 us
  transfers between devices with their start and end apart: 2, of which 1 were waited for; matrix products, arithmetic and copies ran while one was open for 0% of the time, Pallas kernels for 0%

profile of v8, /device:TPU:1, one launch (start us, length us, event | category | flops | bytes accessed | tf_op | source)
XLA Modules:
  0.0 258.0 jit_solution(11823767111990341344)
XLA Ops:
  0.6 1.3 pad_convert_fusion.bias
  1.9 0.8 dynamic_slice.7
  2.7 1.9 fusion.1
  4.6 65.8 %gather.1 = (bf16[2,4,4,2,448,256]{5,4,3,2,1,0:T(8,128)(2,1)}, s32[2,4,2,8,16]{4,3,2,1,0:T(8,128)}, f32[2,8,128]{2,1,0:T(8,128)}, bf16[4,128,3584]{2,1,0:T(8,128)(2,1)}, bf16[8,3584,128]{2,1,0:T(8,128)(2,1)}) custom-call(bf16[448,256]{1,0:T(8,128)(2,1)} %get-tuple-element.34.own, s32[2,8,16]{2,1,0:T(8,128)} %codes.1, f32[8,128]{1,0:T(8,128)} %pad_convert_fusion.bias, ...), custom_call_target="tpu_custom_call" | custom-call | bytes 150000000 | tf_op jit(solution)/shard_map/gather/pallas_call | solution.py:464
  70.4 0.9 constant_dynamic-slice_fusion
  71.3 0.1 fusion.8
  71.3 0.3 fusion.4
  71.6 0.1 copy.18
  71.7 0.1 copy.17
  71.8 0.7 pad_add_fusion.table.sel
  72.5 13.5 %encode.1 = (bf16[8,256,256]{2,1,0:T(8,128)(2,1)}, bf16[8,256,256]{2,1,0:T(8,128)(2,1)}) custom-call(s32[8,6]{1,0:T(8,128)} %pad_add_fusion.table.sel, bf16[8,3584,256]{2,1,0:T(8,128)(2,1)} %bitcast.21, bf16[4,128,3584]{2,1,0:T(8,128)(2,1)} %bitcast.25, bf16[4,128,3584]{2,1,0:T(8,128)(2,1)} %get-tuple-element.20.theirs, f32[2,8,128]{2,1,0:T(8,128)} %get-tuple-element.21.bias), custom_call_target="tpu_custom_call" | custom-call | tf_op jit(solution)/shard_map/encode/pallas_call | solution.py:551
  86.0 128.5 %error.1 = (bf16[448,256]{1,0:T(8,128)(2,1)}, bf16[2,4,4,2,448,256]{5,4,3,2,1,0:T(8,128)(2,1)}, bf16[8,256,256]{2,1,0:T(8,128)(2,1)}) custom-call(s32[8,6]{1,0:T(8,128)} %pad_add_fusion.table.sel, bf16[8,3584,128]{2,1,0:T(8,128)(2,1)} %get-tuple-element.18.wt_hbm, bf16[8,256,256]{2,1,0:T(8,128)(2,1)} %get-tuple-element.22.lat, ...), custom_call_target="tpu_custom_call" | custom-call | tf_op jit(solution)/shard_map/error/pallas_call | solution.py:509
  214.5 20.2 %grad.1 = (bf16[4,128,3584]{2,1,0:T(8,128)(2,1)}, bf16[4,128,3584]{2,1,0:T(8,128)(2,1)}, f32[8,128]{1,0:T(8,128)}, f32[8,128]{1,0:T(8,128)}) custom-call(s32[8,6]{1,0:T(8,128)} %pad_add_fusion.table.sel, bf16[8,3584,256]{2,1,0:T(8,128)(2,1)} %bitcast.23, bf16[8,3584,256]{2,1,0:T(8,128)(2,1)} %bitcast.22, bf16[8,256,256]{2,1,0:T(8,128)(2,1)} %get-tuple-element.22.lat, ...), custom_call_target="tpu_custom_call" | custom-call | tf_op jit(solution)/shard_map/grad/pallas_call | solution.py:599
  234.6 9.0 %collective-permute-start = (bf16[4,128,3584]{2,1,0:T(8,128)(2,1)}, bf16[4,128,3584]{2,1,0:T(8,128)(2,1)S(1)}, u32[]{:S(2)}, u32[]{:S(2)}) collective-permute-start(bf16[4,128,3584]{2,1,0:T(8,128)(2,1)} %get-tuple-element.28), channel_id=1, source_target_pairs={{0,1},{1,0},{2,3},{3,2},{4,5},{5,4},{6,7},{7,6},{8,9},{9,8},{10,11... | collective-permute-start | bytes 11010056 | tf_op jit(solution)/shard_map/ppermute | solution.py:640
  243.6 0.1 collective-permute-start.1
  243.7 6.2 %collective-permute-done.1 = f32[8,128]{1,0:T(8,128)S(1)} collective-permute-done((f32[8,128]{1,0:T(8,128)}, f32[8,128]{1,0:T(8,128)S(1)}, u32[]{:S(2)}, u32[]{:S(2)}) %collective-permute-start.1) | collective-permute-done | bytes 4128 | tf_op jit(solution)/shard_map/ppermute | solution.py:641
  249.9 0.7 add.50
  250.5 0.6 slice_bitcast_fusion
  251.1 0.0 collective-permute-done
  251.1 0.0 copy-start
  251.1 6.2 %convert_add_fusion = f32[4,128,3584]{2,1,0:T(8,128)} fusion(bf16[4,128,3584]{2,1,0:T(8,128)(2,1)S(1)} %collective-permute-done, bf16[4,128,3584]{2,1,0:T(8,128)(2,1)} %get-tuple-element.27), kind=kLoop, calls=%fused_computation | loop fusion | flops 5505024 | bytes 14680064 | tf_op jit(solution)/shard_map/add | solution.py:640
  257.3 0.0 copy-done
  257.3 0.7 copy.24
  (4 shorter events, 0.0 us)
Async XLA Ops:
  234.6 16.5 %collective-permute-start = (bf16[4,128,3584]{2,1,0:T(8,128)(2,1)}, bf16[4,128,3584]{2,1,0:T(8,128)(2,1)S(1)}, u32[]{:S(2)}, u32[]{:S(2)}) collective-permute-start(bf16[4,128,3584]{2,1,0:T(8,128)(2,1)} %get-tuple-element.28), channel_id=1, source_target_pairs={{0,1},{1,0},{2,3},{3,2},{4,5},{5,4},{6,7},{7,6},{8,9},{9,8},{10,11... | collective-permute-start | bytes 11010056 | tf_op jit(solution)/shard_map/ppermute | solution.py:640
  243.6 6.3 %collective-permute-start.1 = (f32[8,128]{1,0:T(8,128)}, f32[8,128]{1,0:T(8,128)S(1)}, u32[]{:S(2)}, u32[]{:S(2)}) collective-permute-start(f32[8,128]{1,0:T(8,128)} %get-tuple-element.30), channel_id=1, source_target_pairs={{0,1},{1,0},{2,3},{3,2},{4,5},{5,4},{6,7},{7,6},{8,9},{9,8},{10,11... | collective-permute-start | bytes 12296 | tf_op jit(solution)/shard_map/ppermute | solution.py:641
  251.1 6.2 %copy-start = (bf16[448,256]{1,0:T(8,128)(2,1)S(1)}, bf16[448,256]{1,0:T(8,128)(2,1)}, u32[]{:S(2)}) copy-start(bf16[448,256]{1,0:T(8,128)(2,1)} %get-tuple-element.24) | copy-start | bytes 688132

commit v9 on v8

--- a/solution.py
+++ b/solution.py
@@ -395,9 +395,9 @@
     return last, [r for k in range(3) for r in (*first[k].values(), second[k], third[k])]
 
 
-def params(collective=None):
+def params(collective=None, mib=60):
     return pltpu.CompilerParams(collective_id=collective, has_side_effects=collective is not None,
-                                vmem_limit_bytes=60 * 1024 * 1024)
+                                vmem_limit_bytes=mib * 1024 * 1024)
 
 
 PIECES = (2, 4, 4, 2, ROWS, TOK)
@@ -610,7 +610,7 @@
             out_specs=(VMEM, VMEM, VMEM, VMEM),
             scratch_shapes=[pltpu.VMEM((4, SPAN, D), jnp.float32)] * 2,
         ),
-        compiler_params=params(), name="grad",
+        compiler_params=params(mib=36), name="grad",
     )(sel, err, cen, lat, slope)
 
 

time: 259 us -> 254 us (0.981)
  other arithmetic: 11.1 us -> 8.34 us
    pallas_call x1, Pallas kernels: 20.2 us -> 17 us  [grad_call(): pl.pallas_call(grad_kernel, out_shape=(jax.ShapeDtypeStruct((4, SPAN, D),...]
where the time goes in v9:
time: 254 us
  Pallas kernels  226 us (89%)
  starting transfers between devices  8.72 us (3%)
  other arithmetic  8.34 us (3%)
  waiting for transfers between devices  5.95 us (2%)
  local copies, waits for them, and re-layouts  4.29 us (2%)
    pallas_call x1, Pallas kernels, error_call(): pl.pallas_call(error_kernel, out_shape=(jax.ShapeDtypeStruct((ROWS, TOK),...  129 us
    pallas_call x1, Pallas kernels, gather_call(): pl.pallas_call(gather_kernel, out_shape=(jax.ShapeDtypeStruct(PIECES, jnp...  65.8 us
    pallas_call x1, Pallas kernels, grad_call(): pl.pallas_call(grad_kernel, out_shape=(jax.ShapeDtypeStruct((4, SPAN, D),...  17 us
    pallas_call x1, Pallas kernels, encode_call(): pl.pallas_call(encode_kernel, out_shape=(jax.ShapeDtypeStruct((8, 2 * SPA...  13.9 us
    ppermute x1, starting transfers between devices, step(): lax.ppermute(other, 'c', SWAP).astype(jnp.float32)  8.63 us
    ppermute x1, waiting for transfers between devices, step(): grad_b = (own_b + lax.ppermute(other_b, 'c', SWAP))[:4]  5.95 us
  transfers between devices with their start and end apart: 2, of which 1 were waited for; matrix products, arithmetic and copies ran while one was open for 0% of the time, Pallas kernels for 0%

profile of v9, /device:TPU:1, one launch (start us, length us, event | category | flops | bytes accessed | tf_op | source)
XLA Modules:
  0.0 253.9 jit_solution(16619202615660247238)
XLA Ops:
  0.6 1.3 pad_convert_fusion.bias
  1.9 0.8 dynamic_slice.7
  2.7 1.9 fusion.1
  4.6 65.8 %gather.1 = (bf16[2,4,4,2,448,256]{5,4,3,2,1,0:T(8,128)(2,1)}, s32[2,4,2,8,16]{4,3,2,1,0:T(8,128)}, f32[2,8,128]{2,1,0:T(8,128)}, bf16[4,128,3584]{2,1,0:T(8,128)(2,1)}, bf16[8,3584,128]{2,1,0:T(8,128)(2,1)}) custom-call(bf16[448,256]{1,0:T(8,128)(2,1)} %get-tuple-element.34.own, s32[2,8,16]{2,1,0:T(8,128)} %codes.1, f32[8,128]{1,0:T(8,128)} %pad_convert_fusion.bias, ...), custom_call_target="tpu_custom_call" | custom-call | bytes 150000000 | tf_op jit(solution)/shard_map/gather/pallas_call | solution.py:464
  70.4 0.9 constant_dynamic-slice_fusion
  71.3 0.1 fusion.8
  71.4 0.3 fusion.4
  71.6 0.1 copy.18
  71.7 0.1 copy.17
  71.8 0.7 pad_add_fusion.table.sel
  72.5 13.9 %encode.1 = (bf16[8,256,256]{2,1,0:T(8,128)(2,1)}, bf16[8,256,256]{2,1,0:T(8,128)(2,1)}) custom-call(s32[8,6]{1,0:T(8,128)} %pad_add_fusion.table.sel, bf16[8,3584,256]{2,1,0:T(8,128)(2,1)} %bitcast.21, bf16[4,128,3584]{2,1,0:T(8,128)(2,1)} %bitcast.25, bf16[4,128,3584]{2,1,0:T(8,128)(2,1)} %get-tuple-element.20.theirs, f32[2,8,128]{2,1,0:T(8,128)} %get-tuple-element.21.bias), custom_call_target="tpu_custom_call" | custom-call | tf_op jit(solution)/shard_map/encode/pallas_call | solution.py:551
  86.3 0.0 copy-start
  86.3 0.0 copy-start.2
  86.3 129.2 %error.1 = (bf16[448,256]{1,0:T(8,128)(2,1)}, bf16[2,4,4,2,448,256]{5,4,3,2,1,0:T(8,128)(2,1)}, bf16[8,256,256]{2,1,0:T(8,128)(2,1)}) custom-call(s32[8,6]{1,0:T(8,128)} %pad_add_fusion.table.sel, bf16[8,3584,128]{2,1,0:T(8,128)(2,1)} %get-tuple-element.18.wt_hbm, bf16[8,256,256]{2,1,0:T(8,128)(2,1)} %get-tuple-element.22.lat, ...), custom_call_target="tpu_custom_call" | custom-call | tf_op jit(solution)/shard_map/error/pallas_call | solution.py:509
  215.5 0.0 copy-done
  215.5 0.0 copy-done.2
  215.6 0.0 copy-start.1
  215.6 1.2 copy-done.1
  216.8 17.0 %grad.1 = (bf16[4,128,3584]{2,1,0:T(8,128)(2,1)S(1)}, bf16[4,128,3584]{2,1,0:T(8,128)(2,1)S(1)}, f32[8,128]{1,0:T(8,128)S(1)}, f32[8,128]{1,0:T(8,128)S(1)}) custom-call(s32[8,6]{1,0:T(8,128)S(1)} %copy-done.2, bf16[8,3584,256]{2,1,0:T(8,128)(2,1)} %bitcast.23, bf16[8,3584,256]{2,1,0:T(8,128)(2,1)} %bitcast.22, bf16[8,256,256]{2,1,0:T(8,128)(2,1)S(1)} %copy-done, ...), custom_call_target="tpu_custom_call" | custom-call | tf_op jit(solution)/shard_map/grad/pallas_call | solution.py:599
  233.8 8.6 %collective-permute-start = (bf16[4,128,3584]{2,1,0:T(8,128)(2,1)S(1)}, bf16[4,128,3584]{2,1,0:T(8,128)(2,1)S(1)}, u32[]{:S(2)}, u32[]{:S(2)}) collective-permute-start(bf16[4,128,3584]{2,1,0:T(8,128)(2,1)S(1)} %get-tuple-element.28), channel_id=1, source_target_pairs={{0,1},{1,0},{2,3},{3,2},{4,5},{5,4},{6,7},{7,6},{8,9},{9,8},{10,11... | collective-permute-start | bytes 11010056 | tf_op jit(solution)/shard_map/ppermute | solution.py:640
  242.5 0.1 collective-permute-start.1
  242.6 5.9 %collective-permute-done.1 = f32[8,128]{1,0:T(8,128)S(1)} collective-permute-done((f32[8,128]{1,0:T(8,128)S(1)}, f32[8,128]{1,0:T(8,128)S(1)}, u32[]{:S(2)}, u32[]{:S(2)}) %collective-permute-start.1) | collective-permute-done | bytes 4128 | tf_op jit(solution)/shard_map/ppermute | solution.py:641
  248.5 0.6 slice_bitcast_fusion
  249.1 0.0 collective-permute-done
  249.1 0.0 copy-start.3
  249.1 4.1 %convert_add_fusion = f32[4,128,3584]{2,1,0:T(8,128)} fusion(bf16[4,128,3584]{2,1,0:T(8,128)(2,1)S(1)} %collective-permute-done, bf16[4,128,3584]{2,1,0:T(8,128)(2,1)S(1)} %get-tuple-element.27), kind=kLoop, calls=%fused_computation | loop fusion | flops 5505024 | bytes 14680064 | tf_op jit(solution)/shard_map/add | solution.py:640
  253.2 0.0 copy-done.3
  253.2 0.7 copy.24
  (5 shorter events, 0.0 us)
Async XLA Ops:
  86.3 129.2 %copy-start = (bf16[8,256,256]{2,1,0:T(8,128)(2,1)S(1)}, bf16[8,256,256]{2,1,0:T(8,128)(2,1)}, u32[]{:S(2)}) copy-start(bf16[8,256,256]{2,1,0:T(8,128)(2,1)} %get-tuple-element.22.lat) | copy-start | bytes 3145732
  86.3 129.2 %copy-start.2 = (s32[8,6]{1,0:T(8,128)S(1)}, s32[8,6]{1,0:T(8,128)}, u32[]{:S(2)}) copy-start(s32[8,6]{1,0:T(8,128)} %pad_add_fusion.table.sel) | copy-start | bytes 580
  215.6 1.2 copy-start.1
  233.8 15.3 %collective-permute-start = (bf16[4,128,3584]{2,1,0:T(8,128)(2,1)S(1)}, bf16[4,128,3584]{2,1,0:T(8,128)(2,1)S(1)}, u32[]{:S(2)}, u32[]{:S(2)}) collective-permute-start(bf16[4,128,3584]{2,1,0:T(8,128)(2,1)S(1)} %get-tuple-element.28), channel_id=1, source_target_pairs={{0,1},{1,0},{2,3},{3,2},{4,5},{5,4},{6,7},{7,6},{8,9},{9,8},{10,11... | collective-permute-start | bytes 11010056 | tf_op jit(solution)/shard_map/ppermute | solution.py:640
  242.5 6.0 %collective-permute-start.1 = (f32[8,128]{1,0:T(8,128)S(1)}, f32[8,128]{1,0:T(8,128)S(1)}, u32[]{:S(2)}, u32[]{:S(2)}) collective-permute-start(f32[8,128]{1,0:T(8,128)S(1)} %get-tuple-element.30), channel_id=1, source_target_pairs={{0,1},{1,0},{2,3},{3,2},{4,5},{5,4},{6,7},{7,6},{8,9},{9,8},{10,11... | collective-permute-start | bytes 12296 | tf_op jit(solution)/shard_map/ppermute | solution.py:641
  249.1 4.1 %copy-start.3 = (bf16[448,256]{1,0:T(8,128)(2,1)S(1)}, bf16[448,256]{1,0:T(8,128)(2,1)}, u32[]{:S(2)}) copy-start(bf16[448,256]{1,0:T(8,128)(2,1)} %get-tuple-element.24) | copy-start | bytes 688132
